TPU v7x, 32 devices: a whole 2x2x4 slice. The times are simulated.
32 devices in a mesh: disp: 8 (over y, x, core), col: 4 (over z).
Axes of the slice: x: 2, y: 2, z: 4, core: 2. Of those that a mesh axis runs over, the one named last changes fastest.
Arguments:
- left_feat: bfloat16 [320, 2, 1024], P('disp', None, 'col'), may hold values from -6 to 6
- right_feat: bfloat16 [320, 2, 1024], P('disp', None, 'col'), may hold values from -6 to 6
- conv1_w: bfloat16 [32, 40, 3, 3, 3], replicated, may hold values from -0.25 to 0.25
- conv2_w: bfloat16 [32, 32, 3, 3, 3], replicated, may hold values from -0.3125 to 0.3125
- conv3_w: bfloat16 [32, 32, 3, 3, 3], replicated, may hold values from -0.3125 to 0.3125
- head_w: float32 [32], replicated, may hold values from -120 to 120
Outputs:
- warped: bfloat16 [320, 2, 1024], P('disp', None, 'col')
- disparity: float32 [2, 1024], P(None, 'col')
All inputs are finite; a program needn't handle non-finite values.
Results may differ from a plain program's by a relative error of at most 0.015.
The roundings to bfloat16 on the way count: a program that leaves them out, or rounds other values in their place, can miss the bound.
Values may be sent and summed in bfloat16 or wider, within the bound.
No kernel may reach another device: no remote copies, remote signals or barrier semaphores. Data moves between devices by JAX's collectives and lax.ppermute only.
A program may use at most 64 MiB of HBM per device.

v0:
```python
import jax
import jax.numpy as jnp
from jax import lax
from jax.sharding import PartitionSpec as P

G = 40
DG = 16
CG = 8


masked_value = -1e30


def with_halo(x, sides, width):
    for axis, dim in sides:
        peers, length = (lax.axis_size(axis), x.shape[dim])
        up = [(i, (i + 1) % peers) for i in range(peers - 1)]
        down = [(j, i) for i, j in up]
        last = lax.slice_in_dim(x, length - width, length, axis=dim)
        initial = lax.slice_in_dim(x, 0, width, axis=dim)
        before = lax.ppermute(last, axis, up)
        after = lax.ppermute(initial, axis, down)
        x = jnp.concatenate([before, x, after], axis=dim)
    return x


def passed_along(value, axis, steps):
    count = lax.axis_size(axis)
    initial, last = (max(0, -steps), min(count, count - steps))
    return lax.ppermute(value, axis, [(source, source + steps) for source in range(initial, last)])


def convolve(activity, kernel):
    padded = jnp.pad(activity, ((0, 0), (0, 0), (1, 1), (0, 0)))
    output = lax.conv_general_dilated(
        padded[None],
        kernel,
        (1, 1, 1),
        "VALID",
        dimension_numbers=("NCDHW", "OIDHW", "NCDHW"),
        preferred_element_type=jnp.float32,
    )
    return jnp.maximum(output[0], 0.0)


def layer_step(activity, kernel):
    widened = with_halo(activity, (("disp", 1), ("col", 3)), 1)
    return convolve(widened, kernel)


def accumulate(weighting, right_rows, start_base, strip_width):
    group_depth = weighting.shape[0]

    def add_term(offset, running):
        shifted = lax.dynamic_slice_in_dim(right_rows, start_base - offset, strip_width, 2)
        weight = lax.dynamic_index_in_dim(weighting, offset, 0, keepdims=False)
        return running + weight[None] * shifted.astype(jnp.float32)

    initial = jnp.zeros((right_rows.shape[0], right_rows.shape[1], strip_width), jnp.float32)
    return lax.fori_loop(0, group_depth, add_term, initial)


def shards(left_feat, right_feat, conv1_w, conv2_w, conv3_w, head_w):
    groups_disp = lax.axis_size("disp")
    channel_count = left_feat.shape[0] * groups_disp
    slab_rows = left_feat.shape[1]
    strip_width = left_feat.shape[2]
    group_depth = DG
    disp_span = group_depth * groups_disp
    group_index = lax.axis_index("disp")
    strip_index = lax.axis_index("col")
    first_disp = group_index * group_depth
    left_full, right_full = (
        lax.all_gather(left_feat, "disp", axis=0, tiled=True),
        lax.all_gather(right_feat, "disp", axis=0, tiled=True),
    )
    tail_columns = passed_along(right_full[:, :, strip_width - disp_span :], "col", 1)
    right_wide = jnp.concatenate([tail_columns, right_full], axis=2)
    start_base = disp_span - first_disp

    def correlate(offset):
        shifted = lax.dynamic_slice_in_dim(right_wide, start_base - offset, strip_width, 2)
        product = left_full.astype(jnp.float32) * shifted.astype(jnp.float32)
        return (jnp.sum(product.reshape(G, CG, slab_rows, strip_width), axis=1) / CG).astype(
            jnp.bfloat16
        )

    volume = jnp.moveaxis(lax.map(correlate, jnp.arange(group_depth, dtype=jnp.int32)), 0, 1)
    activity = layer_step(volume, conv1_w).astype(jnp.bfloat16)
    activity = layer_step(activity, conv2_w).astype(jnp.bfloat16)
    activity = layer_step(activity, conv3_w)
    scores = jnp.sum(head_w[:, None, None, None] * activity, axis=0)
    disp_global = first_disp + jnp.arange(group_depth, dtype=jnp.int32)
    column_global = strip_index * strip_width + jnp.arange(strip_width, dtype=jnp.int32)
    valid_mask = column_global[None, None, :] >= disp_global[:, None, None]
    scores = jnp.where(valid_mask, scores, masked_value)
    own_share = channel_count // groups_disp
    every_score = lax.all_gather(scores, "disp", axis=0, tiled=True)
    every_disp = jnp.arange(disp_span, dtype=jnp.int32)
    every_valid = column_global[None, None, :] >= every_disp[:, None, None]
    top_score = jnp.max(every_score, axis=0)
    weighting = jnp.where(every_valid, jnp.exp(every_score - top_score[None]), 0.0)
    denominator = jnp.sum(weighting, axis=0)
    disp_sum = jnp.sum(weighting * every_disp.astype(jnp.float32)[:, None, None], axis=0)
    own_rows = lax.dynamic_slice_in_dim(right_wide, group_index * own_share, own_share, 0)
    numerator = accumulate(weighting, own_rows, disp_span, strip_width)
    warped = (numerator / denominator[None]).astype(jnp.bfloat16)
    return (warped, disp_sum / denominator / disp_span)


def solution(mesh):
    return jax.shard_map(
        shards,
        mesh=mesh,
        in_specs=(P("disp", None, "col"), P("disp", None, "col"), P(), P(), P(), P()),
        out_specs=(P("disp", None, "col"), P(None, "col")),
        check_vma=False,
    )
```

profile of v0, /device:TPU:0, one launch (start us, length us, event | category | flops | bytes accessed | tf_op | source)
XLA Modules:
  0.0 276.7 jit_solution(700952006049259262)
XLA Ops:
  0.6 11.3 %all_gather.10 = bf16[320,2,256]{2,1,0:T(2,128)(2,1)S(1)} all-gather(bf16[40,2,256]{2,1,0:T(2,128)(2,1)} %param.11), channel_id=1, replica_groups=mesh['disp'=8,'col'=4] {'disp'}, dimensions={0}, use_global_device_ids=true | all-gather | bytes 368640 | tf_op jit(solution)/shard_map/all_gather | solution.py:75
  15.6 9.2 %all_gather.9 = bf16[320,2,256]{2,1,0:T(2,128)(2,1)S(1)} all-gather(bf16[40,2,256]{2,1,0:T(2,128)(2,1)} %param.10), channel_id=1, replica_groups=mesh['disp'=8,'col'=4] {'disp'}, dimensions={0}, use_global_device_ids=true | all-gather | bytes 368640 | tf_op jit(solution)/shard_map/all_gather | solution.py:74
  25.2 35.9 %while.26 = (s32[]{:T(128)}, bf16[16,40,2,256]{3,2,1,0:T(2,128)(2,1)S(1)}, bf16[320,2,256]{2,1,0:T(2,128)(2,1)S(1)}, s32[16]{0:T(128)S(1)}, s32[]{:T(128)}, /*in...) while((s32[]{:T(128)}, bf16[16,40,2,256]{3,2,1,0:T(2,128)(2,1)S(1)}, ...), condition=%wide.region_2.3_spmd, body=%wide.region_0.2_spmd.sunk | while | flops 675846 | bytes 2171059 | solution.py:88
  73.4 5.7 %collective-permute-done.3 = bf16[40,18,2,1]{3,2,0,1:T(2,128)(2,1)S(1)} collective-permute-done((bf16[40,18,2,1]{3,2,0,1:T(2,128)(2,1)S(1)}, bf16[40,18,2,1]{3,2,0,1:T(2,128)(2,1)S(1)}, u32[]{:S(2)}, u32[]{:S(2)}) %collective-permute-start.3) | collective-permute-done | bytes 2912 | tf_op jit(solution)/shard_map/ppermute | solution.py:21
  79.1 4.7 %collective-permute-done.4 = bf16[40,18,2,1]{3,2,0,1:T(2,128)(2,1)S(1)} collective-permute-done((bf16[40,18,2,1]{3,2,0,1:T(2,128)(2,1)S(1)}, bf16[40,18,2,1]{3,2,0,1:T(2,128)(2,1)S(1)}, u32[]{:S(2)}, u32[]{:S(2)}) %collective-permute-start.4) | collective-permute-done | bytes 2912 | tf_op jit(solution)/shard_map/ppermute | solution.py:22
  83.8 6.5 %fusion.31 = bf16[40,18,4,1,258]{4,2,0,1,3:T(4,128)(2,1)S(1)} fusion(bf16[40,18,2,1]{3,2,0,1:T(2,128)(2,1)S(1)} %collective-permute-done.4, bf16[40,18,2,1]{3,2,0,1:T(2,128)(2,1)S(1)} %collective-permute-done.3, bf16[40,1,2,256]{3,2,0,1:T(2,128)(2,1)S(1)} %collective-permute-done.2, bf16[40,16,2,256]{3,2,0,1:T(2,128)(2,1)S(1)} %bitcast.82, ...), kind=kLoop, calls=%fused_computation.42 | loop fusion | flops 13374720 | bytes 2229120 | tf_op jit(solution)/shard_map/broadcast_in_dim | solution.py:36
  91.3 6.3 %reshape.131 = bf16[40,18,4,1,8,33]{5,4,2,0,1,3:T(8,128)(2,1)} reshape(bf16[40,18,4,1,264]{4,2,0,1,3:T(4,128)(2,1)S(1)} %pad.14) | data formatting | bytes 3041280 | tf_op jit(solution)/shard_map/conv_general_dilated | solution.py:35
  97.6 9.3 %copy.20 = bf16[40,18,4,1,8,33]{0,4,5,2,1,3:T(8,128)(2,1)} copy(bf16[40,18,4,1,8,33]{5,4,2,0,1,3:T(8,128)(2,1)} %reshape.131) | data formatting | bytes 3041280 | tf_op jit(solution)/shard_map/conv_general_dilated | solution.py:35
  108.0 13.5 %maximum_convert_fusion.1 = bf16[16,2,8,33,32]{4,2,3,1,0:T(8,128)(2,1)} fusion(pred[8,33]{0,1:T(8,128)(4,1)S(1)} %copy-done.5, bf16[32,40,3,3,3]{1,0,4,3,2:T(8,128)(2,1)S(1)} %copy-done, bf16[40,18,4,1,7,2]{0,4,5,2,1,3:T(8,128)(2,1)S(1)} %slice.63, bf16[40,18,4,1,8,33]{0,4,5,2,1,3:T(8,128)(2,1)} %copy.20), kind=kOutput, calls=%fused_computation.36 | convolution fusion | flops 589575168 | bytes 2211336 | tf_op jit(solution)/shard_map/conv_general_dilated | solution.py:35
  121.6 3.8 %copy.21 = bf16[16,2,8,33,32]{3,2,4,1,0:T(8,128)(2,1)S(1)} copy(bf16[16,2,8,33,32]{4,2,3,1,0:T(8,128)(2,1)} %maximum_convert_fusion.1) | data formatting | bytes 1081344 | tf_op jit(solution)/shard_map/convert_element_type | solution.py:89
  141.5 4.1 %collective-permute-done.7 = bf16[32,18,2,1]{3,0,2,1:T(8,128)(2,1)S(1)} collective-permute-done((bf16[32,18,2,1]{3,0,2,1:T(8,128)(2,1)S(1)}, bf16[32,18,2,1]{3,0,2,1:T(8,128)(2,1)S(1)}, u32[]{:S(2)}, u32[]{:S(2)}) %collective-permute-start.7) | collective-permute-done | bytes 2336 | tf_op jit(solution)/shard_map/ppermute | solution.py:21
  145.6 4.7 %collective-permute-done.8 = bf16[32,18,2,1]{3,0,2,1:T(8,128)(2,1)S(1)} collective-permute-done((bf16[32,18,2,1]{3,0,2,1:T(8,128)(2,1)S(1)}, bf16[32,18,2,1]{3,0,2,1:T(8,128)(2,1)S(1)}, u32[]{:S(2)}, u32[]{:S(2)}) %collective-permute-start.8) | collective-permute-done | bytes 2336 | tf_op jit(solution)/shard_map/ppermute | solution.py:22
  151.6 5.4 %reshape.104 = bf16[32,18,4,1,8,33]{5,4,0,2,1,3:T(8,128)(2,1)} reshape(bf16[32,18,4,1,264]{4,0,2,1,3:T(8,128)(2,1)S(1)} %pad.16) | data formatting | bytes 2433024 | tf_op jit(solution)/shard_map/conv_general_dilated | solution.py:35
  157.0 9.1 %copy.23 = bf16[32,18,4,1,8,33]{0,4,5,2,1,3:T(8,128)(2,1)} copy(bf16[32,18,4,1,8,33]{5,4,0,2,1,3:T(8,128)(2,1)} %reshape.104) | data formatting | bytes 2433024 | tf_op jit(solution)/shard_map/conv_general_dilated | solution.py:35
  167.1 9.1 %maximum_convert_fusion = bf16[16,2,8,33,32]{4,2,3,1,0:T(8,128)(2,1)} fusion(pred[8,33]{0,1:T(8,128)(4,1)S(1)} %copy-done.5, bf16[32,32,3,3,3]{1,0,4,3,2:T(8,128)(2,1)S(1)} %copy-done.3, bf16[32,18,4,1,7,2]{0,4,5,2,1,3:T(8,128)(2,1)S(1)} %slice.69, bf16[32,18,4,1,8,33]{0,4,5,2,1,3:T(8,128)(2,1)} %copy.23), kind=kOutput, calls=%fused_computation.35 | convolution fusion | flops 471822336 | bytes 1877256 | tf_op jit(solution)/shard_map/conv_general_dilated | solution.py:35
  176.2 3.8 %copy.24 = bf16[16,2,8,33,32]{3,2,4,1,0:T(8,128)(2,1)S(1)} copy(bf16[16,2,8,33,32]{4,2,3,1,0:T(8,128)(2,1)} %maximum_convert_fusion) | data formatting | bytes 1081344 | tf_op jit(solution)/shard_map/convert_element_type | solution.py:90
  193.9 3.7 %collective-permute-done.11 = bf16[32,18,2,1]{3,0,2,1:T(8,128)(2,1)S(1)} collective-permute-done((bf16[32,18,2,1]{3,0,2,1:T(8,128)(2,1)S(1)}, bf16[32,18,2,1]{3,0,2,1:T(8,128)(2,1)S(1)}, u32[]{:S(2)}, u32[]{:S(2)}) %collective-permute-start.11) | collective-permute-done | bytes 2336 | tf_op jit(solution)/shard_map/ppermute | solution.py:21
  197.7 4.7 %collective-permute-done.12 = bf16[32,18,2,1]{3,0,2,1:T(8,128)(2,1)S(1)} collective-permute-done((bf16[32,18,2,1]{3,0,2,1:T(8,128)(2,1)S(1)}, bf16[32,18,2,1]{3,0,2,1:T(8,128)(2,1)S(1)}, u32[]{:S(2)}, u32[]{:S(2)}) %collective-permute-start.12) | collective-permute-done | bytes 2336 | tf_op jit(solution)/shard_map/ppermute | solution.py:22
  203.6 5.4 %reshape.111 = bf16[32,18,4,1,8,33]{5,4,0,2,1,3:T(8,128)(2,1)} reshape(bf16[32,18,4,1,264]{4,0,2,1,3:T(8,128)(2,1)S(1)} %pad.18) | data formatting | bytes 2433024 | tf_op jit(solution)/shard_map/conv_general_dilated | solution.py:35
  209.0 9.1 %copy.26 = bf16[32,18,4,1,8,33]{0,4,5,2,1,3:T(8,128)(2,1)} copy(bf16[32,18,4,1,8,33]{5,4,0,2,1,3:T(8,128)(2,1)} %reshape.111) | data formatting | bytes 2433024 | tf_op jit(solution)/shard_map/conv_general_dilated | solution.py:35
  219.2 9.5 %select_maximum_fusion = f32[16,2,8,33,32]{4,2,3,1,0:T(8,128)} fusion(pred[8,33]{0,1:T(8,128)(4,1)S(1)} %copy-done.5, bf16[32,32,3,3,3]{1,0,4,3,2:T(8,128)(2,1)S(1)} %copy-done.4, bf16[32,18,4,1,7,2]{0,4,5,2,1,3:T(8,128)(2,1)S(1)} %slice.75, bf16[32,18,4,1,8,33]{0,4,5,2,1,3:T(8,128)(2,1)} %copy.26), kind=kOutput, calls=%fused_computation.34 | convolution fusion | flops 471552000 | bytes 2417928 | tf_op jit(solution)/shard_map/conv_general_dilated | solution.py:35
  228.6 5.8 %copy.27 = f32[16,2,8,33,32]{3,2,4,1,0:T(8,128)} copy(f32[16,2,8,33,32]{4,2,3,1,0:T(8,128)} %select_maximum_fusion) | data formatting | bytes 2162688 | tf_op jit(solution)/shard_map/max | solution.py:43
  238.2 11.6 %all_gather.11 = f32[128,2,256]{2,1,0:T(2,128)S(1)} all-gather(f32[16,2,256]{2,1,0:T(2,128)S(1)} %broadcast_select_fusion), channel_id=1, replica_groups=mesh['disp'=8,'col'=4] {'disp'}, dimensions={0}, use_global_device_ids=true | all-gather | bytes 294912 | tf_op jit(solution)/shard_map/all_gather | solution.py:98
  250.4 25.1 %while.27 = (s32[]{:T(128)}, f32[40,2,256]{2,1,0:T(2,128)S(1)}, f32[128,2,256]{2,1,0:T(2,128)S(1)}, bf16[40,2,384]{2,1,0:T(2,128)(2,1)S(1)}, s32[]{:T(128)}, /*index=5*/s32[]{:T(128)}, s32[]{:T(128)}, s32[]{:T(128)}) while((s32[]{:T(128)}, f32[40,2,256]{2,1,0:T(2,128)S(1)}, f32[128,2,256]{2,1,0:T(2,128)S(1)}, ...), condition=%wide.region_6.7_spmd.clone, body=%wide.region_5.6_spmd.clone.sunk | while | flops 81927 | bytes 211101 | solution.py:60
  (392 shorter events, 105.7 us)
Async XLA Ops:
  0.6 107.4 %copy-start = (bf16[32,40,3,3,3]{1,0,4,3,2:T(8,128)(2,1)S(1)}, bf16[32,40,3,3,3]{1,0,4,3,2:T(8,128)(2,1)}, u32[]{:S(2)}) copy-start(bf16[32,40,3,3,3]{1,0,4,3,2:T(8,128)(2,1)} %param.12) | copy-start | bytes 207364
  12.1 12.7 %collective-permute-start = (bf16[320,2,128]{2,1,0:T(2,128)(2,1)S(1)}, bf16[320,2,128]{2,1,0:T(2,128)(2,1)S(1)}, u32[]{:S(2)}, u32[]{:S(2)}) collective-permute-start(bf16[320,2,128]{2,1,0:T(2,128)(2,1)S(1)} %slice.58), channel_id=1, source_target_pairs={{0,1},{1,2},{2,3},{4,5},{5,6},{6,7},{8,9},{9,10},{10,11},{12,13},{... | collective-permute-start | bytes 491528 | tf_op jit(solution)/shard_map/ppermute | solution.py:30
  61.2 3.6 %collective-permute-start.1 = (bf16[40,1,2,256]{3,2,0,1:T(2,128)(2,1)S(1)}, bf16[40,1,2,256]{3,2,0,1:T(2,128)(2,1)S(1)}, u32[]{:S(2)}, u32[]{:S(2)}) collective-permute-start(bf16[40,1,2,256]{3,2,0,1:T(2,128)(2,1)S(1)} %get-tuple-element.186), channel_id=1, source_target_pairs={{0,4},{4,8},{8,12},{12,16},{16,20},{20,24},{24,28},{1,5},{5,9},{9,... | collective-permute-start | bytes 122888 | tf_op jit(solution)/shard_map/ppermute | solution.py:21
  63.5 3.2 %collective-permute-start.2 = (bf16[40,1,2,256]{3,2,0,1:T(2,128)(2,1)S(1)}, bf16[40,1,2,256]{3,2,0,1:T(2,128)(2,1)S(1)}, u32[]{:S(2)}, u32[]{:S(2)}) collective-permute-start(bf16[40,1,2,256]{3,2,0,1:T(2,128)(2,1)S(1)} %get-tuple-element.187), channel_id=1, source_target_pairs={{4,0},{8,4},{12,8},{16,12},{20,16},{24,20},{28,24},{5,1},{9,5},{13... | collective-permute-start | bytes 122888 | tf_op jit(solution)/shard_map/ppermute | solution.py:22
  68.4 10.7 %collective-permute-start.3 = (bf16[40,18,2,1]{3,2,0,1:T(2,128)(2,1)S(1)}, bf16[40,18,2,1]{3,2,0,1:T(2,128)(2,1)S(1)}, u32[]{:S(2)}, u32[]{:S(2)}) collective-permute-start(bf16[40,18,2,1]{3,2,0,1:T(2,128)(2,1)S(1)} %get-tuple-element.184), channel_id=1, source_target_pairs={{0,1},{1,2},{2,3},{4,5},{5,6},{6,7},{8,9},{9,10},{10,11},{12,13},{... | collective-permute-start | bytes 8648 | tf_op jit(solution)/shard_map/ppermute | solution.py:21
  71.9 11.9 %collective-permute-start.4 = (bf16[40,18,2,1]{3,2,0,1:T(2,128)(2,1)S(1)}, bf16[40,18,2,1]{3,2,0,1:T(2,128)(2,1)S(1)}, u32[]{:S(2)}, u32[]{:S(2)}) collective-permute-start(bf16[40,18,2,1]{3,2,0,1:T(2,128)(2,1)S(1)} %get-tuple-element.185), channel_id=1, source_target_pairs={{1,0},{2,1},{3,2},{5,4},{6,5},{7,6},{9,8},{10,9},{11,10},{13,12},{... | collective-permute-start | bytes 8648 | tf_op jit(solution)/shard_map/ppermute | solution.py:22
  97.6 10.4 %copy-start.5 = (pred[8,33]{0,1:T(8,128)(4,1)S(1)}, pred[8,33]{0,1:T(8,128)(4,1)}, u32[]{:S(2)}) copy-start(pred[8,33]{0,1:T(8,128)(4,1)} %constant.115) | copy-start | bytes 796
  128.7 4.5 %collective-permute-start.5 = (bf16[32,1,2,256]{3,0,2,1:T(8,128)(2,1)S(1)}, bf16[32,1,2,256]{3,0,2,1:T(8,128)(2,1)S(1)}, u32[]{:S(2)}, u32[]{:S(2)}) collective-permute-start(bf16[32,1,2,256]{3,0,2,1:T(8,128)(2,1)S(1)} %get-tuple-element.194), channel_id=1, source_target_pairs={{0,4},{4,8},{8,12},{12,16},{16,20},{20,24},{24,28},{1,5},{5,9},{9,... | collective-permute-start | bytes 98312 | tf_op jit(solution)/shard_map/ppermute | solution.py:21
  131.9 4.2 %collective-permute-start.6 = (bf16[32,1,2,256]{3,0,2,1:T(8,128)(2,1)S(1)}, bf16[32,1,2,256]{3,0,2,1:T(8,128)(2,1)S(1)}, u32[]{:S(2)}, u32[]{:S(2)}) collective-permute-start(bf16[32,1,2,256]{3,0,2,1:T(8,128)(2,1)S(1)} %get-tuple-element.195), channel_id=1, source_target_pairs={{4,0},{8,4},{12,8},{16,12},{20,16},{24,20},{28,24},{5,1},{9,5},{13... | collective-permute-start | bytes 98312 | tf_op jit(solution)/shard_map/ppermute | solution.py:22
  136.4 9.2 %collective-permute-start.7 = (bf16[32,18,2,1]{3,0,2,1:T(8,128)(2,1)S(1)}, bf16[32,18,2,1]{3,0,2,1:T(8,128)(2,1)S(1)}, u32[]{:S(2)}, u32[]{:S(2)}) collective-permute-start(bf16[32,18,2,1]{3,0,2,1:T(8,128)(2,1)S(1)} %get-tuple-element.190), channel_id=1, source_target_pairs={{0,1},{1,2},{2,3},{4,5},{5,6},{6,7},{8,9},{9,10},{10,11},{12,13},{... | collective-permute-start | bytes 6920 | tf_op jit(solution)/shard_map/ppermute | solution.py:21
  139.9 10.4 %collective-permute-start.8 = (bf16[32,18,2,1]{3,0,2,1:T(8,128)(2,1)S(1)}, bf16[32,18,2,1]{3,0,2,1:T(8,128)(2,1)S(1)}, u32[]{:S(2)}, u32[]{:S(2)}) collective-permute-start(bf16[32,18,2,1]{3,0,2,1:T(8,128)(2,1)S(1)} %get-tuple-element.191), channel_id=1, source_target_pairs={{1,0},{2,1},{3,2},{5,4},{6,5},{7,6},{9,8},{10,9},{11,10},{13,12},{... | collective-permute-start | bytes 6920 | tf_op jit(solution)/shard_map/ppermute | solution.py:22
  157.0 10.1 %copy-start.3 = (bf16[32,32,3,3,3]{1,0,4,3,2:T(8,128)(2,1)S(1)}, bf16[32,32,3,3,3]{1,0,4,3,2:T(8,128)(2,1)}, u32[]{:S(2)}) copy-start(bf16[32,32,3,3,3]{1,0,4,3,2:T(8,128)(2,1)} %param.13) | copy-start | bytes 165892
  183.3 4.4 %collective-permute-start.9 = (bf16[32,1,2,256]{3,0,2,1:T(8,128)(2,1)S(1)}, bf16[32,1,2,256]{3,0,2,1:T(8,128)(2,1)S(1)}, u32[]{:S(2)}, u32[]{:S(2)}) collective-permute-start(bf16[32,1,2,256]{3,0,2,1:T(8,128)(2,1)S(1)} %get-tuple-element.192), channel_id=1, source_target_pairs={{0,4},{4,8},{8,12},{12,16},{16,20},{20,24},{24,28},{1,5},{5,9},{9,... | collective-permute-start | bytes 98312 | tf_op jit(solution)/shard_map/ppermute | solution.py:21
  186.4 3.4 %collective-permute-start.10 = (bf16[32,1,2,256]{3,0,2,1:T(8,128)(2,1)S(1)}, bf16[32,1,2,256]{3,0,2,1:T(8,128)(2,1)S(1)}, u32[]{:S(2)}, u32[]{:S(2)}) collective-permute-start(bf16[32,1,2,256]{3,0,2,1:T(8,128)(2,1)S(1)} %get-tuple-element.193), channel_id=1, source_target_pairs={{4,0},{8,4},{12,8},{16,12},{20,16},{24,20},{28,24},{5,1},{9,5},{13... | collective-permute-start | bytes 98312 | tf_op jit(solution)/shard_map/ppermute | solution.py:22
  190.1 7.6 %collective-permute-start.11 = (bf16[32,18,2,1]{3,0,2,1:T(8,128)(2,1)S(1)}, bf16[32,18,2,1]{3,0,2,1:T(8,128)(2,1)S(1)}, u32[]{:S(2)}, u32[]{:S(2)}) collective-permute-start(bf16[32,18,2,1]{3,0,2,1:T(8,128)(2,1)S(1)} %get-tuple-element.188), channel_id=1, source_target_pairs={{0,1},{1,2},{2,3},{4,5},{5,6},{6,7},{8,9},{9,10},{10,11},{12,13},{... | collective-permute-start | bytes 6920 | tf_op jit(solution)/shard_map/ppermute | solution.py:21
  192.3 10.0 %collective-permute-start.12 = (bf16[32,18,2,1]{3,0,2,1:T(8,128)(2,1)S(1)}, bf16[32,18,2,1]{3,0,2,1:T(8,128)(2,1)S(1)}, u32[]{:S(2)}, u32[]{:S(2)}) collective-permute-start(bf16[32,18,2,1]{3,0,2,1:T(8,128)(2,1)S(1)} %get-tuple-element.189), channel_id=1, source_target_pairs={{1,0},{2,1},{3,2},{5,4},{6,5},{7,6},{9,8},{10,9},{11,10},{13,12},{... | collective-permute-start | bytes 6920 | tf_op jit(solution)/shard_map/ppermute | solution.py:22
  209.0 10.1 %copy-start.4 = (bf16[32,32,3,3,3]{1,0,4,3,2:T(8,128)(2,1)S(1)}, bf16[32,32,3,3,3]{1,0,4,3,2:T(8,128)(2,1)}, u32[]{:S(2)}) copy-start(bf16[32,32,3,3,3]{1,0,4,3,2:T(8,128)(2,1)} %param.14) | copy-start | bytes 165892
  228.6 48.1 %copy-start.1 = (bf16[32,40,3,3,3]{1,0,4,3,2:T(8,128)(2,1)S(1)}, bf16[32,40,3,3,3]{1,0,4,3,2:T(8,128)(2,1)}, u32[]{:S(2)}) copy-start(bf16[32,40,3,3,3]{1,0,4,3,2:T(8,128)(2,1)} %param.12) | copy-start | bytes 207364
  234.4 3.5 %copy-start.2 = (f32[32]{0:T(128)S(1)}, f32[32]{0:T(128)}, u32[]{:S(2)}) copy-start(f32[32]{0:T(128)} %param.15) | copy-start | bytes 388
where the time goes:
time: 278 us; the launch traced here: 277 us
  local copies, waits for them, and re-layouts  85.1 us (31%)
  other arithmetic  48.5 us (17%)
  waiting for transfers between devices  34.5 us (12%)
  blocking collectives  32.1 us (12%)
  matrix products  32.1 us (12%)
  starting transfers between devices  29.7 us (11%)
  loops' own time  13.6 us (5%)
    conv_general_dilated x9, local copies, waits for them, and re-layouts, convolve(): lax.conv_general_dilated(padded[None], kernel, (1, 1, 1), 'VALID', dimens...  47.8 us
    conv_general_dilated x3, matrix products, convolve(): lax.conv_general_dilated(padded[None], kernel, (1, 1, 1), 'VALID', dimens...  32.1 us
    ppermute x6, waiting for transfers between devices, with_halo(): after = lax.ppermute(initial, axis, down)  20.9 us
    add x128, other arithmetic, add_term(): return running + weight[None] * shifted.astype(jnp.float32)  19.7 us
    ppermute x6, starting transfers between devices, with_halo(): before = lax.ppermute(last, axis, up)  17.8 us
    ppermute x6, waiting for transfers between devices, with_halo(): before = lax.ppermute(last, axis, up)  13.5 us
    all_gather x1, blocking collectives, shards(): every_score = lax.all_gather(scores, 'disp', axis=0, tiled=True)  11.6 us
    all_gather x1, blocking collectives, shards(): lax.all_gather(right_feat, 'disp', axis=0, tiled=True)  11.3 us
  transfers between devices with their start and end apart: 13, of which 9 were waited for; matrix products, arithmetic and copies ran while one was open for 0% of the time, Pallas kernels for 0%

commit v1 on v0

v1 whole, which is shorter than its diff:
```python
import functools

import jax
import jax.numpy as jnp
from jax import lax
from jax.experimental import pallas as pl
from jax.experimental.pallas import tpu as pltpu
from jax.sharding import PartitionSpec as P

DG = 16
CG = 8
LANES = 128
KROWS = 256

masked_value = -1e30


def round_up(value, unit):
    return -(-value // unit) * unit


class Dims:
    def __init__(self, left, conv1, conv2, groups_disp, strips):
        own, self.h, self.strip = left
        self.n = groups_disp
        self.strips = strips
        self.own_rows = own * self.h
        self.rows = self.own_rows * self.n
        self.d = DG * self.n
        self.bw = self.strip // self.n
        self.mw = self.bw + 6
        self.tail = self.d + 2
        self.g = conv1[1]
        self.f = conv2[0]
        self.lo = round_up(self.mw + self.d - 1, 8)
        self.lb = self.lo // LANES * LANES
        self.lw = round_up(self.lo + self.mw, LANES)
        self.hops = []
        left_over = self.tail
        while left_over > 0:
            self.hops.append(min(left_over, self.strip))
            left_over -= self.strip
        per = KROWS // (CG * self.h)
        self.chunks = [min(per, self.g - k) for k in range(0, self.g, per)]
        self.lg = LANES // self.bw
        self.rg = round_up(-(-(self.own_rows + self.h) // self.lg), 8)


def lane_iota(shape):
    return lax.broadcasted_iota(jnp.int32, shape, 1)


def widen(x, lanes):
    have = x.shape[1]
    if have == lanes:
        return x
    return jnp.concatenate([x, jnp.zeros((x.shape[0], lanes - have), x.dtype)], axis=1)


def rolled(x, shift):
    shift %= x.shape[1]
    return x if shift == 0 else pltpu.roll(x, shift, 1)


def edge_kernel(dm, left_ref, right_ref, *outs):
    left = left_ref[...].astype(jnp.float32)
    right = right_ref[...].astype(jnp.float32)
    for k, count in enumerate(dm.hops):
        out = outs[k]
        width = out.shape[1]
        block = rolled(widen(right, max(width, dm.strip)), count - dm.strip)[:, :width]
        lane = lane_iota(block.shape)
        if k == 0:
            edge = rolled(widen(left, max(width, dm.strip)), count + 3 - dm.strip)[:, :width]
            block = jnp.where(lane < count, block, edge)
        out[...] = block.astype(out.dtype)
    out = outs[-1]
    first = right[:, :LANES]
    second = rolled(left[:, :LANES], 3)
    out[...] = jnp.where(lane_iota(first.shape) < 3, first, second).astype(out.dtype)


def pack_kernel(dm, left_ref, right_ref, *refs):
    ups, down_ref, out_ref = refs[: len(dm.hops)], refs[-2], refs[-1]
    left = left_ref[...].astype(jnp.float32)
    right = right_ref[...].astype(jnp.float32)
    down = down_ref[...].astype(jnp.float32)
    ext = round_up(dm.tail + dm.strip + 3, LANES)
    ext = max(ext, dm.lw)
    lane = lane_iota((dm.own_rows, ext))
    row = rolled(widen(right, ext), dm.tail)
    row = jnp.where(lane < dm.tail + dm.strip, row, rolled(widen(down, ext), dm.tail + dm.strip))
    for k, count in enumerate(dm.hops):
        start = dm.tail - sum(dm.hops[: k + 1])
        piece = rolled(widen(ups[k][...].astype(jnp.float32), ext), start)
        row = jnp.where((lane >= start) & (lane < start + count), piece, row)
    lext = max(round_up(dm.strip + 6, LANES), dm.lw)
    lane_l = lane_iota((dm.own_rows, lext))
    lrow = rolled(widen(left, lext), 3)
    edge = rolled(widen(ups[0][...].astype(jnp.float32), max(lext, ups[0].shape[1])), -dm.hops[0])
    lrow = jnp.where(lane_l < 3, edge[:, :lext], lrow)
    lrow = jnp.where(lane_l >= dm.strip + 3, rolled(widen(down, lext), dm.strip), lrow)
    lane_o = lane_iota((dm.own_rows, dm.lw))
    for j in range(dm.n):
        a = rolled(row, -dm.bw * j)[:, : dm.lw]
        b = rolled(lrow, dm.lo - dm.bw * j)[:, : dm.lw]
        out_ref[j] = jnp.where(lane_o < dm.lo, a, b).astype(out_ref.dtype)


def prep_kernel(dm, w1_ref, w2_ref, w3_ref, o1_ref, o2_ref, o3_ref):
    for layer, (w_ref, o_ref) in enumerate(((w1_ref, o1_ref), (w2_ref, o2_ref), (w3_ref, o3_ref))):
        inputs = w_ref.shape[2]
        per_a = dm.h * inputs
        shape = (inputs, 3 * per_a)
        i = lax.broadcasted_iota(jnp.int32, shape, 0)
        col = lane_iota(shape)
        total = None
        for a in range(3):
            for hi in range(dm.h):
                if layer == 0:
                    pos = jnp.zeros(shape, jnp.int32)
                    first = 0
                    for count in dm.chunks:
                        here = first * dm.h + hi * count + (i - first)
                        pos = jnp.where(i >= first, here, pos)
                        first += count
                else:
                    pos = hi * inputs + i
                place = jnp.where(col == a * per_a + pos, 1.0, 0.0).astype(jnp.bfloat16)
                blocks = []
                for e in range(3):
                    for ho in range(dm.h):
                        b = hi - ho + 1
                        if 0 <= b <= 2:
                            blocks.append(w_ref[(a * 3 + b) * 3 + e])
                        else:
                            blocks.append(jnp.zeros((dm.f, inputs), jnp.bfloat16))
                term = jnp.dot(
                    jnp.concatenate(blocks, axis=0), place, preferred_element_type=jnp.float32
                )
                total = term if total is None else total + term
        o_ref[...] = total.astype(o_ref.dtype)


def main_kernel(dm, x_ref, w1_ref, w2_ref, w3_ref, head_ref, out_ref, lt_ref, lhs_ref, pc_ref, a1_ref, a2_ref, a3_ref, ps_ref, s_ref):
    d, mw, h, f = dm.d, dm.mw, dm.h, dm.f
    base = lax.axis_index("col") * dm.strip + lax.axis_index("disp") * dm.bw
    total = dm.strips * dm.strip

    lt_ref[...] = jnp.transpose(x_ref[:, dm.lb : dm.lw].astype(jnp.float32))

    first = 0
    for k, count in enumerate(dm.chunks):
        r = count * h
        q = count * CG * h
        lane = lane_iota((r, q))
        sub = lax.broadcasted_iota(jnp.int32, (r, q), 0)
        keep = (lane % h == sub // count) & (lane // (CG * h) == sub % count)
        for m in range(mw):
            at = dm.lo - dm.lb + m
            line = jnp.broadcast_to(lt_ref[at : at + 1, first : first + q], (r, q))
            lhs_ref[m * r : (m + 1) * r, :q] = jnp.where(keep, line, 0.0).astype(jnp.bfloat16)
        pc_ref[k, : mw * r] = jnp.dot(
            lhs_ref[: mw * r, :q], x_ref[first : first + q, :], preferred_element_type=jnp.float32
        )
        first += q

    lane_d = {}

    def spread(ref, m, v):
        rows = v.shape[0]
        if rows not in lane_d:
            lane_d[rows] = lane_iota((rows, d))
        lane = lane_d[rows]
        at = slice(m * d, (m + 1) * d)
        ref[:rows, at] = jnp.where(lane < d - 1, rolled(v, -1), 0.0).astype(jnp.bfloat16)
        ref[rows : 2 * rows, at] = v.astype(jnp.bfloat16)
        ref[2 * rows :, at] = jnp.where(lane > 0, rolled(v, 1), 0.0).astype(jnp.bfloat16)

    for m in range(mw):
        parts = [pc_ref[k, m * c * h : (m + 1) * c * h] for k, c in enumerate(dm.chunks)]
        block = jnp.concatenate(parts, axis=0)
        spread(a1_ref, m, rolled(block, -m)[:, :d] * (1.0 / CG))

    step = 4 * LANES

    def layer(w_ref, a_ref, columns, emit):
        width = columns * d
        for t in range(0, width, step):
            size = min(step, width - t)
            ps_ref[:, t : t + size] = jnp.dot(
                w_ref[...], a_ref[:, t : t + size], preferred_element_type=jnp.float32
            )
        fh = f * h
        for m in range(1, columns - 1):
            z = ps_ref[:fh, (m - 1) * d : m * d]
            z = z + ps_ref[fh : 2 * fh, m * d : (m + 1) * d]
            z = z + ps_ref[2 * fh :, (m + 1) * d : (m + 2) * d]
            emit(m - 1, jnp.maximum(z, 0.0))

    def inside(column, z):
        if 3 <= column < mw - 3:
            return z
        at = base - 3 + column
        return jnp.where((at >= 0) & (at < total), z, 0.0)

    layer(w1_ref, a1_ref, mw, lambda m, z: spread(a2_ref, m, inside(m + 1, z)))
    layer(w2_ref, a2_ref, mw - 2, lambda m, z: spread(a3_ref, m, inside(m + 2, z)))

    head = head_ref[...]

    def score(m, z):
        z = z * head
        for row in range(h):
            s_ref[row, m : m + 1, :] = jnp.sum(z[row * f : (row + 1) * f], axis=0, keepdims=True)

    layer(w3_ref, a3_ref, mw - 4, score)

    disp = (d - 1) - lane_iota((dm.bw, d))
    column = base + lax.broadcasted_iota(jnp.int32, (dm.bw, d), 0)
    valid = column >= disp
    disp_f = disp.astype(jnp.float32)
    bands, disparity = [], []
    for row in range(h):
        s = jnp.where(valid, s_ref[row], masked_value)
        top = jnp.max(s, axis=1, keepdims=True)
        weighting = jnp.where(valid, jnp.exp(s - top), 0.0)
        denominator = jnp.sum(weighting, axis=1, keepdims=True)
        disp_sum = jnp.sum(weighting * disp_f, axis=1, keepdims=True)
        disparity.append(disp_sum / denominator / d)
        band = widen(weighting / denominator, dm.lw)
        bands.append(pltpu.roll(band, 3, 1, stride=1, stride_axis=0))
    band = jnp.concatenate(bands, axis=0)
    high = band.astype(jnp.bfloat16)
    low = (band - high.astype(jnp.float32)).astype(jnp.bfloat16)
    sums = lax.dot_general(
        x_ref[...],
        jnp.concatenate([high, low], axis=0),
        (((1,), (1,)), ((), ())),
        preferred_element_type=jnp.float32,
    )
    hb = h * dm.bw
    sums = widen(sums, round_up(2 * hb, LANES))
    sums = sums + rolled(sums, -hb)
    row = lax.broadcasted_iota(jnp.int32, sums.shape, 0) % h
    warped = sums
    for k in range(1, h):
        warped = jnp.where(row == k, rolled(sums, -k * dm.bw), warped)
    warped = warped[:, :LANES]

    eye = lane_iota((dm.bw, LANES)) == lax.broadcasted_iota(jnp.int32, (dm.bw, LANES), 0)
    lines = [jnp.sum(jnp.where(eye, v, 0.0), axis=0, keepdims=True) for v in disparity]
    lines.append(jnp.zeros((dm.lg * dm.rg - dm.own_rows - h, LANES), jnp.float32))
    lines = jnp.concatenate(lines, axis=0)
    lane = lane_iota((dm.rg, LANES))
    for j in range(dm.n):
        mine = jnp.concatenate([warped[j * dm.own_rows : (j + 1) * dm.own_rows], lines], axis=0)
        packed = mine[: dm.rg]
        for g in range(1, dm.lg):
            packed = jnp.where(
                (lane >= g * dm.bw) & (lane < (g + 1) * dm.bw),
                rolled(mine[g * dm.rg : (g + 1) * dm.rg], g * dm.bw),
                packed,
            )
        out_ref[j] = packed


def unpack_kernel(dm, y_ref, warped_ref, disparity_ref):
    per = LANES // dm.bw
    lane = lane_iota((dm.rg, LANES))
    tiles = []
    for t in range(dm.n // per):
        groups = []
        for g in range(dm.lg):
            total = None
            for p in range(per):
                piece = rolled(y_ref[t * per + p], (p - g) * dm.bw)
                keep = (lane >= p * dm.bw) & (lane < (p + 1) * dm.bw)
                total = piece if total is None else jnp.where(keep, piece, total)
            groups.append(total)
        tiles.append(jnp.concatenate(groups, axis=0))
    full = jnp.concatenate(tiles, axis=1)
    warped_ref[...] = full[: dm.own_rows].astype(warped_ref.dtype)
    disparity_ref[...] = full[dm.own_rows : dm.own_rows + dm.h]


def shards(left_feat, right_feat, conv1_w, conv2_w, conv3_w, head_w):
    n, strips = lax.axis_size("disp"), lax.axis_size("col")
    dm = Dims(left_feat.shape, conv1_w.shape, conv2_w.shape, n, strips)
    bf, f32 = jnp.bfloat16, jnp.float32
    left = left_feat.reshape(dm.own_rows, dm.strip)
    right = right_feat.reshape(dm.own_rows, dm.strip)

    widths = [round_up(c + (3 if k == 0 else 0), LANES) for k, c in enumerate(dm.hops)]
    edges = pl.pallas_call(
        functools.partial(edge_kernel, dm),
        out_shape=[jax.ShapeDtypeStruct((dm.own_rows, w), bf) for w in widths + [LANES]],
    )(left, right)
    ups = [
        lax.ppermute(e, "col", [(s, s + k + 1) for s in range(strips - k - 1)])
        for k, e in enumerate(edges[:-1])
    ]
    down = lax.ppermute(edges[-1], "col", [(s + 1, s) for s in range(strips - 1)])

    kernels = [w.transpose(2, 3, 4, 0, 1).reshape(27, w.shape[0], w.shape[1]) for w in (conv1_w, conv2_w, conv3_w)]
    m3 = 3 * dm.h * dm.f
    depths = [3 * dm.h * w.shape[2] for w in kernels]
    w1, w2, w3 = pl.pallas_call(
        functools.partial(prep_kernel, dm),
        out_shape=[jax.ShapeDtypeStruct((m3, k), bf) for k in depths],
    )(*kernels)

    send = pl.pallas_call(
        functools.partial(pack_kernel, dm),
        out_shape=jax.ShapeDtypeStruct((n, dm.own_rows, dm.lw), bf),
    )(left, right, *ups, down)
    x = lax.all_to_all(send, "disp", 0, 0).reshape(dm.rows, dm.lw)

    head = jnp.broadcast_to(jnp.tile(head_w, dm.h)[:, None], (dm.h * dm.f, dm.d))
    r_max = max(dm.chunks) * dm.h
    columns = [dm.mw, dm.mw - 2, dm.mw - 4]
    packed = pl.pallas_call(
        functools.partial(main_kernel, dm),
        out_shape=jax.ShapeDtypeStruct((n, dm.rg, LANES), f32),
        scratch_shapes=[
            pltpu.VMEM((dm.lw - dm.lb, dm.rows), f32),
            pltpu.VMEM((dm.mw * r_max, KROWS), bf),
            pltpu.VMEM((len(dm.chunks), dm.mw * r_max, dm.lw), f32),
            pltpu.VMEM((depths[0], columns[0] * dm.d), bf),
            pltpu.VMEM((depths[1], columns[1] * dm.d), bf),
            pltpu.VMEM((depths[2], columns[2] * dm.d), bf),
            pltpu.VMEM((m3, columns[0] * dm.d), f32),
            pltpu.VMEM((dm.h, dm.bw, dm.d), f32),
        ],
    )(x, w1, w2, w3, head)
    y = lax.all_to_all(packed, "disp", 0, 0)
    warped, disparity = pl.pallas_call(
        functools.partial(unpack_kernel, dm),
        out_shape=[
            jax.ShapeDtypeStruct((dm.own_rows, dm.strip), bf),
            jax.ShapeDtypeStruct((dm.h, dm.strip), f32),
        ],
    )(y)
    return (warped.reshape(left_feat.shape), disparity)


def solution(mesh):
    return jax.shard_map(
        shards,
        mesh=mesh,
        in_specs=(P("disp", None, "col"), P("disp", None, "col"), P(), P(), P(), P()),
        out_specs=(P("disp", None, "col"), P(None, "col")),
        check_vma=False,
    )
```

time: 278 us -> 49.7 us (0.18)
  local copies, waits for them, and re-layouts: 85.1 us -> 5.5 us
  other arithmetic: 48.5 us -> 0 us
  matrix products: 32.1 us -> 0 us
  waiting for transfers between devices: 34.5 us -> 9.85 us
  blocking collectives: 32.1 us -> 9.16 us
  starting transfers between devices: 29.7 us -> 10.1 us
  Pallas kernels: 0 us -> 13.8 us
  loops' own time: 13.6 us -> 0 us
    conv_general_dilated x9 -> x0, local copies, waits for them, and re-layouts: 47.8 us -> none  [convolve(): lax.conv_general_dilated(padded[None], kernel, (1, 1, 1), 'VALID', dimens...]
    all_gather x3 -> x0, blocking collectives: 32.1 us -> none  [the longest x1 11.6 us: shards(): every_score = lax.all_gather(scores, 'disp', axis=0, tiled=True)]
    conv_general_dilated x3 -> x0, matrix products: 32.1 us -> none  [convolve(): lax.conv_general_dilated(padded[None], kernel, (1, 1, 1), 'VALID', dimens...]
    ppermute x13 -> x2, waiting for transfers between devices: 34.5 us -> 4.59 us  [the longest x1 4.59 us: shards(): lax.ppermute(edges[-1], 'col', [(s + 1, s) for s in range(strips - 1)])]
    ppermute x13 -> x2, starting transfers between devices: 29.7 us -> 6.24 us  [the longest x1 4.95 us: shards(): lax.ppermute(e, 'col', [(s, s + k + 1) for s in range(strips - k - 1)])]
    add x130 -> x0, other arithmetic: 19.7 us -> none  [the longest x128 19.7 us: add_term(): return running + weight[None] * shifted.astype(jnp.float32)]
    convert_element_type x6 -> x0, local copies, waits for them, and re-layouts: 14.1 us -> none  [the longest x3 7.07 us: shards(): activity = layer_step(volume, conv1_w).astype(jnp.bfloat16)]
    pallas_call x0 -> x5, Pallas kernels: none -> 13.8 us  [the longest x1 6.55 us: shards(): pl.pallas_call(functools.partial(main_kernel, dm), out_shape=jax.ShapeDty...]
  transfers between devices with their start and end apart: 13 -> 3, of which waited for: 9 -> 2; matrix products, arithmetic and copies ran while one was open for 0% -> 0% of each run, Pallas kernels for 0% -> 5%
where the time goes in v1:
time: 49.7 us; the launch traced here: 49.1 us
  Pallas kernels  13.8 us (28%)
  starting transfers between devices  10.1 us (20%)
  waiting for transfers between devices  9.85 us (20%)
  blocking collectives  9.16 us (18%)
  local copies, waits for them, and re-layouts  5.5 us (11%)
  between operations  0.68 us (1%)
    all_to_all x1, blocking collectives, shards(): y = lax.all_to_all(packed, 'disp', 0, 0)  9.16 us
    pallas_call x1, Pallas kernels, shards(): pl.pallas_call(functools.partial(main_kernel, dm), out_shape=jax.ShapeDty...  6.55 us
    all_to_all x1, waiting for transfers between devices, shards(): x = lax.all_to_all(send, 'disp', 0, 0).reshape(dm.rows, dm.lw)  5.26 us
    ppermute x1, starting transfers between devices, shards(): lax.ppermute(e, 'col', [(s, s + k + 1) for s in range(strips - k - 1)])  4.95 us
    ppermute x1, waiting for transfers between devices, shards(): lax.ppermute(edges[-1], 'col', [(s + 1, s) for s in range(strips - 1)])  4.59 us
    all_to_all x1, starting transfers between devices, shards(): x = lax.all_to_all(send, 'disp', 0, 0).reshape(dm.rows, dm.lw)  3.85 us
    pallas_call x1, Pallas kernels, shards(): pl.pallas_call(functools.partial(prep_kernel, dm), out_shape=[jax.ShapeDt...  2.25 us
    pallas_call x1, Pallas kernels, shards(): pl.pallas_call(functools.partial(pack_kernel, dm), out_shape=jax.ShapeDty...  1.84 us
  transfers between devices with their start and end apart: 3, of which 2 were waited for; matrix products, arithmetic and copies ran while one was open for 0% of the time, Pallas kernels for 5%

profile of v1, /device:TPU:0, one launch (start us, length us, event | category | flops | bytes accessed | tf_op | source)
XLA Modules:
  0.0 49.1 jit_solution(5718067648934945620)
XLA Ops:
  0.6 0.0 copy-start.2
  0.6 1.4 %reshape.27.left_ref = bf16[80,256]{1,0:T(8,128)(2,1)} reshape(bf16[40,2,256]{2,1,0:T(2,128)(2,1)} %param.6) | data formatting | bytes 81920 | tf_op jit(solution)/shard_map/reshape | solution.py:291
  2.1 0.0 copy-done.2
  2.1 0.6 %reshape.28.right_ref = bf16[80,256]{1,0:T(8,128)(2,1)} reshape(bf16[40,2,256]{2,1,0:T(2,128)(2,1)S(1)} %copy-done.2) | data formatting | bytes 81920 | tf_op jit(solution)/shard_map/reshape | solution.py:292
  2.7 1.5 %shard_map.77 = (bf16[80,256]{1,0:T(8,128)(2,1)}, bf16[80,128]{1,0:T(8,128)(2,1)}) custom-call(bf16[80,256]{1,0:T(8,128)(2,1)} %reshape.27.left_ref, bf16[80,256]{1,0:T(8,128)(2,1)} %reshape.28.right_ref), custom_call_target="tpu_custom_call" | custom-call | tf_op jit(solution)/shard_map/pallas_call | solution.py:295
  4.2 4.9 %collective-permute-start = (bf16[80,256]{1,0:T(8,128)(2,1)}, bf16[80,256]{1,0:T(8,128)(2,1)S(1)}, u32[]{:S(2)}, u32[]{:S(2)}) collective-permute-start(bf16[80,256]{1,0:T(8,128)(2,1)} %get-tuple-element.9), channel_id=1, source_target_pairs={{0,1},{1,2},{2,3},{4,5},{5,6},{6,7},{8,9},{9,10},{10,11},{12,13},{... | collective-permute-start | bytes 122888 | tf_op jit(solution)/shard_map/ppermute | solution.py:300
  9.2 1.3 %collective-permute-start.1 = (bf16[80,128]{1,0:T(8,128)(2,1)}, bf16[80,128]{1,0:T(8,128)(2,1)S(1)}, u32[]{:S(2)}, u32[]{:S(2)}) collective-permute-start(bf16[80,128]{1,0:T(8,128)(2,1)} %get-tuple-element.10), channel_id=1, source_target_pairs={{1,0},{2,1},{3,2},{5,4},{6,5},{7,6},{9,8},{10,9},{11,10},{13,12},{... | collective-permute-start | bytes 61448 | tf_op jit(solution)/shard_map/ppermute | solution.py:303
  10.5 4.6 %collective-permute-done.1.refs_1_ = bf16[80,128]{1,0:T(8,128)(2,1)S(1)} collective-permute-done((bf16[80,128]{1,0:T(8,128)(2,1)}, bf16[80,128]{1,0:T(8,128)(2,1)S(1)}, u32[]{:S(2)}, u32[]{:S(2)}) %collective-permute-start.1) | collective-permute-done | bytes 20512 | tf_op jit(solution)/shard_map/ppermute | solution.py:303
  15.1 0.0 copy-start.3
  15.1 0.0 collective-permute-done.refs_0_
  15.1 0.6 %copy-done.3 = bf16[80,128]{1,0:T(8,128)(2,1)} copy-done((bf16[80,128]{1,0:T(8,128)(2,1)}, bf16[80,128]{1,0:T(8,128)(2,1)S(1)}, u32[]{:S(2)}) %copy-start.3) | copy-done | bytes 20504
  15.7 0.6 %copy-done.1 = bf16[80,256]{1,0:T(8,128)(2,1)} copy-done((bf16[80,256]{1,0:T(8,128)(2,1)}, bf16[80,256]{1,0:T(8,128)(2,1)S(1)}, u32[]{:S(2)}) %copy-start.1) | copy-done | bytes 40984
  16.3 1.8 %shard_map.78 = bf16[8,80,256]{2,1,0:T(8,128)(2,1)} custom-call(bf16[80,256]{1,0:T(8,128)(2,1)} %reshape.27.left_ref, bf16[80,256]{1,0:T(8,128)(2,1)} %reshape.28.right_ref, bf16[80,256]{1,0:T(8,128)(2,1)} %copy-done.1, bf16[80,128]{1,0:T(8,128)(2,1)} %copy-done.3), custom_call_target="tpu_custom_call" | custom-call | tf_op jit(solution)/shard_map/pallas_call | solution.py:313
  18.1 3.9 %all-to-all-start = ((bf16[8,80,256]{2,1,0:T(8,128)(2,1)}), bf16[8,80,256]{2,1,0:T(8,128)(2,1)S(1)}, u32[]{:S(2)}, u32[]{:S(2)}) async-start(bf16[8,80,256]{2,1,0:T(8,128)(2,1)} %shard_map.78), calls=%async_computation | async-start | bytes 655360 | tf_op jit(solution)/shard_map/all_to_all | solution.py:317
  22.0 0.0 copy-done.4
  22.0 0.1 broadcast_in_dim.7
  22.1 2.2 %shard_map.79 = (bf16[192,240]{1,0:T(8,128)(2,1)}, bf16[192,192]{1,0:T(8,128)(2,1)}, bf16[192,192]{1,0:T(8,128)(2,1)}) custom-call(bf16[27,32,40]{2,1,0:T(8,128)(2,1)} %bitcast.11, bf16[27,32,32]{2,1,0:T(8,128)(2,1)} %bitcast.12, bf16[27,32,32]{2,1,0:T(8,128)(2,1)} %bitcast.13), custom_call_target="tpu_custom_call" | custom-call | tf_op jit(solution)/shard_map/pallas_call | solution.py:308
  24.3 5.3 %all-to-all-done = bf16[8,80,256]{2,1,0:T(8,128)(2,1)S(1)} async-done(((bf16[8,80,256]{2,1,0:T(8,128)(2,1)}), bf16[8,80,256]{2,1,0:T(8,128)(2,1)S(1)}, u32[]{:S(2)}, u32[]{:S(2)}) %all-to-all-start) | async-done | bytes 327712 | tf_op jit(solution)/shard_map/all_to_all | solution.py:317
  29.6 0.7 %broadcast_in_dim.8.head_ref = f32[64,128]{1,0:T(8,128)} broadcast(f32[64]{0:T(128)S(1)} %broadcast_in_dim.7), dimensions={0} | broadcast | bytes 33024 | tf_op jit(solution)/shard_map/broadcast_in_dim | solution.py:319
  30.3 0.0 copy-done
  30.3 6.6 %shard_map.80 = f32[8,24,128]{2,1,0:T(8,128)} custom-call(bf16[640,256]{1,0:T(8,128)(2,1)} %bitcast.10, bf16[192,240]{1,0:T(8,128)(2,1)} %get-tuple-element.11.w1_ref, bf16[192,192]{1,0:T(8,128)(2,1)} %get-tuple-element.12.w2_ref, bf16[192,192]{1,0:T(8,128)(2,1)} %get-tuple-element.13.w3_ref, f32[64,128]{1,0:T(8,128)} %broadcast_in_dim.8.head_ref), custom_call_target="tpu_custom_call" | custom-call | tf_op jit(solution)/shard_map/pallas_call | solution.py:322
  36.9 9.2 %all_to_all.10.y_ref = f32[8,24,128]{2,1,0:T(8,128)} all-to-all(f32[8,24,128]{2,1,0:T(8,128)} %shard_map.80), channel_id=1, replica_groups=mesh['disp'=8,'col'=4] {'disp'}, dimensions={0} | all-to-all | bytes 196608 | tf_op jit(solution)/shard_map/all_to_all | solution.py:336
  46.0 1.6 %shard_map.81 = (bf16[80,256]{1,0:T(8,128)(2,1)}, f32[2,256]{1,0:T(2,128)}) custom-call(f32[8,24,128]{2,1,0:T(8,128)} %all_to_all.10.y_ref), custom_call_target="tpu_custom_call" | custom-call | tf_op jit(solution)/shard_map/pallas_call | solution.py:337
  47.6 1.4 %reshape.33 = bf16[40,2,256]{2,1,0:T(2,128)(2,1)} reshape(bf16[80,256]{1,0:T(8,128)(2,1)} %get-tuple-element.14) | data formatting | bytes 81920 | tf_op jit(solution)/shard_map/reshape | solution.py:344
  (4 shorter events, 0.0 us)
Async XLA Ops:
  0.6 1.4 %copy-start.2 = (bf16[40,2,256]{2,1,0:T(2,128)(2,1)S(1)}, bf16[40,2,256]{2,1,0:T(2,128)(2,1)}, u32[]{:S(2)}) copy-start(bf16[40,2,256]{2,1,0:T(2,128)(2,1)} %param.7) | copy-start | bytes 122884
  4.2 10.8 %collective-permute-start = (bf16[80,256]{1,0:T(8,128)(2,1)}, bf16[80,256]{1,0:T(8,128)(2,1)S(1)}, u32[]{:S(2)}, u32[]{:S(2)}) collective-permute-start(bf16[80,256]{1,0:T(8,128)(2,1)} %get-tuple-element.9), channel_id=1, source_target_pairs={{0,1},{1,2},{2,3},{4,5},{5,6},{6,7},{8,9},{9,10},{10,11},{12,13},{... | collective-permute-start | bytes 122888 | tf_op jit(solution)/shard_map/ppermute | solution.py:300
  9.2 5.9 %collective-permute-start.1 = (bf16[80,128]{1,0:T(8,128)(2,1)}, bf16[80,128]{1,0:T(8,128)(2,1)S(1)}, u32[]{:S(2)}, u32[]{:S(2)}) collective-permute-start(bf16[80,128]{1,0:T(8,128)(2,1)} %get-tuple-element.10), channel_id=1, source_target_pairs={{1,0},{2,1},{3,2},{5,4},{6,5},{7,6},{9,8},{10,9},{11,10},{13,12},{... | collective-permute-start | bytes 61448 | tf_op jit(solution)/shard_map/ppermute | solution.py:303
  15.1 0.6 %copy-start.3 = (bf16[80,128]{1,0:T(8,128)(2,1)}, bf16[80,128]{1,0:T(8,128)(2,1)S(1)}, u32[]{:S(2)}) copy-start(bf16[80,128]{1,0:T(8,128)(2,1)S(1)} %collective-permute-done.1.refs_1_) | copy-start | bytes 61444
  15.7 0.6 %copy-start.1 = (bf16[80,256]{1,0:T(8,128)(2,1)}, bf16[80,256]{1,0:T(8,128)(2,1)S(1)}, u32[]{:S(2)}) copy-start(bf16[80,256]{1,0:T(8,128)(2,1)S(1)} %collective-permute-done.refs_0_) | copy-start | bytes 122884
  18.1 3.9 %copy-start.4 = (f32[32]{0:T(128)S(1)}, f32[32]{0:T(128)}, u32[]{:S(2)}) copy-start(f32[32]{0:T(128)} %param.11) | copy-start | bytes 388
  18.1 11.5 %all-to-all-start = ((bf16[8,80,256]{2,1,0:T(8,128)(2,1)}), bf16[8,80,256]{2,1,0:T(8,128)(2,1)S(1)}, u32[]{:S(2)}, u32[]{:S(2)}) async-start(bf16[8,80,256]{2,1,0:T(8,128)(2,1)} %shard_map.78), calls=%async_computation | async-start | bytes 655360 | tf_op jit(solution)/shard_map/all_to_all | solution.py:317
  29.6 0.7 %copy-start = (bf16[8,80,256]{2,1,0:T(8,128)(2,1)}, bf16[8,80,256]{2,1,0:T(8,128)(2,1)S(1)}, u32[]{:S(2)}) copy-start(bf16[8,80,256]{2,1,0:T(8,128)(2,1)S(1)} %all-to-all-done) | copy-start | bytes 983044

commit v2 on v1

--- a/solution.py
+++ b/solution.py
@@ -11,6 +11,7 @@
 CG = 8
 LANES = 128
 KROWS = 256
+VMEM = pl.BlockSpec(memory_space=pltpu.VMEM)
 
 masked_value = -1e30
 
@@ -62,43 +63,46 @@
     return x if shift == 0 else pltpu.roll(x, shift, 1)
 
 
+def flat(ref):
+    return ref[...].astype(jnp.float32).reshape(-1, ref.shape[-1])
+
+
 def edge_kernel(dm, left_ref, right_ref, *outs):
-    left = left_ref[...].astype(jnp.float32)
-    right = right_ref[...].astype(jnp.float32)
-    for k, count in enumerate(dm.hops):
-        out = outs[k]
-        width = out.shape[1]
-        block = rolled(widen(right, max(width, dm.strip)), count - dm.strip)[:, :width]
-        lane = lane_iota(block.shape)
-        if k == 0:
-            edge = rolled(widen(left, max(width, dm.strip)), count + 3 - dm.strip)[:, :width]
-            block = jnp.where(lane < count, block, edge)
-        out[...] = block.astype(out.dtype)
-    out = outs[-1]
-    first = right[:, :LANES]
-    second = rolled(left[:, :LANES], 3)
-    out[...] = jnp.where(lane_iota(first.shape) < 3, first, second).astype(out.dtype)
-
-
-def pack_kernel(dm, left_ref, right_ref, *refs):
-    ups, down_ref, out_ref = refs[: len(dm.hops)], refs[-2], refs[-1]
-    left = left_ref[...].astype(jnp.float32)
-    right = right_ref[...].astype(jnp.float32)
-    down = down_ref[...].astype(jnp.float32)
-    ext = round_up(dm.tail + dm.strip + 3, LANES)
-    ext = max(ext, dm.lw)
+    left, right = flat(left_ref), flat(right_ref)
+    width = outs[0].shape[1]
+    count = dm.hops[0]
+    lane = lane_iota((dm.own_rows, width))
+    last = rolled(widen(right, width), count - dm.strip)
+    edge = rolled(widen(left, width), count + 3 - dm.strip)
+    up = jnp.where(lane < count, last, edge)
+    down = jnp.where(lane < 3, widen(right, width), rolled(widen(left, width), 3))
+    even = lax.axis_index("col") % 2 == 0
+    outs[0][...] = jnp.where(even, up, down).astype(outs[0].dtype)
+    outs[1][...] = jnp.where(even, down, up).astype(outs[1].dtype)
+    for out, count in zip(outs[2:], dm.hops[1:]):
+        out[...] = rolled(right, count - dm.strip)[:, : out.shape[1]].astype(out.dtype)
+
+
+def pack_kernel(dm, left_ref, right_ref, pair0_ref, pair1_ref, *refs):
+    out_ref = refs[-1]
+    left, right = flat(left_ref), flat(right_ref)
+    pair0, pair1 = flat(pair0_ref), flat(pair1_ref)
+    even = lax.axis_index("col") % 2 == 0
+    up = jnp.where(even, pair1, pair0)
+    down = jnp.where(even, pair0, pair1)[:, :LANES]
+    ext = max(round_up(dm.tail + dm.strip + 3, LANES), dm.lw, up.shape[1])
     lane = lane_iota((dm.own_rows, ext))
     row = rolled(widen(right, ext), dm.tail)
     row = jnp.where(lane < dm.tail + dm.strip, row, rolled(widen(down, ext), dm.tail + dm.strip))
+    pieces = [up] + [flat(ref) for ref in refs[:-1]]
     for k, count in enumerate(dm.hops):
         start = dm.tail - sum(dm.hops[: k + 1])
-        piece = rolled(widen(ups[k][...].astype(jnp.float32), ext), start)
+        piece = rolled(widen(pieces[k], ext), start)
         row = jnp.where((lane >= start) & (lane < start + count), piece, row)
-    lext = max(round_up(dm.strip + 6, LANES), dm.lw)
+    lext = max(round_up(dm.strip + 6, LANES), dm.lw, up.shape[1])
     lane_l = lane_iota((dm.own_rows, lext))
     lrow = rolled(widen(left, lext), 3)
-    edge = rolled(widen(ups[0][...].astype(jnp.float32), max(lext, ups[0].shape[1])), -dm.hops[0])
-    lrow = jnp.where(lane_l < 3, edge[:, :lext], lrow)
+    lrow = jnp.where(lane_l < 3, rolled(widen(up, lext), -dm.hops[0]), lrow)
     lrow = jnp.where(lane_l >= dm.strip + 3, rolled(widen(down, lext), dm.strip), lrow)
     lane_o = lane_iota((dm.own_rows, dm.lw))
     for j in range(dm.n):
@@ -107,7 +111,7 @@
         out_ref[j] = jnp.where(lane_o < dm.lo, a, b).astype(out_ref.dtype)
 
 
-def prep_kernel(dm, w1_ref, w2_ref, w3_ref, o1_ref, o2_ref, o3_ref):
+def prep_kernel(dm, w1_ref, w2_ref, w3_ref, head_ref, o1_ref, o2_ref, o3_ref, column_ref):
     for layer, (w_ref, o_ref) in enumerate(((w1_ref, o1_ref), (w2_ref, o2_ref), (w3_ref, o3_ref))):
         inputs = w_ref.shape[2]
         per_a = dm.h * inputs
@@ -140,6 +144,11 @@
                 )
                 total = term if total is None else total + term
         o_ref[...] = total.astype(o_ref.dtype)
+    square = (dm.f, dm.f)
+    eye = lane_iota(square) == lax.broadcasted_iota(jnp.int32, square, 0)
+    column = jnp.sum(jnp.where(eye, head_ref[...], 0.0), axis=1, keepdims=True)
+    column = jnp.broadcast_to(column, (dm.f, dm.d))
+    column_ref[...] = jnp.concatenate([column] * dm.h, axis=0)
 
 
 def main_kernel(dm, x_ref, w1_ref, w2_ref, w3_ref, head_ref, out_ref, lt_ref, lhs_ref, pc_ref, a1_ref, a2_ref, a3_ref, ps_ref, s_ref):
@@ -280,7 +289,7 @@
             groups.append(total)
         tiles.append(jnp.concatenate(groups, axis=0))
     full = jnp.concatenate(tiles, axis=1)
-    warped_ref[...] = full[: dm.own_rows].astype(warped_ref.dtype)
+    warped_ref[...] = full[: dm.own_rows].reshape(warped_ref.shape).astype(warped_ref.dtype)
     disparity_ref[...] = full[dm.own_rows : dm.own_rows + dm.h]
 
 
@@ -288,40 +297,56 @@
     n, strips = lax.axis_size("disp"), lax.axis_size("col")
     dm = Dims(left_feat.shape, conv1_w.shape, conv2_w.shape, n, strips)
     bf, f32 = jnp.bfloat16, jnp.float32
-    left = left_feat.reshape(dm.own_rows, dm.strip)
-    right = right_feat.reshape(dm.own_rows, dm.strip)
-
-    widths = [round_up(c + (3 if k == 0 else 0), LANES) for k, c in enumerate(dm.hops)]
-    edges = pl.pallas_call(
-        functools.partial(edge_kernel, dm),
-        out_shape=[jax.ShapeDtypeStruct((dm.own_rows, w), bf) for w in widths + [LANES]],
-    )(left, right)
-    ups = [
-        lax.ppermute(e, "col", [(s, s + k + 1) for s in range(strips - k - 1)])
-        for k, e in enumerate(edges[:-1])
-    ]
-    down = lax.ppermute(edges[-1], "col", [(s + 1, s) for s in range(strips - 1)])
+
+    def call(kernel, out_shape, operands, mib=8, **options):
+        return pl.pallas_call(
+            functools.partial(kernel, dm),
+            out_shape=out_shape,
+            in_specs=[VMEM] * len(operands),
+            out_specs=jax.tree.map(lambda _: VMEM, out_shape),
+            compiler_params=pltpu.CompilerParams(vmem_limit_bytes=mib << 20),
+            **options,
+        )(*operands)
+
+    wide = max(round_up(dm.hops[0] + 3, LANES), dm.strip)
+    widths = [wide, wide] + [round_up(c, LANES) for c in dm.hops[1:]]
+    edges = call(
+        edge_kernel,
+        [jax.ShapeDtypeStruct((dm.own_rows, w), bf) for w in widths],
+        [left_feat, right_feat],
+    )
+    arrived = []
+    for first in range(2):
+        pairs = [(s, s + 1) for s in range(first, strips - 1, 2)]
+        pairs += [(b, a) for a, b in pairs]
+        arrived.append(lax.ppermute(edges[first], "col", pairs))
+    for k, e in enumerate(edges[2:], 2):
+        arrived.append(lax.ppermute(e, "col", [(s, s + k) for s in range(strips - k)]))
 
     kernels = [w.transpose(2, 3, 4, 0, 1).reshape(27, w.shape[0], w.shape[1]) for w in (conv1_w, conv2_w, conv3_w)]
     m3 = 3 * dm.h * dm.f
     depths = [3 * dm.h * w.shape[2] for w in kernels]
-    w1, w2, w3 = pl.pallas_call(
-        functools.partial(prep_kernel, dm),
-        out_shape=[jax.ShapeDtypeStruct((m3, k), bf) for k in depths],
-    )(*kernels)
-
-    send = pl.pallas_call(
-        functools.partial(pack_kernel, dm),
-        out_shape=jax.ShapeDtypeStruct((n, dm.own_rows, dm.lw), bf),
-    )(left, right, *ups, down)
+    w1, w2, w3, head = call(
+        prep_kernel,
+        [jax.ShapeDtypeStruct((m3, k), bf) for k in depths]
+        + [jax.ShapeDtypeStruct((dm.h * dm.f, dm.d), f32)],
+        kernels + [head_w[None]],
+    )
+
+    send = call(
+        pack_kernel,
+        jax.ShapeDtypeStruct((n, dm.own_rows, dm.lw), bf),
+        [left_feat, right_feat] + arrived,
+    )
     x = lax.all_to_all(send, "disp", 0, 0).reshape(dm.rows, dm.lw)
 
-    head = jnp.broadcast_to(jnp.tile(head_w, dm.h)[:, None], (dm.h * dm.f, dm.d))
     r_max = max(dm.chunks) * dm.h
     columns = [dm.mw, dm.mw - 2, dm.mw - 4]
-    packed = pl.pallas_call(
-        functools.partial(main_kernel, dm),
-        out_shape=jax.ShapeDtypeStruct((n, dm.rg, LANES), f32),
+    packed = call(
+        main_kernel,
+        jax.ShapeDtypeStruct((n, dm.rg, LANES), f32),
+        [x, w1, w2, w3, head],
+        mib=32,
         scratch_shapes=[
             pltpu.VMEM((dm.lw - dm.lb, dm.rows), f32),
             pltpu.VMEM((dm.mw * r_max, KROWS), bf),
@@ -332,16 +357,18 @@
             pltpu.VMEM((m3, columns[0] * dm.d), f32),
             pltpu.VMEM((dm.h, dm.bw, dm.d), f32),
         ],
-    )(x, w1, w2, w3, head)
+    )
     y = lax.all_to_all(packed, "disp", 0, 0)
-    warped, disparity = pl.pallas_call(
-        functools.partial(unpack_kernel, dm),
-        out_shape=[
-            jax.ShapeDtypeStruct((dm.own_rows, dm.strip), bf),
-            jax.ShapeDtypeStruct((dm.h, dm.strip), f32),
-        ],
-    )(y)
-    return (warped.reshape(left_feat.shape), disparity)
+    return tuple(
+        call(
+            unpack_kernel,
+            [
+                jax.ShapeDtypeStruct(left_feat.shape, bf),
+                jax.ShapeDtypeStruct((dm.h, dm.strip), f32),
+            ],
+            [y],
+        )
+    )
 
 
 def solution(mesh):

time: 49.7 us -> 36 us (0.72)
  the two profiles are of different devices: /device:TPU:0 before, /device:TPU:16 now
where the time goes in v2:
time: 36 us; the launch traced here: 35.6 us
  waiting for transfers between devices  10.4 us (29%)
  blocking collectives  7.58 us (21%)
  starting transfers between devices  7.4 us (21%)
  Pallas kernels  7.31 us (20%)
  local copies, waits for them, and re-layouts  2.18 us (6%)
  between operations  0.7 us (2%)
    all_to_all x1, blocking collectives, shards(): y = lax.all_to_all(packed, 'disp', 0, 0)  7.58 us
    pallas_call x5, Pallas kernels, call(): pl.pallas_call(functools.partial(kernel, dm), out_shape=out_shape, in_spe...  7.31 us
    all_to_all x1, waiting for transfers between devices, shards(): x = lax.all_to_all(send, 'disp', 0, 0).reshape(dm.rows, dm.lw)  6.47 us
    ppermute x2, waiting for transfers between devices, shards(): arrived.append(lax.ppermute(edges[first], 'col', pairs))  3.97 us
    all_to_all x1, starting transfers between devices, shards(): x = lax.all_to_all(send, 'disp', 0, 0).reshape(dm.rows, dm.lw)  3.85 us
    ppermute x2, starting transfers between devices, shards(): arrived.append(lax.ppermute(edges[first], 'col', pairs))  3.55 us
    unnamed x12, local copies, waits for them, and re-layouts  2.18 us
  transfers between devices with their start and end apart: 3, of which 3 were waited for; matrix products, arithmetic and copies ran while one was open for 0% of the time, Pallas kernels for 1%

profile of v2, /device:TPU:16, one launch (start us, length us, event | category | flops | bytes accessed | tf_op | source)
XLA Modules:
  0.0 35.6 jit_solution(16277739489884530770)
XLA Ops:
  0.6 0.0 copy-start.3
  0.6 0.8 %copy-done.3 = bf16[40,2,256]{2,1,0:T(2,128)(2,1)S(1)} copy-done((bf16[40,2,256]{2,1,0:T(2,128)(2,1)S(1)}, bf16[40,2,256]{2,1,0:T(2,128)(2,1)}, u32[]{:S(2)}) %copy-start.3) | copy-done | bytes 40984
  1.4 0.0 copy-start.4
  1.4 0.8 %copy-done.4 = bf16[40,2,256]{2,1,0:T(2,128)(2,1)S(1)} copy-done((bf16[40,2,256]{2,1,0:T(2,128)(2,1)S(1)}, bf16[40,2,256]{2,1,0:T(2,128)(2,1)}, u32[]{:S(2)}) %copy-start.4) | copy-done | bytes 40984
  2.2 0.1 shard_map.77
  2.3 1.6 %collective-permute-start = (bf16[80,256]{1,0:T(8,128)(2,1)S(1)}, bf16[80,256]{1,0:T(8,128)(2,1)S(1)}, u32[]{:S(2)}, u32[]{:S(2)}) collective-permute-start(bf16[80,256]{1,0:T(8,128)(2,1)S(1)} %get-tuple-element.8), channel_id=1, source_target_pairs={{0,1},{2,3},{1,0},{3,2},{4,5},{6,7},{5,4},{7,6},{8,9},{10,11},{9,8... | collective-permute-start | bytes 122888 | tf_op jit(solution)/shard_map/ppermute | solution.py:322
  4.0 1.9 %collective-permute-start.1 = (bf16[80,256]{1,0:T(8,128)(2,1)S(1)}, bf16[80,256]{1,0:T(8,128)(2,1)S(1)}, u32[]{:S(2)}, u32[]{:S(2)}) collective-permute-start(bf16[80,256]{1,0:T(8,128)(2,1)S(1)} %get-tuple-element.9), channel_id=1, source_target_pairs={{1,2},{2,1},{5,6},{6,5},{9,10},{10,9},{13,14},{14,13},{17,18},{18,... | collective-permute-start | bytes 122888 | tf_op jit(solution)/shard_map/ppermute | solution.py:322
  5.9 0.5 %collective-permute-done.pair0_ref = bf16[80,256]{1,0:T(8,128)(2,1)S(1)} collective-permute-done((bf16[80,256]{1,0:T(8,128)(2,1)S(1)}, bf16[80,256]{1,0:T(8,128)(2,1)S(1)}, u32[]{:S(2)}, u32[]{:S(2)}) %collective-permute-start) | collective-permute-done | bytes 40992 | tf_op jit(solution)/shard_map/ppermute | solution.py:322
  6.4 3.5 %collective-permute-done.1.pair1_ref = bf16[80,256]{1,0:T(8,128)(2,1)S(1)} collective-permute-done((bf16[80,256]{1,0:T(8,128)(2,1)S(1)}, bf16[80,256]{1,0:T(8,128)(2,1)S(1)}, u32[]{:S(2)}, u32[]{:S(2)}) %collective-permute-start.1) | collective-permute-done | bytes 40992 | tf_op jit(solution)/shard_map/ppermute | solution.py:322
  9.8 0.0 copy-start.2
  9.8 1.0 %shard_map.78 = bf16[8,80,256]{2,1,0:T(8,128)(2,1)} custom-call(bf16[40,2,256]{2,1,0:T(2,128)(2,1)S(1)} %copy-done.3, bf16[40,2,256]{2,1,0:T(2,128)(2,1)S(1)} %copy-done.4, bf16[80,256]{1,0:T(8,128)(2,1)S(1)} %collective-permute-done.pair0_ref, bf16[80,256]{1,0:T(8,128)(2,1)S(1)} %collective-permute-done.1.pair1_ref), custom_call_target="tpu_custom_call" | custom-call | tf_op jit(solution)/shard_map/pallas_call | solution.py:302
  10.9 0.0 copy-start
  10.9 0.0 copy-start.1
  10.9 3.9 %all-to-all-start = ((bf16[8,80,256]{2,1,0:T(8,128)(2,1)}), bf16[8,80,256]{2,1,0:T(8,128)(2,1)S(1)}, u32[]{:S(2)}, u32[]{:S(2)}) async-start(bf16[8,80,256]{2,1,0:T(8,128)(2,1)} %shard_map.78), calls=%async_computation | async-start | bytes 655360 | tf_op jit(solution)/shard_map/all_to_all | solution.py:341
  14.7 0.0 copy-start.5
  14.7 0.0 copy-done.2
  14.7 0.0 copy-done
  14.8 0.0 copy-done.1
  14.8 0.6 %copy-done.5 = f32[32]{0:T(128)S(1)} copy-done((f32[32]{0:T(128)S(1)}, f32[32]{0:T(128)}, u32[]{:S(2)}) %copy-start.5) | copy-done | bytes 152
  15.4 0.5 %shard_map.79 = (bf16[192,240]{1,0:T(8,128)(2,1)S(1)}, bf16[192,192]{1,0:T(8,128)(2,1)S(1)}, bf16[192,192]{1,0:T(8,128)(2,1)S(1)}, f32[64,128]{1,0:T(8,128)S(1)}) custom-call(bf16[27,32,40]{2,1,0:T(8,128)(2,1)S(1)} %bitcast.12, bf16[27,32,32]{2,1,0:T(8,128)(2,1)S(1)} %bitcast.13, bf16[27,32,32]{2,1,0:T(8,128)(2,1)S(1)} %bitcast.14, f32[1,32]{1,0:T(1,128)S(1)} %bitcast.15), custom_call_target="tpu_custom_call" | custom-call | tf_op jit(solution)/shard_map/pallas_call | solution.py:302
  15.9 6.5 %all-to-all-done = bf16[8,80,256]{2,1,0:T(8,128)(2,1)S(1)} async-done(((bf16[8,80,256]{2,1,0:T(8,128)(2,1)}), bf16[8,80,256]{2,1,0:T(8,128)(2,1)S(1)}, u32[]{:S(2)}, u32[]{:S(2)}) %all-to-all-start) | async-done | bytes 327712 | tf_op jit(solution)/shard_map/all_to_all | solution.py:341
  22.3 4.9 %shard_map.80 = f32[8,24,128]{2,1,0:T(8,128)S(1)} custom-call(bf16[640,256]{1,0:T(8,128)(2,1)S(1)} %bitcast.11, bf16[192,240]{1,0:T(8,128)(2,1)S(1)} %get-tuple-element.10.w1_ref, bf16[192,192]{1,0:T(8,128)(2,1)S(1)} %get-tuple-element.11.w2_ref, bf16[192,192]{1,0:T(8,128)(2,1)S(1)} %get-tuple-element.12.w3_ref, f32[64,128]{1,0:T(8,128)S(1)} %get-tuple-element.13.head_ref), custom_call_target="tpu_custom_call" | custom-call | tf_op jit(solution)/shard_map/pallas_call | solution.py:302
  27.3 7.6 %all_to_all.10.y_ref = f32[8,24,128]{2,1,0:T(8,128)S(1)} all-to-all(f32[8,24,128]{2,1,0:T(8,128)S(1)} %shard_map.80), channel_id=1, replica_groups=mesh['disp'=8,'col'=4] {'disp'}, dimensions={0} | all-to-all | bytes 196608 | tf_op jit(solution)/shard_map/all_to_all | solution.py:361
  34.8 0.8 %shard_map.81 = (bf16[40,2,256]{2,1,0:T(2,128)(2,1)}, f32[2,256]{1,0:T(2,128)}) custom-call(f32[8,24,128]{2,1,0:T(8,128)S(1)} %all_to_all.10.y_ref), custom_call_target="tpu_custom_call" | custom-call | tf_op jit(solution)/shard_map/pallas_call | solution.py:302
Async XLA Ops:
  0.6 0.8 %copy-start.3 = (bf16[40,2,256]{2,1,0:T(2,128)(2,1)S(1)}, bf16[40,2,256]{2,1,0:T(2,128)(2,1)}, u32[]{:S(2)}) copy-start(bf16[40,2,256]{2,1,0:T(2,128)(2,1)} %left_ref.3) | copy-start | bytes 122884
  1.4 0.8 %copy-start.4 = (bf16[40,2,256]{2,1,0:T(2,128)(2,1)S(1)}, bf16[40,2,256]{2,1,0:T(2,128)(2,1)}, u32[]{:S(2)}) copy-start(bf16[40,2,256]{2,1,0:T(2,128)(2,1)} %right_ref.3) | copy-start | bytes 122884
  2.3 4.1 %collective-permute-start = (bf16[80,256]{1,0:T(8,128)(2,1)S(1)}, bf16[80,256]{1,0:T(8,128)(2,1)S(1)}, u32[]{:S(2)}, u32[]{:S(2)}) collective-permute-start(bf16[80,256]{1,0:T(8,128)(2,1)S(1)} %get-tuple-element.8), channel_id=1, source_target_pairs={{0,1},{2,3},{1,0},{3,2},{4,5},{6,7},{5,4},{7,6},{8,9},{10,11},{9,8... | collective-permute-start | bytes 122888 | tf_op jit(solution)/shard_map/ppermute | solution.py:322
  4.0 5.9 %collective-permute-start.1 = (bf16[80,256]{1,0:T(8,128)(2,1)S(1)}, bf16[80,256]{1,0:T(8,128)(2,1)S(1)}, u32[]{:S(2)}, u32[]{:S(2)}) collective-permute-start(bf16[80,256]{1,0:T(8,128)(2,1)S(1)} %get-tuple-element.9), channel_id=1, source_target_pairs={{1,2},{2,1},{5,6},{6,5},{9,10},{10,9},{13,14},{14,13},{17,18},{18,... | collective-permute-start | bytes 122888 | tf_op jit(solution)/shard_map/ppermute | solution.py:322
  9.8 4.9 %copy-start.2 = (bf16[32,32,3,3,3]{1,0,4,3,2:T(8,128)(2,1)S(1)}, bf16[32,32,3,3,3]{1,0,4,3,2:T(8,128)(2,1)}, u32[]{:S(2)}) copy-start(bf16[32,32,3,3,3]{1,0,4,3,2:T(8,128)(2,1)} %param.10) | copy-start | bytes 165892
  10.9 3.9 %copy-start = (bf16[32,40,3,3,3]{1,0,4,3,2:T(8,128)(2,1)S(1)}, bf16[32,40,3,3,3]{1,0,4,3,2:T(8,128)(2,1)}, u32[]{:S(2)}) copy-start(bf16[32,40,3,3,3]{1,0,4,3,2:T(8,128)(2,1)} %param.8) | copy-start | bytes 207364
  10.9 3.9 %copy-start.1 = (bf16[32,32,3,3,3]{1,0,4,3,2:T(8,128)(2,1)S(1)}, bf16[32,32,3,3,3]{1,0,4,3,2:T(8,128)(2,1)}, u32[]{:S(2)}) copy-start(bf16[32,32,3,3,3]{1,0,4,3,2:T(8,128)(2,1)} %param.9) | copy-start | bytes 165892
  10.9 11.5 %all-to-all-start = ((bf16[8,80,256]{2,1,0:T(8,128)(2,1)}), bf16[8,80,256]{2,1,0:T(8,128)(2,1)S(1)}, u32[]{:S(2)}, u32[]{:S(2)}) async-start(bf16[8,80,256]{2,1,0:T(8,128)(2,1)} %shard_map.78), calls=%async_computation | async-start | bytes 655360 | tf_op jit(solution)/shard_map/all_to_all | solution.py:341
  14.7 0.7 %copy-start.5 = (f32[32]{0:T(128)S(1)}, f32[32]{0:T(128)}, u32[]{:S(2)}) copy-start(f32[32]{0:T(128)} %param.11) | copy-start | bytes 388

commit v3 on v2

--- a/solution.py
+++ b/solution.py
@@ -43,6 +43,9 @@
             left_over -= self.strip
         per = KROWS // (CG * self.h)
         self.chunks = [min(per, self.g - k) for k in range(0, self.g, per)]
+        self.chips = self.n // 2
+        self.lo2 = round_up(self.mw + self.bw + self.d - 1, 8)
+        self.lw2 = round_up(self.lo2 + self.mw + self.bw, LANES)
         self.lg = LANES // self.bw
         self.rg = round_up(-(-(self.own_rows + self.h) // self.lg), 8)
 
@@ -67,8 +70,23 @@
     return ref[...].astype(jnp.float32).reshape(-1, ref.shape[-1])
 
 
-def edge_kernel(dm, left_ref, right_ref, *outs):
+def copied_in(sources, targets, sems):
+    copies = [
+        pltpu.make_async_copy(source, target, sems.at[k])
+        for k, (source, target) in enumerate(zip(sources, targets))
+    ]
+    for copy in copies:
+        copy.start()
+    return [copy.wait for copy in copies]
+
+
+def edge_kernel(dm, left_hbm, right_hbm, *refs):
+    *outs, flat_left_ref, flat_right_ref, left_ref, right_ref, sems = refs
+    for wait in copied_in((left_hbm, right_hbm), (left_ref, right_ref), sems):
+        wait()
     left, right = flat(left_ref), flat(right_ref)
+    flat_left_ref[...] = left.astype(flat_left_ref.dtype)
+    flat_right_ref[...] = right.astype(flat_right_ref.dtype)
     width = outs[0].shape[1]
     count = dm.hops[0]
     lane = lane_iota((dm.own_rows, width))
@@ -84,39 +102,66 @@
 
 
 def pack_kernel(dm, left_ref, right_ref, pair0_ref, pair1_ref, *refs):
-    out_ref = refs[-1]
+    more, outs, windows_ref = refs[: len(dm.hops) - 1], refs[len(dm.hops) - 1 : -1], refs[-1]
     left, right = flat(left_ref), flat(right_ref)
     pair0, pair1 = flat(pair0_ref), flat(pair1_ref)
     even = lax.axis_index("col") % 2 == 0
     up = jnp.where(even, pair1, pair0)
     down = jnp.where(even, pair0, pair1)[:, :LANES]
-    ext = max(round_up(dm.tail + dm.strip + 3, LANES), dm.lw, up.shape[1])
+    ext = max(round_up(dm.tail + dm.strip + 3, LANES), dm.lw2, up.shape[1])
     lane = lane_iota((dm.own_rows, ext))
     row = rolled(widen(right, ext), dm.tail)
     row = jnp.where(lane < dm.tail + dm.strip, row, rolled(widen(down, ext), dm.tail + dm.strip))
-    pieces = [up] + [flat(ref) for ref in refs[:-1]]
+    pieces = [up] + [flat(ref) for ref in more]
     for k, count in enumerate(dm.hops):
         start = dm.tail - sum(dm.hops[: k + 1])
         piece = rolled(widen(pieces[k], ext), start)
         row = jnp.where((lane >= start) & (lane < start + count), piece, row)
-    lext = max(round_up(dm.strip + 6, LANES), dm.lw, up.shape[1])
+    lext = max(round_up(dm.strip + 6, LANES), dm.lw2, up.shape[1])
     lane_l = lane_iota((dm.own_rows, lext))
     lrow = rolled(widen(left, lext), 3)
     lrow = jnp.where(lane_l < 3, rolled(widen(up, lext), -dm.hops[0]), lrow)
     lrow = jnp.where(lane_l >= dm.strip + 3, rolled(widen(down, lext), dm.strip), lrow)
-    lane_o = lane_iota((dm.own_rows, dm.lw))
-    for j in range(dm.n):
-        a = rolled(row, -dm.bw * j)[:, : dm.lw]
-        b = rolled(lrow, dm.lo - dm.bw * j)[:, : dm.lw]
-        out_ref[j] = jnp.where(lane_o < dm.lo, a, b).astype(out_ref.dtype)
-
-
-def prep_kernel(dm, w1_ref, w2_ref, w3_ref, head_ref, o1_ref, o2_ref, o3_ref, column_ref):
+    lane_o = lane_iota((dm.own_rows, dm.lw2))
+    for q in range(dm.chips):
+        a = rolled(row, -2 * dm.bw * q)[:, : dm.lw2]
+        b = rolled(lrow, dm.lo2 - 2 * dm.bw * q)[:, : dm.lw2]
+        windows_ref[q] = jnp.where(lane_o < dm.lo2, a, b).astype(windows_ref.dtype)
+    chip = lax.axis_index("disp") // 2
+    for m, out in enumerate(outs):
+        out[...] = windows_ref[chip ^ m]
+
+
+def split_kernel(dm, *refs):
+    *windows, keep_ref, give_ref = refs
+    first_core = lax.axis_index("disp") % 2 == 0
+    for m, ref in enumerate(windows):
+        x = flat(ref)
+        lane = lane_iota((dm.own_rows, dm.lw))
+        parts = []
+        for core in range(2):
+            a = rolled(x, -core * dm.bw)[:, : dm.lw]
+            b = rolled(x, dm.lo - dm.lo2 - core * dm.bw)[:, : dm.lw]
+            parts.append(jnp.where(lane < dm.lo, a, b))
+        keep_ref[m] = jnp.where(first_core, parts[0], parts[1]).astype(keep_ref.dtype)
+        give_ref[m] = jnp.where(first_core, parts[1], parts[0]).astype(give_ref.dtype)
+
+
+def prep_kernel(dm, *refs):
+    outs, targets, sems = refs[4:8], refs[8:12], refs[12]
+    waits = copied_in(refs[:4], targets, sems)
+    w1_ref, w2_ref, w3_ref, head_ref = targets
+    o1_ref, o2_ref, o3_ref, column_ref = outs
+    chip = lax.axis_index("disp") // 2
     for layer, (w_ref, o_ref) in enumerate(((w1_ref, o1_ref), (w2_ref, o2_ref), (w3_ref, o3_ref))):
         inputs = w_ref.shape[2]
         per_a = dm.h * inputs
+        waits[layer]()
         shape = (inputs, 3 * per_a)
         i = lax.broadcasted_iota(jnp.int32, shape, 0)
+        if layer == 0:
+            per_chip = inputs // dm.chips
+            i = ((i // per_chip) ^ chip) * per_chip + i % per_chip
         col = lane_iota(shape)
         total = None
         for a in range(3):
@@ -144,6 +189,7 @@
                 )
                 total = term if total is None else total + term
         o_ref[...] = total.astype(o_ref.dtype)
+    waits[3]()
     square = (dm.f, dm.f)
     eye = lane_iota(square) == lax.broadcasted_iota(jnp.int32, square, 0)
     column = jnp.sum(jnp.where(eye, head_ref[...], 0.0), axis=1, keepdims=True)
@@ -151,10 +197,17 @@
     column_ref[...] = jnp.concatenate([column] * dm.h, axis=0)
 
 
-def main_kernel(dm, x_ref, w1_ref, w2_ref, w3_ref, head_ref, out_ref, lt_ref, lhs_ref, pc_ref, a1_ref, a2_ref, a3_ref, ps_ref, s_ref):
+def main_kernel(dm, keep_ref, got_ref, w1_ref, w2_ref, w3_ref, head_ref, out_ref, x_ref, lt_ref, lhs_ref, pc_ref, a1_ref, a2_ref, a3_ref, ps_ref, s_ref):
     d, mw, h, f = dm.d, dm.mw, dm.h, dm.f
     base = lax.axis_index("col") * dm.strip + lax.axis_index("disp") * dm.bw
     total = dm.strips * dm.strip
+
+    chip, core = lax.axis_index("disp") // 2, lax.axis_index("disp") % 2
+    for m in range(dm.chips):
+        kept, got = flat(keep_ref.at[m]), flat(got_ref.at[m])
+        both = [jnp.where(core == 0, kept, got), jnp.where(core == 0, got, kept)]
+        rows = 2 * dm.own_rows
+        x_ref[m * rows : (m + 1) * rows] = jnp.concatenate(both, axis=0).astype(x_ref.dtype)
 
     lt_ref[...] = jnp.transpose(x_ref[:, dm.lb : dm.lw].astype(jnp.float32))
 
@@ -271,7 +324,7 @@
                 rolled(mine[g * dm.rg : (g + 1) * dm.rg], g * dm.bw),
                 packed,
             )
-        out_ref[j] = packed
+        out_ref[(j // 2 ^ chip) * 2 + j % 2] = packed
 
 
 def unpack_kernel(dm, y_ref, warped_ref, disparity_ref):
@@ -298,11 +351,15 @@
     dm = Dims(left_feat.shape, conv1_w.shape, conv2_w.shape, n, strips)
     bf, f32 = jnp.bfloat16, jnp.float32
 
-    def call(kernel, out_shape, operands, mib=8, **options):
+    def call(kernel, out_shape, operands, mib=8, in_hbm=False, **options):
+        spec = VMEM
+        if in_hbm:
+            spec = pl.BlockSpec(memory_space=pltpu.HBM)
+            operands = [pltpu.with_memory_space_constraint(v, pltpu.HBM) for v in operands]
         return pl.pallas_call(
             functools.partial(kernel, dm),
             out_shape=out_shape,
-            in_specs=[VMEM] * len(operands),
+            in_specs=[spec] * len(operands),
             out_specs=jax.tree.map(lambda _: VMEM, out_shape),
             compiler_params=pltpu.CompilerParams(vmem_limit_bytes=mib << 20),
             **options,
@@ -310,10 +367,16 @@
 
     wide = max(round_up(dm.hops[0] + 3, LANES), dm.strip)
     widths = [wide, wide] + [round_up(c, LANES) for c in dm.hops[1:]]
-    edges = call(
+    *edges, left, right = call(
         edge_kernel,
-        [jax.ShapeDtypeStruct((dm.own_rows, w), bf) for w in widths],
+        [jax.ShapeDtypeStruct((dm.own_rows, w), bf) for w in widths + [dm.strip] * 2],
         [left_feat, right_feat],
+        in_hbm=True,
+        scratch_shapes=[
+            pltpu.VMEM(left_feat.shape, bf),
+            pltpu.VMEM(left_feat.shape, bf),
+            pltpu.SemaphoreType.DMA((2,)),
+        ],
     )
     arrived = []
     for first in range(2):
@@ -324,6 +387,7 @@
         arrived.append(lax.ppermute(e, "col", [(s, s + k) for s in range(strips - k)]))
 
     kernels = [w.transpose(2, 3, 4, 0, 1).reshape(27, w.shape[0], w.shape[1]) for w in (conv1_w, conv2_w, conv3_w)]
+    arrived, kernels = lax.optimization_barrier((arrived, kernels))
     m3 = 3 * dm.h * dm.f
     depths = [3 * dm.h * w.shape[2] for w in kernels]
     w1, w2, w3, head = call(
@@ -331,23 +395,35 @@
         [jax.ShapeDtypeStruct((m3, k), bf) for k in depths]
         + [jax.ShapeDtypeStruct((dm.h * dm.f, dm.d), f32)],
         kernels + [head_w[None]],
-    )
-
-    send = call(
+        in_hbm=True,
+        scratch_shapes=[pltpu.VMEM(w.shape, bf) for w in kernels]
+        + [pltpu.VMEM((1, dm.f), f32), pltpu.SemaphoreType.DMA((4,))],
+    )
+
+    own_window, *windows = call(
         pack_kernel,
-        jax.ShapeDtypeStruct((n, dm.own_rows, dm.lw), bf),
-        [left_feat, right_feat] + arrived,
-    )
-    x = lax.all_to_all(send, "disp", 0, 0).reshape(dm.rows, dm.lw)
+        [jax.ShapeDtypeStruct((dm.own_rows, dm.lw2), bf)] * dm.chips,
+        [left, right] + arrived,
+        scratch_shapes=[pltpu.VMEM((dm.chips, dm.own_rows, dm.lw2), bf)],
+    )
+    windows = [own_window] + [
+        lax.ppermute(v, "disp", [(i, i ^ (2 * m)) for i in range(n)])
+        for m, v in enumerate(windows, 1)
+    ]
+    windows, (w1, w2, w3, head) = lax.optimization_barrier((windows, (w1, w2, w3, head)))
+    half = jax.ShapeDtypeStruct((dm.chips, dm.own_rows, dm.lw), bf)
+    keep, give = call(split_kernel, [half, half], windows)
+    got = lax.ppermute(give, "disp", [(i, i ^ 1) for i in range(n)])
 
     r_max = max(dm.chunks) * dm.h
     columns = [dm.mw, dm.mw - 2, dm.mw - 4]
     packed = call(
         main_kernel,
         jax.ShapeDtypeStruct((n, dm.rg, LANES), f32),
-        [x, w1, w2, w3, head],
+        [keep, got, w1, w2, w3, head],
         mib=32,
         scratch_shapes=[
+            pltpu.VMEM((dm.rows, dm.lw), bf),
             pltpu.VMEM((dm.lw - dm.lb, dm.rows), f32),
             pltpu.VMEM((dm.mw * r_max, KROWS), bf),
             pltpu.VMEM((len(dm.chunks), dm.mw * r_max, dm.lw), f32),

time: 36 us -> 32.6 us (0.906)
  waiting for transfers between devices: 10.4 us -> 7.88 us
  local copies, waits for them, and re-layouts: 2.18 us -> 0 us
  Pallas kernels: 7.31 us -> 9.03 us
    all_to_all x1 -> x0, waiting for transfers between devices: 6.47 us -> none  [shards(): x = lax.all_to_all(send, 'disp', 0, 0).reshape(dm.rows, dm.lw)]
    ppermute x0 -> x4, waiting for transfers between devices: none -> 3.91 us  [the longest x3 2.53 us: shards(): lax.ppermute(v, 'disp', [(i, i ^ 2 * m) for i in range(n)])]
    all_to_all x1 -> x0, starting transfers between devices: 3.85 us -> none  [shards(): x = lax.all_to_all(send, 'disp', 0, 0).reshape(dm.rows, dm.lw)]
    ppermute x0 -> x4, starting transfers between devices: none -> 3.62 us  [the longest x3 3.55 us: shards(): lax.ppermute(v, 'disp', [(i, i ^ 2 * m) for i in range(n)])]
    unnamed x12 -> x0, local copies, waits for them, and re-layouts: 2.18 us -> none
    pallas_call x5 -> x6, Pallas kernels: 7.31 us -> 9.03 us  [call(): pl.pallas_call(functools.partial(kernel, dm), out_shape=out_shape, in_spe...]
  transfers between devices with their start and end apart: 3 -> 6, of which waited for: 3 -> 5; matrix products, arithmetic and copies ran while one was open for 0% -> 0% of each run, Pallas kernels for 1% -> 6%
where the time goes in v3:
time: 32.6 us; the launch traced here: 32.4 us
  Pallas kernels  9.03 us (28%)
  waiting for transfers between devices  7.88 us (24%)
  blocking collectives  7.58 us (23%)
  starting transfers between devices  7.17 us (22%)
  between operations  0.69 us (2%)
    pallas_call x6, Pallas kernels, call(): pl.pallas_call(functools.partial(kernel, dm), out_shape=out_shape, in_spe...  9.03 us
    all_to_all x1, blocking collectives, shards(): y = lax.all_to_all(packed, 'disp', 0, 0)  7.58 us
    ppermute x2, waiting for transfers between devices, shards(): arrived.append(lax.ppermute(edges[first], 'col', pairs))  3.97 us
    ppermute x3, starting transfers between devices, shards(): lax.ppermute(v, 'disp', [(i, i ^ 2 * m) for i in range(n)])  3.55 us
    ppermute x2, starting transfers between devices, shards(): arrived.append(lax.ppermute(edges[first], 'col', pairs))  3.55 us
    ppermute x3, waiting for transfers between devices, shards(): lax.ppermute(v, 'disp', [(i, i ^ 2 * m) for i in range(n)])  2.53 us
    ppermute x1, waiting for transfers between devices, shards(): got = lax.ppermute(give, 'disp', [(i, i ^ 1) for i in range(n)])  1.38 us
  transfers between devices with their start and end apart: 6, of which 5 were waited for; matrix products, arithmetic and copies ran while one was open for 0% of the time, Pallas kernels for 6%

profile of v3, /device:TPU:16, one launch (start us, length us, event | category | flops | bytes accessed | tf_op | source)
XLA Modules:
  0.0 32.4 jit_solution(386563395336827391)
XLA Ops:
  0.6 0.9 %shard_map.77 = (bf16[80,256]{1,0:T(8,128)(2,1)S(1)}, bf16[80,256]{1,0:T(8,128)(2,1)S(1)}, bf16[80,256]{1,0:T(8,128)(2,1)S(1)}, bf16[80,256]{1,0:T(8,128)(2,1)S(1)}) custom-call(bf16[40,2,256]{2,1,0:T(2,128)(2,1)} %left_hbm.1, bf16[40,2,256]{2,1,0:T(2,128)(2,1)} %right_hbm.1), custom_call_target="tpu_custom_call" | custom-call | tf_op jit(solution)/shard_map/pallas_call | solution.py:359
  1.6 1.6 %collective-permute-start = (bf16[80,256]{1,0:T(8,128)(2,1)S(1)}, bf16[80,256]{1,0:T(8,128)(2,1)S(1)}, u32[]{:S(2)}, u32[]{:S(2)}) collective-permute-start(bf16[80,256]{1,0:T(8,128)(2,1)S(1)} %get-tuple-element.31), channel_id=1, source_target_pairs={{0,1},{2,3},{1,0},{3,2},{4,5},{6,7},{5,4},{7,6},{8,9},{10,11},{9,8... | collective-permute-start | bytes 122888 | tf_op jit(solution)/shard_map/ppermute | solution.py:385
  3.2 1.9 %collective-permute-start.1 = (bf16[80,256]{1,0:T(8,128)(2,1)S(1)}, bf16[80,256]{1,0:T(8,128)(2,1)S(1)}, u32[]{:S(2)}, u32[]{:S(2)}) collective-permute-start(bf16[80,256]{1,0:T(8,128)(2,1)S(1)} %get-tuple-element.32), channel_id=1, source_target_pairs={{1,2},{2,1},{5,6},{6,5},{9,10},{10,9},{13,14},{14,13},{17,18},{18,... | collective-permute-start | bytes 122888 | tf_op jit(solution)/shard_map/ppermute | solution.py:385
  5.1 0.5 %collective-permute-done.pair0_ref = bf16[80,256]{1,0:T(8,128)(2,1)S(1)} collective-permute-done((bf16[80,256]{1,0:T(8,128)(2,1)S(1)}, bf16[80,256]{1,0:T(8,128)(2,1)S(1)}, u32[]{:S(2)}, u32[]{:S(2)}) %collective-permute-start) | collective-permute-done | bytes 40992 | tf_op jit(solution)/shard_map/ppermute | solution.py:385
  5.6 3.5 %collective-permute-done.1.pair1_ref = bf16[80,256]{1,0:T(8,128)(2,1)S(1)} collective-permute-done((bf16[80,256]{1,0:T(8,128)(2,1)S(1)}, bf16[80,256]{1,0:T(8,128)(2,1)S(1)}, u32[]{:S(2)}, u32[]{:S(2)}) %collective-permute-start.1) | collective-permute-done | bytes 40992 | tf_op jit(solution)/shard_map/ppermute | solution.py:385
  9.1 0.2 shard_map.78
  9.4 1.6 %collective-permute-start.2 = (bf16[80,384]{1,0:T(8,128)(2,1)S(1)}, bf16[80,384]{1,0:T(8,128)(2,1)S(1)}, u32[]{:S(2)}, u32[]{:S(2)}) collective-permute-start(bf16[80,384]{1,0:T(8,128)(2,1)S(1)} %get-tuple-element.36), channel_id=1, source_target_pairs={{0,8},{4,12},{8,0},{12,4},{16,24},{20,28},{24,16},{28,20},{1,9},{5... | collective-permute-start | bytes 184328 | tf_op jit(solution)/shard_map/ppermute | solution.py:410
  10.9 1.5 %collective-permute-start.3 = (bf16[80,384]{1,0:T(8,128)(2,1)S(1)}, bf16[80,384]{1,0:T(8,128)(2,1)S(1)}, u32[]{:S(2)}, u32[]{:S(2)}) collective-permute-start(bf16[80,384]{1,0:T(8,128)(2,1)S(1)} %get-tuple-element.37), channel_id=1, source_target_pairs={{0,16},{4,20},{8,24},{12,28},{16,0},{20,4},{24,8},{28,12},{1,17},{... | collective-permute-start | bytes 184328 | tf_op jit(solution)/shard_map/ppermute | solution.py:410
  12.4 0.5 %collective-permute-start.4 = (bf16[80,384]{1,0:T(8,128)(2,1)S(1)}, bf16[80,384]{1,0:T(8,128)(2,1)S(1)}, u32[]{:S(2)}, u32[]{:S(2)}) collective-permute-start(bf16[80,384]{1,0:T(8,128)(2,1)S(1)} %get-tuple-element.38), channel_id=1, source_target_pairs={{0,24},{4,28},{8,16},{12,20},{16,8},{20,12},{24,0},{28,4},{1,25},{... | collective-permute-start | bytes 184328 | tf_op jit(solution)/shard_map/ppermute | solution.py:410
  12.9 2.1 %shard_map.79 = (bf16[192,240]{1,0:T(8,128)(2,1)S(1)}, bf16[192,192]{1,0:T(8,128)(2,1)S(1)}, bf16[192,192]{1,0:T(8,128)(2,1)S(1)}, f32[64,128]{1,0:T(8,128)S(1)}) custom-call(bf16[27,32,40]{2,1,0:T(8,128)(2,1)} %bitcast.10, bf16[27,32,32]{2,1,0:T(8,128)(2,1)} %bitcast.11, bf16[27,32,32]{2,1,0:T(8,128)(2,1)} %bitcast.12, f32[1,32]{1,0:T(1,128)} %bitcast.13), custom_call_target="tpu_custom_call" | custom-call | tf_op jit(solution)/shard_map/pallas_call | solution.py:359
  15.0 0.0 collective-permute-done.2.refs_1_
  15.0 0.3 %collective-permute-done.3.refs_2_ = bf16[80,384]{1,0:T(8,128)(2,1)S(1)} collective-permute-done((bf16[80,384]{1,0:T(8,128)(2,1)S(1)}, bf16[80,384]{1,0:T(8,128)(2,1)S(1)}, u32[]{:S(2)}, u32[]{:S(2)}) %collective-permute-start.3) | collective-permute-done | bytes 61472 | tf_op jit(solution)/shard_map/ppermute | solution.py:410
  15.4 2.2 %collective-permute-done.4.refs_3_ = bf16[80,384]{1,0:T(8,128)(2,1)S(1)} collective-permute-done((bf16[80,384]{1,0:T(8,128)(2,1)S(1)}, bf16[80,384]{1,0:T(8,128)(2,1)S(1)}, u32[]{:S(2)}, u32[]{:S(2)}) %collective-permute-start.4) | collective-permute-done | bytes 61472 | tf_op jit(solution)/shard_map/ppermute | solution.py:410
  17.6 0.2 shard_map.80
  17.8 0.1 collective-permute-start.5
  17.8 1.4 %collective-permute-done.5.got_ref = bf16[4,80,256]{2,1,0:T(8,128)(2,1)S(1)} collective-permute-done((bf16[4,80,256]{2,1,0:T(8,128)(2,1)S(1)}, bf16[4,80,256]{2,1,0:T(8,128)(2,1)S(1)}, u32[]{:S(2)}, u32[]{:S(2)}) %collective-permute-start.5) | collective-permute-done | bytes 163872 | tf_op jit(solution)/shard_map/ppermute | solution.py:416
  19.2 4.8 %shard_map.81 = f32[8,24,128]{2,1,0:T(8,128)S(1)} custom-call(bf16[4,80,256]{2,1,0:T(8,128)(2,1)S(1)} %get-tuple-element.50.keep_ref, bf16[4,80,256]{2,1,0:T(8,128)(2,1)S(1)} %collective-permute-done.5.got_ref, bf16[192,240]{1,0:T(8,128)(2,1)S(1)} %get-tuple-element.52.w1_ref, bf16[192,192]{1,0:T(8,128)(2,1)S(1)} %get-tuple-element.53.w2_ref, ...), custom_call_target="tpu_custom_call" | custom-call | tf_op jit(solution)/shard_map/pallas_call | solution.py:359
  24.0 7.6 %all_to_all.5.y_ref = f32[8,24,128]{2,1,0:T(8,128)S(1)} all-to-all(f32[8,24,128]{2,1,0:T(8,128)S(1)} %shard_map.81), channel_id=1, replica_groups=mesh['disp'=8,'col'=4] {'disp'}, dimensions={0} | all-to-all | bytes 196608 | tf_op jit(solution)/shard_map/all_to_all | solution.py:437
  31.6 0.8 %shard_map.82 = (bf16[40,2,256]{2,1,0:T(2,128)(2,1)}, f32[2,256]{1,0:T(2,128)}) custom-call(f32[8,24,128]{2,1,0:T(8,128)S(1)} %all_to_all.5.y_ref), custom_call_target="tpu_custom_call" | custom-call | tf_op jit(solution)/shard_map/pallas_call | solution.py:359
Async XLA Ops:
  1.6 4.1 %collective-permute-start = (bf16[80,256]{1,0:T(8,128)(2,1)S(1)}, bf16[80,256]{1,0:T(8,128)(2,1)S(1)}, u32[]{:S(2)}, u32[]{:S(2)}) collective-permute-start(bf16[80,256]{1,0:T(8,128)(2,1)S(1)} %get-tuple-element.31), channel_id=1, source_target_pairs={{0,1},{2,3},{1,0},{3,2},{4,5},{6,7},{5,4},{7,6},{8,9},{10,11},{9,8... | collective-permute-start | bytes 122888 | tf_op jit(solution)/shard_map/ppermute | solution.py:385
  3.2 5.9 %collective-permute-start.1 = (bf16[80,256]{1,0:T(8,128)(2,1)S(1)}, bf16[80,256]{1,0:T(8,128)(2,1)S(1)}, u32[]{:S(2)}, u32[]{:S(2)}) collective-permute-start(bf16[80,256]{1,0:T(8,128)(2,1)S(1)} %get-tuple-element.32), channel_id=1, source_target_pairs={{1,2},{2,1},{5,6},{6,5},{9,10},{10,9},{13,14},{14,13},{17,18},{18,... | collective-permute-start | bytes 122888 | tf_op jit(solution)/shard_map/ppermute | solution.py:385
  9.4 5.7 %collective-permute-start.2 = (bf16[80,384]{1,0:T(8,128)(2,1)S(1)}, bf16[80,384]{1,0:T(8,128)(2,1)S(1)}, u32[]{:S(2)}, u32[]{:S(2)}) collective-permute-start(bf16[80,384]{1,0:T(8,128)(2,1)S(1)} %get-tuple-element.36), channel_id=1, source_target_pairs={{0,8},{4,12},{8,0},{12,4},{16,24},{20,28},{24,16},{28,20},{1,9},{5... | collective-permute-start | bytes 184328 | tf_op jit(solution)/shard_map/ppermute | solution.py:410
  10.9 4.4 %collective-permute-start.3 = (bf16[80,384]{1,0:T(8,128)(2,1)S(1)}, bf16[80,384]{1,0:T(8,128)(2,1)S(1)}, u32[]{:S(2)}, u32[]{:S(2)}) collective-permute-start(bf16[80,384]{1,0:T(8,128)(2,1)S(1)} %get-tuple-element.37), channel_id=1, source_target_pairs={{0,16},{4,20},{8,24},{12,28},{16,0},{20,4},{24,8},{28,12},{1,17},{... | collective-permute-start | bytes 184328 | tf_op jit(solution)/shard_map/ppermute | solution.py:410
  12.4 5.1 %collective-permute-start.4 = (bf16[80,384]{1,0:T(8,128)(2,1)S(1)}, bf16[80,384]{1,0:T(8,128)(2,1)S(1)}, u32[]{:S(2)}, u32[]{:S(2)}) collective-permute-start(bf16[80,384]{1,0:T(8,128)(2,1)S(1)} %get-tuple-element.38), channel_id=1, source_target_pairs={{0,24},{4,28},{8,16},{12,20},{16,8},{20,12},{24,0},{28,4},{1,25},{... | collective-permute-start | bytes 184328 | tf_op jit(solution)/shard_map/ppermute | solution.py:410
  17.8 1.5 %collective-permute-start.5 = (bf16[4,80,256]{2,1,0:T(8,128)(2,1)S(1)}, bf16[4,80,256]{2,1,0:T(8,128)(2,1)S(1)}, u32[]{:S(2)}, u32[]{:S(2)}) collective-permute-start(bf16[4,80,256]{2,1,0:T(8,128)(2,1)S(1)} %get-tuple-element.51), channel_id=1, source_target_pairs={{0,4},{4,0},{8,12},{12,8},{16,20},{20,16},{24,28},{28,24},{1,5},{5... | collective-permute-start | bytes 491528 | tf_op jit(solution)/shard_map/ppermute | solution.py:416

commit v4 on v3

--- a/solution.py
+++ b/solution.py
@@ -11,6 +11,8 @@
 CG = 8
 LANES = 128
 KROWS = 256
+TILE = 4
+TERMS = 3
 VMEM = pl.BlockSpec(memory_space=pltpu.VMEM)
 
 masked_value = -1e30
@@ -47,7 +49,7 @@
         self.lo2 = round_up(self.mw + self.bw + self.d - 1, 8)
         self.lw2 = round_up(self.lo2 + self.mw + self.bw, LANES)
         self.lg = LANES // self.bw
-        self.rg = round_up(-(-(self.own_rows + self.h) // self.lg), 8)
+        self.rg = round_up(-(-(self.own_rows + TERMS * self.h) // self.lg), 8)
 
 
 def lane_iota(shape):
@@ -197,77 +199,88 @@
     column_ref[...] = jnp.concatenate([column] * dm.h, axis=0)
 
 
-def main_kernel(dm, keep_ref, got_ref, w1_ref, w2_ref, w3_ref, head_ref, out_ref, x_ref, lt_ref, lhs_ref, pc_ref, a1_ref, a2_ref, a3_ref, ps_ref, s_ref):
-    d, mw, h, f = dm.d, dm.mw, dm.h, dm.f
+def main_kernel(dm, keep_ref, got_ref, w1_ref, w2_ref, w3_ref, head_ref, out_ref, x_ref, lt_ref, lhs_ref, pc_ref, a1_ref, a2_ref, a3_ref, p1_ref, p2_ref, p3_ref, s_ref):
+    d, mw, h, f, bf = dm.d, dm.mw, dm.h, dm.f, jnp.bfloat16
+    chip, core = lax.axis_index("disp") // 2, lax.axis_index("disp") % 2
     base = lax.axis_index("col") * dm.strip + lax.axis_index("disp") * dm.bw
     total = dm.strips * dm.strip
 
-    chip, core = lax.axis_index("disp") // 2, lax.axis_index("disp") % 2
     for m in range(dm.chips):
         kept, got = flat(keep_ref.at[m]), flat(got_ref.at[m])
         both = [jnp.where(core == 0, kept, got), jnp.where(core == 0, got, kept)]
         rows = 2 * dm.own_rows
-        x_ref[m * rows : (m + 1) * rows] = jnp.concatenate(both, axis=0).astype(x_ref.dtype)
-
-    lt_ref[...] = jnp.transpose(x_ref[:, dm.lb : dm.lw].astype(jnp.float32))
-
-    first = 0
-    for k, count in enumerate(dm.chunks):
-        r = count * h
-        q = count * CG * h
+        both = jnp.concatenate(both, axis=0)
+        x_ref[m * rows : (m + 1) * rows] = both.astype(bf)
+        lt_ref[:, m * rows : (m + 1) * rows] = jnp.transpose(both[:, dm.lb :]) * (1.0 / CG)
+
+    keeps = []
+    for count in dm.chunks:
+        r, q = count * h, count * CG * h
         lane = lane_iota((r, q))
         sub = lax.broadcasted_iota(jnp.int32, (r, q), 0)
-        keep = (lane % h == sub // count) & (lane // (CG * h) == sub % count)
-        for m in range(mw):
-            at = dm.lo - dm.lb + m
-            line = jnp.broadcast_to(lt_ref[at : at + 1, first : first + q], (r, q))
-            lhs_ref[m * r : (m + 1) * r, :q] = jnp.where(keep, line, 0.0).astype(jnp.bfloat16)
-        pc_ref[k, : mw * r] = jnp.dot(
-            lhs_ref[: mw * r, :q], x_ref[first : first + q, :], preferred_element_type=jnp.float32
-        )
-        first += q
-
-    lane_d = {}
+        keeps.append((lane % h == sub // count) & (lane // (CG * h) == sub % count))
+
+    def correlate(m0, m1):
+        first = 0
+        for k, count in enumerate(dm.chunks):
+            r, q = count * h, count * CG * h
+            for m in range(m0, m1):
+                at = dm.lo - dm.lb + m
+                line = jnp.broadcast_to(lt_ref[at : at + 1, first : first + q], (r, q))
+                lhs_ref[k, m * r : (m + 1) * r, :q] = jnp.where(keeps[k], line, 0.0).astype(bf)
+            pc_ref[k, m0 * r : m1 * r] = jnp.dot(
+                lhs_ref[k, m0 * r : m1 * r, :q],
+                x_ref[first : first + q, :],
+                preferred_element_type=jnp.float32,
+            )
+            first += q
+
+    lanes = {}
 
     def spread(ref, m, v):
         rows = v.shape[0]
-        if rows not in lane_d:
-            lane_d[rows] = lane_iota((rows, d))
-        lane = lane_d[rows]
+        if rows not in lanes:
+            lanes[rows] = lane_iota((rows, d))
+        lane = lanes[rows]
         at = slice(m * d, (m + 1) * d)
-        ref[:rows, at] = jnp.where(lane < d - 1, rolled(v, -1), 0.0).astype(jnp.bfloat16)
-        ref[rows : 2 * rows, at] = v.astype(jnp.bfloat16)
-        ref[2 * rows :, at] = jnp.where(lane > 0, rolled(v, 1), 0.0).astype(jnp.bfloat16)
-
-    for m in range(mw):
-        parts = [pc_ref[k, m * c * h : (m + 1) * c * h] for k, c in enumerate(dm.chunks)]
-        block = jnp.concatenate(parts, axis=0)
-        spread(a1_ref, m, rolled(block, -m)[:, :d] * (1.0 / CG))
-
-    step = 4 * LANES
-
-    def layer(w_ref, a_ref, columns, emit):
-        width = columns * d
-        for t in range(0, width, step):
-            size = min(step, width - t)
-            ps_ref[:, t : t + size] = jnp.dot(
-                w_ref[...], a_ref[:, t : t + size], preferred_element_type=jnp.float32
-            )
+        zero = jnp.zeros_like(v)
+        ref[:rows, at] = jnp.where(lane < d - 1, rolled(v, -1), zero)
+        ref[rows : 2 * rows, at] = v
+        ref[2 * rows :, at] = jnp.where(lane > 0, rolled(v, 1), zero)
+
+    def volume(m0, m1):
+        for m in range(m0, m1):
+            parts = [pc_ref[k, m * c * h : (m + 1) * c * h].astype(bf) for k, c in enumerate(dm.chunks)]
+            spread(a1_ref, m, rolled(jnp.concatenate(parts, axis=0), -m)[:, :d])
+
+    def product(w_ref, a_ref, p_ref):
+        def run(m0, m1):
+            at = slice(m0 * d, m1 * d)
+            p_ref[:, at] = jnp.dot(w_ref[...], a_ref[:, at], preferred_element_type=jnp.float32)
+
+        return run
+
+    def taken(p_ref, emit):
         fh = f * h
-        for m in range(1, columns - 1):
-            z = ps_ref[:fh, (m - 1) * d : m * d]
-            z = z + ps_ref[fh : 2 * fh, m * d : (m + 1) * d]
-            z = z + ps_ref[2 * fh :, (m + 1) * d : (m + 2) * d]
-            emit(m - 1, jnp.maximum(z, 0.0))
-
-    def inside(column, z):
-        if 3 <= column < mw - 3:
-            return z
-        at = base - 3 + column
-        return jnp.where((at >= 0) & (at < total), z, 0.0)
-
-    layer(w1_ref, a1_ref, mw, lambda m, z: spread(a2_ref, m, inside(m + 1, z)))
-    layer(w2_ref, a2_ref, mw - 2, lambda m, z: spread(a3_ref, m, inside(m + 2, z)))
+
+        def run(m0, m1):
+            for m in range(m0, m1):
+                z = p_ref[:fh, m * d : (m + 1) * d]
+                z = z + p_ref[fh : 2 * fh, (m + 1) * d : (m + 2) * d]
+                z = z + p_ref[2 * fh :, (m + 2) * d : (m + 3) * d]
+                emit(m, jnp.maximum(z, 0.0))
+
+        return run
+
+    def activity(a_ref, margin):
+        def emit(m, z):
+            column = m + margin
+            if not 3 <= column < mw - 3:
+                at = base - 3 + column
+                z = jnp.where((at >= 0) & (at < total), z, 0.0)
+            spread(a_ref, m, z.astype(bf))
+
+        return emit
 
     head = head_ref[...]
 
@@ -276,7 +289,28 @@
         for row in range(h):
             s_ref[row, m : m + 1, :] = jnp.sum(z[row * f : (row + 1) * f], axis=0, keepdims=True)
 
-    layer(w3_ref, a3_ref, mw - 4, score)
+    stages = [
+        (correlate, mw, 0),
+        (volume, mw, 0),
+        (product(w1_ref, a1_ref, p1_ref), mw, 0),
+        (taken(p1_ref, activity(a2_ref, 1)), mw - 2, 2),
+        (product(w2_ref, a2_ref, p2_ref), mw - 2, 0),
+        (taken(p2_ref, activity(a3_ref, 2)), mw - 4, 2),
+        (product(w3_ref, a3_ref, p3_ref), mw - 4, 0),
+        (taken(p3_ref, score), mw - 6, 2),
+    ]
+    done = [0] * len(stages)
+    while done[-1] < stages[-1][1]:
+        before = list(done)
+        for k in reversed(range(len(stages))):
+            run, count, beyond = stages[k]
+            ready = count if k == 0 else min(count, before[k - 1] - beyond)
+            last = ready == count
+            size = ready - done[k] if last else (ready - done[k]) // TILE * TILE
+            size = min(size, TILE)
+            if size > 0:
+                run(done[k], done[k] + size)
+                done[k] += size
 
     disp = (d - 1) - lane_iota((dm.bw, d))
     column = base + lax.broadcasted_iota(jnp.int32, (dm.bw, d), 0)
@@ -291,40 +325,38 @@
         disp_sum = jnp.sum(weighting * disp_f, axis=1, keepdims=True)
         disparity.append(disp_sum / denominator / d)
         band = widen(weighting / denominator, dm.lw)
-        bands.append(pltpu.roll(band, 3, 1, stride=1, stride_axis=0))
+        band = pltpu.roll(band, 3, 1, stride=1, stride_axis=0)
+        bands += [band] * dm.lg
     band = jnp.concatenate(bands, axis=0)
-    high = band.astype(jnp.bfloat16)
-    low = (band - high.astype(jnp.float32)).astype(jnp.bfloat16)
-    sums = lax.dot_general(
-        x_ref[...],
-        jnp.concatenate([high, low], axis=0),
-        (((1,), (1,)), ((), ())),
-        preferred_element_type=jnp.float32,
-    )
-    hb = h * dm.bw
-    sums = widen(sums, round_up(2 * hb, LANES))
-    sums = sums + rolled(sums, -hb)
-    row = lax.broadcasted_iota(jnp.int32, sums.shape, 0) % h
-    warped = sums
+    high = band.astype(bf)
+    low = (band - high.astype(jnp.float32)).astype(bf)
+    sums = None
+    for part in (high, low):
+        term = lax.dot_general(
+            x_ref[...], part, (((1,), (1,)), ((), ())), preferred_element_type=jnp.float32
+        )
+        sums = term if sums is None else sums + term
+    row = lax.broadcasted_iota(jnp.int32, (dm.rows, LANES), 0) % h
+    warped = sums[:, :LANES]
     for k in range(1, h):
-        warped = jnp.where(row == k, rolled(sums, -k * dm.bw), warped)
-    warped = warped[:, :LANES]
-
-    eye = lane_iota((dm.bw, LANES)) == lax.broadcasted_iota(jnp.int32, (dm.bw, LANES), 0)
-    lines = [jnp.sum(jnp.where(eye, v, 0.0), axis=0, keepdims=True) for v in disparity]
-    lines.append(jnp.zeros((dm.lg * dm.rg - dm.own_rows - h, LANES), jnp.float32))
+        warped = jnp.where(row == k, sums[:, k * LANES : (k + 1) * LANES], warped)
+
+    eye = lane_iota((dm.bw, LANES)) % dm.bw == lax.broadcasted_iota(jnp.int32, (dm.bw, LANES), 0)
+    rest = [jnp.sum(jnp.where(eye, v, 0.0), axis=0, keepdims=True) for v in disparity]
+    lines = []
+    for _ in range(TERMS):
+        terms = [v.astype(bf).astype(jnp.float32) for v in rest]
+        rest = [v - t for v, t in zip(rest, terms)]
+        lines += terms
+    lines.append(jnp.zeros((dm.lg * dm.rg - dm.own_rows - len(lines), LANES), jnp.float32))
     lines = jnp.concatenate(lines, axis=0)
-    lane = lane_iota((dm.rg, LANES))
+    group = lane_iota((dm.rg, LANES)) // dm.bw
     for j in range(dm.n):
         mine = jnp.concatenate([warped[j * dm.own_rows : (j + 1) * dm.own_rows], lines], axis=0)
         packed = mine[: dm.rg]
         for g in range(1, dm.lg):
-            packed = jnp.where(
-                (lane >= g * dm.bw) & (lane < (g + 1) * dm.bw),
-                rolled(mine[g * dm.rg : (g + 1) * dm.rg], g * dm.bw),
-                packed,
-            )
-        out_ref[(j // 2 ^ chip) * 2 + j % 2] = packed
+            packed = jnp.where(group == g, mine[g * dm.rg : (g + 1) * dm.rg], packed)
+        out_ref[(j // 2 ^ chip) * 2 + j % 2] = packed.astype(out_ref.dtype)
 
 
 def unpack_kernel(dm, y_ref, warped_ref, disparity_ref):
@@ -336,14 +368,19 @@
         for g in range(dm.lg):
             total = None
             for p in range(per):
-                piece = rolled(y_ref[t * per + p], (p - g) * dm.bw)
+                piece = rolled(flat(y_ref.at[t * per + p]), (p - g) * dm.bw)
                 keep = (lane >= p * dm.bw) & (lane < (p + 1) * dm.bw)
                 total = piece if total is None else jnp.where(keep, piece, total)
             groups.append(total)
         tiles.append(jnp.concatenate(groups, axis=0))
     full = jnp.concatenate(tiles, axis=1)
     warped_ref[...] = full[: dm.own_rows].reshape(warped_ref.shape).astype(warped_ref.dtype)
-    disparity_ref[...] = full[dm.own_rows : dm.own_rows + dm.h]
+    total = None
+    for k in reversed(range(TERMS)):
+        at = dm.own_rows + k * dm.h
+        term = full[at : at + dm.h]
+        total = term if total is None else term + total
+    disparity_ref[...] = total
 
 
 def shards(left_feat, right_feat, conv1_w, conv2_w, conv3_w, head_w):
@@ -419,18 +456,16 @@
     columns = [dm.mw, dm.mw - 2, dm.mw - 4]
     packed = call(
         main_kernel,
-        jax.ShapeDtypeStruct((n, dm.rg, LANES), f32),
+        jax.ShapeDtypeStruct((n, dm.rg, LANES), bf),
         [keep, got, w1, w2, w3, head],
         mib=32,
         scratch_shapes=[
             pltpu.VMEM((dm.rows, dm.lw), bf),
             pltpu.VMEM((dm.lw - dm.lb, dm.rows), f32),
-            pltpu.VMEM((dm.mw * r_max, KROWS), bf),
+            pltpu.VMEM((len(dm.chunks), dm.mw * r_max, KROWS), bf),
             pltpu.VMEM((len(dm.chunks), dm.mw * r_max, dm.lw), f32),
-            pltpu.VMEM((depths[0], columns[0] * dm.d), bf),
-            pltpu.VMEM((depths[1], columns[1] * dm.d), bf),
-            pltpu.VMEM((depths[2], columns[2] * dm.d), bf),
-            pltpu.VMEM((m3, columns[0] * dm.d), f32),
+            *[pltpu.VMEM((k, c * dm.d), bf) for k, c in zip(depths, columns)],
+            *[pltpu.VMEM((m3, c * dm.d), f32) for c in columns],
             pltpu.VMEM((dm.h, dm.bw, dm.d), f32),
         ],
     )

time: 32.6 us -> 31.7 us (0.972)
  Pallas kernels: 9.03 us -> 8.45 us
    pallas_call x6, Pallas kernels: 9.03 us -> 8.45 us  [call(): pl.pallas_call(functools.partial(kernel, dm), out_shape=out_shape, in_spe...]
  transfers between devices with their start and end apart: 6 -> 6, of which waited for: 5 -> 5; matrix products, arithmetic and copies ran while one was open for 0% -> 0% of each run, Pallas kernels for 6% -> 7%
where the time goes in v4:
time: 31.7 us; the launch traced here: 31.5 us
  Pallas kernels  8.45 us (27%)
  waiting for transfers between devices  7.88 us (25%)
  blocking collectives  7.31 us (23%)
  starting transfers between devices  7.17 us (23%)
  between operations  0.7 us (2%)
    pallas_call x6, Pallas kernels, call(): pl.pallas_call(functools.partial(kernel, dm), out_shape=out_shape, in_spe...  8.45 us
    all_to_all x1, blocking collectives, shards(): y = lax.all_to_all(packed, 'disp', 0, 0)  7.31 us
    ppermute x2, waiting for transfers between devices, shards(): arrived.append(lax.ppermute(edges[first], 'col', pairs))  3.97 us
    ppermute x3, starting transfers between devices, shards(): lax.ppermute(v, 'disp', [(i, i ^ 2 * m) for i in range(n)])  3.55 us
    ppermute x2, starting transfers between devices, shards(): arrived.append(lax.ppermute(edges[first], 'col', pairs))  3.55 us
    ppermute x3, waiting for transfers between devices, shards(): lax.ppermute(v, 'disp', [(i, i ^ 2 * m) for i in range(n)])  2.53 us
    ppermute x1, waiting for transfers between devices, shards(): got = lax.ppermute(give, 'disp', [(i, i ^ 1) for i in range(n)])  1.38 us
  transfers between devices with their start and end apart: 6, of which 5 were waited for; matrix products, arithmetic and copies ran while one was open for 0% of the time, Pallas kernels for 7%

profile of v4, /device:TPU:16, one launch (start us, length us, event | category | flops | bytes accessed | tf_op | source)
XLA Modules:
  0.0 31.5 jit_solution(16587675616678497164)
XLA Ops:
  0.6 0.9 %shard_map.77 = (bf16[80,256]{1,0:T(8,128)(2,1)S(1)}, bf16[80,256]{1,0:T(8,128)(2,1)S(1)}, bf16[80,256]{1,0:T(8,128)(2,1)S(1)}, bf16[80,256]{1,0:T(8,128)(2,1)S(1)}) custom-call(bf16[40,2,256]{2,1,0:T(2,128)(2,1)} %left_hbm.1, bf16[40,2,256]{2,1,0:T(2,128)(2,1)} %right_hbm.1), custom_call_target="tpu_custom_call" | custom-call | tf_op jit(solution)/shard_map/pallas_call | solution.py:396
  1.6 1.6 %collective-permute-start = (bf16[80,256]{1,0:T(8,128)(2,1)S(1)}, bf16[80,256]{1,0:T(8,128)(2,1)S(1)}, u32[]{:S(2)}, u32[]{:S(2)}) collective-permute-start(bf16[80,256]{1,0:T(8,128)(2,1)S(1)} %get-tuple-element.31), channel_id=1, source_target_pairs={{0,1},{2,3},{1,0},{3,2},{4,5},{6,7},{5,4},{7,6},{8,9},{10,11},{9,8... | collective-permute-start | bytes 122888 | tf_op jit(solution)/shard_map/ppermute | solution.py:422
  3.2 1.9 %collective-permute-start.1 = (bf16[80,256]{1,0:T(8,128)(2,1)S(1)}, bf16[80,256]{1,0:T(8,128)(2,1)S(1)}, u32[]{:S(2)}, u32[]{:S(2)}) collective-permute-start(bf16[80,256]{1,0:T(8,128)(2,1)S(1)} %get-tuple-element.32), channel_id=1, source_target_pairs={{1,2},{2,1},{5,6},{6,5},{9,10},{10,9},{13,14},{14,13},{17,18},{18,... | collective-permute-start | bytes 122888 | tf_op jit(solution)/shard_map/ppermute | solution.py:422
  5.1 0.5 %collective-permute-done.pair0_ref = bf16[80,256]{1,0:T(8,128)(2,1)S(1)} collective-permute-done((bf16[80,256]{1,0:T(8,128)(2,1)S(1)}, bf16[80,256]{1,0:T(8,128)(2,1)S(1)}, u32[]{:S(2)}, u32[]{:S(2)}) %collective-permute-start) | collective-permute-done | bytes 40992 | tf_op jit(solution)/shard_map/ppermute | solution.py:422
  5.6 3.5 %collective-permute-done.1.pair1_ref = bf16[80,256]{1,0:T(8,128)(2,1)S(1)} collective-permute-done((bf16[80,256]{1,0:T(8,128)(2,1)S(1)}, bf16[80,256]{1,0:T(8,128)(2,1)S(1)}, u32[]{:S(2)}, u32[]{:S(2)}) %collective-permute-start.1) | collective-permute-done | bytes 40992 | tf_op jit(solution)/shard_map/ppermute | solution.py:422
  9.1 0.2 shard_map.78
  9.4 1.6 %collective-permute-start.2 = (bf16[80,384]{1,0:T(8,128)(2,1)S(1)}, bf16[80,384]{1,0:T(8,128)(2,1)S(1)}, u32[]{:S(2)}, u32[]{:S(2)}) collective-permute-start(bf16[80,384]{1,0:T(8,128)(2,1)S(1)} %get-tuple-element.36), channel_id=1, source_target_pairs={{0,8},{4,12},{8,0},{12,4},{16,24},{20,28},{24,16},{28,20},{1,9},{5... | collective-permute-start | bytes 184328 | tf_op jit(solution)/shard_map/ppermute | solution.py:447
  10.9 1.5 %collective-permute-start.3 = (bf16[80,384]{1,0:T(8,128)(2,1)S(1)}, bf16[80,384]{1,0:T(8,128)(2,1)S(1)}, u32[]{:S(2)}, u32[]{:S(2)}) collective-permute-start(bf16[80,384]{1,0:T(8,128)(2,1)S(1)} %get-tuple-element.37), channel_id=1, source_target_pairs={{0,16},{4,20},{8,24},{12,28},{16,0},{20,4},{24,8},{28,12},{1,17},{... | collective-permute-start | bytes 184328 | tf_op jit(solution)/shard_map/ppermute | solution.py:447
  12.4 0.5 %collective-permute-start.4 = (bf16[80,384]{1,0:T(8,128)(2,1)S(1)}, bf16[80,384]{1,0:T(8,128)(2,1)S(1)}, u32[]{:S(2)}, u32[]{:S(2)}) collective-permute-start(bf16[80,384]{1,0:T(8,128)(2,1)S(1)} %get-tuple-element.38), channel_id=1, source_target_pairs={{0,24},{4,28},{8,16},{12,20},{16,8},{20,12},{24,0},{28,4},{1,25},{... | collective-permute-start | bytes 184328 | tf_op jit(solution)/shard_map/ppermute | solution.py:447
  12.9 2.1 %shard_map.79 = (bf16[192,240]{1,0:T(8,128)(2,1)S(1)}, bf16[192,192]{1,0:T(8,128)(2,1)S(1)}, bf16[192,192]{1,0:T(8,128)(2,1)S(1)}, f32[64,128]{1,0:T(8,128)S(1)}) custom-call(bf16[27,32,40]{2,1,0:T(8,128)(2,1)} %bitcast.10, bf16[27,32,32]{2,1,0:T(8,128)(2,1)} %bitcast.11, bf16[27,32,32]{2,1,0:T(8,128)(2,1)} %bitcast.12, f32[1,32]{1,0:T(1,128)} %bitcast.13), custom_call_target="tpu_custom_call" | custom-call | tf_op jit(solution)/shard_map/pallas_call | solution.py:396
  15.0 0.0 collective-permute-done.2.refs_1_
  15.0 0.3 %collective-permute-done.3.refs_2_ = bf16[80,384]{1,0:T(8,128)(2,1)S(1)} collective-permute-done((bf16[80,384]{1,0:T(8,128)(2,1)S(1)}, bf16[80,384]{1,0:T(8,128)(2,1)S(1)}, u32[]{:S(2)}, u32[]{:S(2)}) %collective-permute-start.3) | collective-permute-done | bytes 61472 | tf_op jit(solution)/shard_map/ppermute | solution.py:447
  15.4 2.2 %collective-permute-done.4.refs_3_ = bf16[80,384]{1,0:T(8,128)(2,1)S(1)} collective-permute-done((bf16[80,384]{1,0:T(8,128)(2,1)S(1)}, bf16[80,384]{1,0:T(8,128)(2,1)S(1)}, u32[]{:S(2)}, u32[]{:S(2)}) %collective-permute-start.4) | collective-permute-done | bytes 61472 | tf_op jit(solution)/shard_map/ppermute | solution.py:447
  17.6 0.2 shard_map.80
  17.8 0.1 collective-permute-start.5
  17.8 1.4 %collective-permute-done.5.got_ref = bf16[4,80,256]{2,1,0:T(8,128)(2,1)S(1)} collective-permute-done((bf16[4,80,256]{2,1,0:T(8,128)(2,1)S(1)}, bf16[4,80,256]{2,1,0:T(8,128)(2,1)S(1)}, u32[]{:S(2)}, u32[]{:S(2)}) %collective-permute-start.5) | collective-permute-done | bytes 163872 | tf_op jit(solution)/shard_map/ppermute | solution.py:453
  19.2 4.2 %shard_map.81 = bf16[8,24,128]{2,1,0:T(8,128)(2,1)S(1)} custom-call(bf16[4,80,256]{2,1,0:T(8,128)(2,1)S(1)} %get-tuple-element.50.keep_ref, bf16[4,80,256]{2,1,0:T(8,128)(2,1)S(1)} %collective-permute-done.5.got_ref, bf16[192,240]{1,0:T(8,128)(2,1)S(1)} %get-tuple-element.52.w1_ref, bf16[192,192]{1,0:T(8,128)(2,1)S(1)} %get-tuple-element.53.w2_ref, ...), custom_call_target="tpu_custom_call" | custom-call | tf_op jit(solution)/shard_map/pallas_call | solution.py:396
  23.4 7.3 %all_to_all.5.y_ref = bf16[8,24,128]{2,1,0:T(8,128)(2,1)S(1)} all-to-all(bf16[8,24,128]{2,1,0:T(8,128)(2,1)S(1)} %shard_map.81), channel_id=1, replica_groups=mesh['disp'=8,'col'=4] {'disp'}, dimensions={0} | all-to-all | bytes 98304 | tf_op jit(solution)/shard_map/all_to_all | solution.py:472
  30.8 0.8 %shard_map.82 = (bf16[40,2,256]{2,1,0:T(2,128)(2,1)}, f32[2,256]{1,0:T(2,128)}) custom-call(bf16[8,24,128]{2,1,0:T(8,128)(2,1)S(1)} %all_to_all.5.y_ref), custom_call_target="tpu_custom_call" | custom-call | tf_op jit(solution)/shard_map/pallas_call | solution.py:396
Async XLA Ops:
  1.6 4.1 %collective-permute-start = (bf16[80,256]{1,0:T(8,128)(2,1)S(1)}, bf16[80,256]{1,0:T(8,128)(2,1)S(1)}, u32[]{:S(2)}, u32[]{:S(2)}) collective-permute-start(bf16[80,256]{1,0:T(8,128)(2,1)S(1)} %get-tuple-element.31), channel_id=1, source_target_pairs={{0,1},{2,3},{1,0},{3,2},{4,5},{6,7},{5,4},{7,6},{8,9},{10,11},{9,8... | collective-permute-start | bytes 122888 | tf_op jit(solution)/shard_map/ppermute | solution.py:422
  3.2 5.9 %collective-permute-start.1 = (bf16[80,256]{1,0:T(8,128)(2,1)S(1)}, bf16[80,256]{1,0:T(8,128)(2,1)S(1)}, u32[]{:S(2)}, u32[]{:S(2)}) collective-permute-start(bf16[80,256]{1,0:T(8,128)(2,1)S(1)} %get-tuple-element.32), channel_id=1, source_target_pairs={{1,2},{2,1},{5,6},{6,5},{9,10},{10,9},{13,14},{14,13},{17,18},{18,... | collective-permute-start | bytes 122888 | tf_op jit(solution)/shard_map/ppermute | solution.py:422
  9.4 5.7 %collective-permute-start.2 = (bf16[80,384]{1,0:T(8,128)(2,1)S(1)}, bf16[80,384]{1,0:T(8,128)(2,1)S(1)}, u32[]{:S(2)}, u32[]{:S(2)}) collective-permute-start(bf16[80,384]{1,0:T(8,128)(2,1)S(1)} %get-tuple-element.36), channel_id=1, source_target_pairs={{0,8},{4,12},{8,0},{12,4},{16,24},{20,28},{24,16},{28,20},{1,9},{5... | collective-permute-start | bytes 184328 | tf_op jit(solution)/shard_map/ppermute | solution.py:447
  10.9 4.4 %collective-permute-start.3 = (bf16[80,384]{1,0:T(8,128)(2,1)S(1)}, bf16[80,384]{1,0:T(8,128)(2,1)S(1)}, u32[]{:S(2)}, u32[]{:S(2)}) collective-permute-start(bf16[80,384]{1,0:T(8,128)(2,1)S(1)} %get-tuple-element.37), channel_id=1, source_target_pairs={{0,16},{4,20},{8,24},{12,28},{16,0},{20,4},{24,8},{28,12},{1,17},{... | collective-permute-start | bytes 184328 | tf_op jit(solution)/shard_map/ppermute | solution.py:447
  12.4 5.1 %collective-permute-start.4 = (bf16[80,384]{1,0:T(8,128)(2,1)S(1)}, bf16[80,384]{1,0:T(8,128)(2,1)S(1)}, u32[]{:S(2)}, u32[]{:S(2)}) collective-permute-start(bf16[80,384]{1,0:T(8,128)(2,1)S(1)} %get-tuple-element.38), channel_id=1, source_target_pairs={{0,24},{4,28},{8,16},{12,20},{16,8},{20,12},{24,0},{28,4},{1,25},{... | collective-permute-start | bytes 184328 | tf_op jit(solution)/shard_map/ppermute | solution.py:447
  17.8 1.5 %collective-permute-start.5 = (bf16[4,80,256]{2,1,0:T(8,128)(2,1)S(1)}, bf16[4,80,256]{2,1,0:T(8,128)(2,1)S(1)}, u32[]{:S(2)}, u32[]{:S(2)}) collective-permute-start(bf16[4,80,256]{2,1,0:T(8,128)(2,1)S(1)} %get-tuple-element.51), channel_id=1, source_target_pairs={{0,4},{4,0},{8,12},{12,8},{16,20},{20,16},{24,28},{28,24},{1,5},{5... | collective-permute-start | bytes 491528 | tf_op jit(solution)/shard_map/ppermute | solution.py:453

commit v5 on v4

--- a/solution.py
+++ b/solution.py
@@ -11,7 +11,7 @@
 CG = 8
 LANES = 128
 KROWS = 256
-TILE = 4
+TILE = 8
 TERMS = 3
 VMEM = pl.BlockSpec(memory_space=pltpu.VMEM)
 
@@ -43,11 +43,21 @@
         while left_over > 0:
             self.hops.append(min(left_over, self.strip))
             left_over -= self.strip
-        per = KROWS // (CG * self.h)
-        self.chunks = [min(per, self.g - k) for k in range(0, self.g, per)]
         self.chips = self.n // 2
         self.lo2 = round_up(self.mw + self.bw + self.d - 1, 8)
         self.lw2 = round_up(self.lo2 + self.mw + self.bw, LANES)
+        per = KROWS // (CG * self.h)
+        self.kept = self.g // 2
+        self.full = self.kept // per * per
+        rest = 2 * (self.kept - self.full)
+        self.split = own % CG == 0 and self.full > 0 and rest <= per and rest * self.h % 16 == 0
+        if self.split:
+            self.chunks = [per] * (2 * self.full // per) + ([rest] if rest else [])
+            self.early = self.full // per
+        else:
+            self.chunks = [min(per, self.g - k) for k in range(0, self.g, per)]
+            self.early = 0
+        self.early_rows = sum(self.chunks[: self.early]) * self.h
         self.lg = LANES // self.bw
         self.rg = round_up(-(-(self.own_rows + TERMS * self.h) // self.lg), 8)
 
@@ -154,14 +164,21 @@
     waits = copied_in(refs[:4], targets, sems)
     w1_ref, w2_ref, w3_ref, head_ref = targets
     o1_ref, o2_ref, o3_ref, column_ref = outs
-    chip = lax.axis_index("disp") // 2
+    chip, core = lax.axis_index("disp") // 2, lax.axis_index("disp") % 2
     for layer, (w_ref, o_ref) in enumerate(((w1_ref, o1_ref), (w2_ref, o2_ref), (w3_ref, o3_ref))):
         inputs = w_ref.shape[2]
         per_a = dm.h * inputs
         waits[layer]()
         shape = (inputs, 3 * per_a)
         i = lax.broadcasted_iota(jnp.int32, shape, 0)
-        if layer == 0:
+        if layer == 0 and dm.split:
+            per_device = inputs // dm.n
+            device = i // per_device
+            side = (device % 2) ^ core
+            i = ((device // 2) ^ chip) * per_device + i % per_device
+            rest = 2 * dm.full + side * (dm.kept - dm.full) + i - dm.full
+            i = jnp.where(i < dm.full, side * dm.full + i, rest)
+        elif layer == 0:
             per_chip = inputs // dm.chips
             i = ((i // per_chip) ^ chip) * per_chip + i % per_chip
         col = lane_iota(shape)
@@ -199,59 +216,133 @@
     column_ref[...] = jnp.concatenate([column] * dm.h, axis=0)
 
 
-def main_kernel(dm, keep_ref, got_ref, w1_ref, w2_ref, w3_ref, head_ref, out_ref, x_ref, lt_ref, lhs_ref, pc_ref, a1_ref, a2_ref, a3_ref, p1_ref, p2_ref, p3_ref, s_ref):
+def correlator(dm, chunks, x_of, lt_ref, lhs_ref, pc_ref):
+    keeps = []
+    for count in chunks:
+        r, q = count * dm.h, count * CG * dm.h
+        lane = lane_iota((r, q))
+        sub = lax.broadcasted_iota(jnp.int32, (r, q), 0)
+        keeps.append((lane % dm.h == sub // count) & (lane // (CG * dm.h) == sub % count))
+
+    def run(m0, m1):
+        first = 0
+        for k, count in enumerate(chunks):
+            r, q = count * dm.h, count * CG * dm.h
+            for m in range(m0, m1):
+                at = dm.lo - dm.lb + m
+                line = jnp.broadcast_to(lt_ref[at : at + 1, first : first + q], (r, q))
+                line = jnp.where(keeps[k], line, 0.0).astype(jnp.bfloat16)
+                lhs_ref[k, m * r : (m + 1) * r, :q] = line
+            pc_ref[k, m0 * r : m1 * r] = jnp.dot(
+                lhs_ref[k, m0 * r : m1 * r, :q], x_of(k), preferred_element_type=jnp.float32
+            )
+            first += q
+
+    return run
+
+
+def shifts(v, lanes):
+    if v.shape not in lanes:
+        lanes[v.shape] = lane_iota(v.shape)
+    lane, zero = lanes[v.shape], jnp.zeros_like(v)
+    last = v.shape[1] - 1
+    return (
+        jnp.where(lane < last, rolled(v, -1), zero),
+        v,
+        jnp.where(lane > 0, rolled(v, 1), zero),
+    )
+
+
+def column_of(dm, chunks, pc_ref, m):
+    parts = []
+    for k, count in enumerate(chunks):
+        r = count * dm.h
+        parts.append(pc_ref[k, m * r : (m + 1) * r].astype(jnp.bfloat16))
+    return rolled(jnp.concatenate(parts, axis=0), -m)[:, : dm.d]
+
+
+def left_columns(dm, x):
+    return jnp.transpose(x[:, dm.lb :].astype(jnp.float32)) * (1.0 / CG)
+
+
+def pipeline(stages):
+    done = [0] * len(stages)
+    while done[-1] < stages[-1][1]:
+        before = list(done)
+        for k in reversed(range(len(stages))):
+            run, count, beyond = stages[k]
+            ready = count if k == 0 else min(count, before[k - 1] - beyond)
+            size = ready - done[k] if ready == count else (ready - done[k]) // TILE * TILE
+            size = min(size, TILE)
+            if size > 0:
+                run(done[k], done[k] + size)
+                done[k] += size
+
+
+def early_kernel(dm, keep_ref, part_ref, lt_ref, lhs_ref, pc_ref):
+    chunks = dm.chunks[: dm.early]
+    x = keep_ref[...].reshape(-1, dm.lw)
+    rows = KROWS * dm.early
+    lt_ref[...] = left_columns(dm, x[:rows])
+    lanes = {}
+
+    def volume(m0, m1):
+        for m in range(m0, m1):
+            for a, v in enumerate(shifts(column_of(dm, chunks, pc_ref, m), lanes)):
+                part_ref[a, :, m * dm.d : (m + 1) * dm.d] = v
+
+    x_of = lambda k: x[k * KROWS : (k + 1) * KROWS]
+    pipeline([(correlator(dm, chunks, x_of, lt_ref, lhs_ref, pc_ref), dm.mw, 0), (volume, dm.mw, 0)])
+
+
+def main_kernel(dm, keep_ref, got_ref, *refs):
+    part_ref, refs = (refs[0], refs[1:]) if dm.split else (None, refs)
+    w1_ref, w2_ref, w3_ref, head_ref, out_ref, x_ref, lt_ref, lhs_ref, pc_ref = refs[:9]
+    a1_ref, a2_ref, a3_ref, p1_ref, p2_ref, p3_ref, s_ref = refs[9:]
     d, mw, h, f, bf = dm.d, dm.mw, dm.h, dm.f, jnp.bfloat16
     chip, core = lax.axis_index("disp") // 2, lax.axis_index("disp") % 2
     base = lax.axis_index("col") * dm.strip + lax.axis_index("disp") * dm.bw
     total = dm.strips * dm.strip
-
-    for m in range(dm.chips):
-        kept, got = flat(keep_ref.at[m]), flat(got_ref.at[m])
-        both = [jnp.where(core == 0, kept, got), jnp.where(core == 0, got, kept)]
+    chunks = dm.chunks[dm.early :]
+
+    if dm.split:
+        half, early = dm.rows // 2, KROWS * dm.early
+        x_ref[:half] = keep_ref[...].reshape(half, dm.lw)
+        x_ref[half:] = got_ref[...].reshape(half, dm.lw)
+        sources = [x_ref[half + k * KROWS : half + (k + 1) * KROWS] for k in range(dm.early)]
+        if early < half:
+            rest = [keep_ref[...].reshape(half, dm.lw)[early:], got_ref[...].reshape(half, dm.lw)[early:]]
+            sources.append(jnp.concatenate(rest, axis=0))
+        at = 0
+        for x in sources:
+            lt_ref[:, at : at + x.shape[0]] = left_columns(dm, x)
+            at += x.shape[0]
+        x_of = lambda k: sources[k]
+    else:
         rows = 2 * dm.own_rows
-        both = jnp.concatenate(both, axis=0)
-        x_ref[m * rows : (m + 1) * rows] = both.astype(bf)
-        lt_ref[:, m * rows : (m + 1) * rows] = jnp.transpose(both[:, dm.lb :]) * (1.0 / CG)
-
-    keeps = []
-    for count in dm.chunks:
-        r, q = count * h, count * CG * h
-        lane = lane_iota((r, q))
-        sub = lax.broadcasted_iota(jnp.int32, (r, q), 0)
-        keeps.append((lane % h == sub // count) & (lane // (CG * h) == sub % count))
-
-    def correlate(m0, m1):
-        first = 0
-        for k, count in enumerate(dm.chunks):
-            r, q = count * h, count * CG * h
-            for m in range(m0, m1):
-                at = dm.lo - dm.lb + m
-                line = jnp.broadcast_to(lt_ref[at : at + 1, first : first + q], (r, q))
-                lhs_ref[k, m * r : (m + 1) * r, :q] = jnp.where(keeps[k], line, 0.0).astype(bf)
-            pc_ref[k, m0 * r : m1 * r] = jnp.dot(
-                lhs_ref[k, m0 * r : m1 * r, :q],
-                x_ref[first : first + q, :],
-                preferred_element_type=jnp.float32,
-            )
-            first += q
+        for m in range(dm.chips):
+            kept, got = flat(keep_ref.at[m]), flat(got_ref.at[m])
+            both = [jnp.where(core == 0, kept, got), jnp.where(core == 0, got, kept)]
+            both = jnp.concatenate(both, axis=0)
+            x_ref[m * rows : (m + 1) * rows] = both.astype(bf)
+            lt_ref[:, m * rows : (m + 1) * rows] = left_columns(dm, both)
+        x_of = lambda k: x_ref[k * KROWS : k * KROWS + chunks[k] * CG * h]
 
     lanes = {}
 
-    def spread(ref, m, v):
-        rows = v.shape[0]
-        if rows not in lanes:
-            lanes[rows] = lane_iota((rows, d))
-        lane = lanes[rows]
-        at = slice(m * d, (m + 1) * d)
-        zero = jnp.zeros_like(v)
-        ref[:rows, at] = jnp.where(lane < d - 1, rolled(v, -1), zero)
-        ref[rows : 2 * rows, at] = v
-        ref[2 * rows :, at] = jnp.where(lane > 0, rolled(v, 1), zero)
+    def spread(ref, m, v, first=0):
+        rows = first + v.shape[0]
+        for a, shifted in enumerate(shifts(v, lanes)):
+            ref[a * rows + first : (a + 1) * rows, m * d : (m + 1) * d] = shifted
 
     def volume(m0, m1):
         for m in range(m0, m1):
-            parts = [pc_ref[k, m * c * h : (m + 1) * c * h].astype(bf) for k, c in enumerate(dm.chunks)]
-            spread(a1_ref, m, rolled(jnp.concatenate(parts, axis=0), -m)[:, :d])
+            spread(a1_ref, m, column_of(dm, chunks, pc_ref, m), dm.early_rows)
+            if dm.split:
+                at = slice(m * d, (m + 1) * d)
+                for a in range(3):
+                    first = a * h * dm.g
+                    a1_ref[first : first + dm.early_rows, at] = part_ref[a, :, at]
 
     def product(w_ref, a_ref, p_ref):
         def run(m0, m1):
@@ -290,7 +381,7 @@
             s_ref[row, m : m + 1, :] = jnp.sum(z[row * f : (row + 1) * f], axis=0, keepdims=True)
 
     stages = [
-        (correlate, mw, 0),
+        (correlator(dm, chunks, x_of, lt_ref, lhs_ref, pc_ref), mw, 0),
         (volume, mw, 0),
         (product(w1_ref, a1_ref, p1_ref), mw, 0),
         (taken(p1_ref, activity(a2_ref, 1)), mw - 2, 2),
@@ -299,18 +390,7 @@
         (product(w3_ref, a3_ref, p3_ref), mw - 4, 0),
         (taken(p3_ref, score), mw - 6, 2),
     ]
-    done = [0] * len(stages)
-    while done[-1] < stages[-1][1]:
-        before = list(done)
-        for k in reversed(range(len(stages))):
-            run, count, beyond = stages[k]
-            ready = count if k == 0 else min(count, before[k - 1] - beyond)
-            last = ready == count
-            size = ready - done[k] if last else (ready - done[k]) // TILE * TILE
-            size = min(size, TILE)
-            if size > 0:
-                run(done[k], done[k] + size)
-                done[k] += size
+    pipeline(stages)
 
     disp = (d - 1) - lane_iota((dm.bw, d))
     column = base + lax.broadcasted_iota(jnp.int32, (dm.bw, d), 0)
@@ -328,14 +408,9 @@
         band = pltpu.roll(band, 3, 1, stride=1, stride_axis=0)
         bands += [band] * dm.lg
     band = jnp.concatenate(bands, axis=0)
-    high = band.astype(bf)
-    low = (band - high.astype(jnp.float32)).astype(bf)
-    sums = None
-    for part in (high, low):
-        term = lax.dot_general(
-            x_ref[...], part, (((1,), (1,)), ((), ())), preferred_element_type=jnp.float32
-        )
-        sums = term if sums is None else sums + term
+    sums = lax.dot_general(
+        x_ref[...], band.astype(bf), (((1,), (1,)), ((), ())), preferred_element_type=jnp.float32
+    )
     row = lax.broadcasted_iota(jnp.int32, (dm.rows, LANES), 0) % h
     warped = sums[:, :LANES]
     for k in range(1, h):
@@ -356,7 +431,11 @@
         packed = mine[: dm.rg]
         for g in range(1, dm.lg):
             packed = jnp.where(group == g, mine[g * dm.rg : (g + 1) * dm.rg], packed)
-        out_ref[(j // 2 ^ chip) * 2 + j % 2] = packed.astype(out_ref.dtype)
+        if dm.split:
+            target = (j % dm.chips ^ chip) * 2 + (j // dm.chips ^ core)
+        else:
+            target = (j // 2 ^ chip) * 2 + j % 2
+        out_ref[target] = packed.astype(out_ref.dtype)
 
 
 def unpack_kernel(dm, y_ref, warped_ref, disparity_ref):
@@ -452,18 +531,34 @@
     keep, give = call(split_kernel, [half, half], windows)
     got = lax.ppermute(give, "disp", [(i, i ^ 1) for i in range(n)])
 
-    r_max = max(dm.chunks) * dm.h
+    def stage(chunks):
+        r = max(chunks) * dm.h
+        return [
+            pltpu.VMEM((dm.lw - dm.lb, sum(chunks) * CG * dm.h), f32),
+            pltpu.VMEM((len(chunks), dm.mw * r, KROWS), bf),
+            pltpu.VMEM((len(chunks), dm.mw * r, dm.lw), f32),
+        ]
+
     columns = [dm.mw, dm.mw - 2, dm.mw - 4]
+    operands = [keep, got]
+    if dm.split:
+        operands.append(
+            call(
+                early_kernel,
+                jax.ShapeDtypeStruct((3, dm.early_rows, dm.mw * dm.d), bf),
+                [keep],
+                mib=16,
+                scratch_shapes=stage(dm.chunks[: dm.early]),
+            )
+        )
     packed = call(
         main_kernel,
         jax.ShapeDtypeStruct((n, dm.rg, LANES), bf),
-        [keep, got, w1, w2, w3, head],
+        operands + [w1, w2, w3, head],
         mib=32,
         scratch_shapes=[
             pltpu.VMEM((dm.rows, dm.lw), bf),
-            pltpu.VMEM((dm.lw - dm.lb, dm.rows), f32),
-            pltpu.VMEM((len(dm.chunks), dm.mw * r_max, KROWS), bf),
-            pltpu.VMEM((len(dm.chunks), dm.mw * r_max, dm.lw), f32),
+            *stage(dm.chunks[dm.early :]),
             *[pltpu.VMEM((k, c * dm.d), bf) for k, c in zip(depths, columns)],
             *[pltpu.VMEM((m3, c * dm.d), f32) for c in columns],
             pltpu.VMEM((dm.h, dm.bw, dm.d), f32),

time: 31.7 us -> 30.7 us (0.968)
  waiting for transfers between devices: 7.88 us -> 7.2 us
  Pallas kernels: 8.45 us -> 8.1 us
    ppermute x1, waiting for transfers between devices: 1.38 us -> 0.73 us  [shards(): got = lax.ppermute(give, 'disp', [(i, i ^ 1) for i in range(n)])]
    pallas_call x6 -> x7, Pallas kernels: 8.45 us -> 8.1 us  [call(): pl.pallas_call(functools.partial(kernel, dm), out_shape=out_shape, in_spe...]
  transfers between devices with their start and end apart: 6 -> 6, of which waited for: 5 -> 5; matrix products, arithmetic and copies ran while one was open for 0% -> 0% of each run, Pallas kernels for 7% -> 9%
where the time goes in v5:
time: 30.7 us; the launch traced here: 30.5 us
  Pallas kernels  8.1 us (26%)
  blocking collectives  7.31 us (24%)
  waiting for transfers between devices  7.2 us (23%)
  starting transfers between devices  7.17 us (23%)
  between operations  0.7 us (2%)
    pallas_call x7, Pallas kernels, call(): pl.pallas_call(functools.partial(kernel, dm), out_shape=out_shape, in_spe...  8.1 us
    all_to_all x1, blocking collectives, shards(): y = lax.all_to_all(packed, 'disp', 0, 0)  7.31 us
    ppermute x2, waiting for transfers between devices, shards(): arrived.append(lax.ppermute(edges[first], 'col', pairs))  3.97 us
    ppermute x3, starting transfers between devices, shards(): lax.ppermute(v, 'disp', [(i, i ^ 2 * m) for i in range(n)])  3.55 us
    ppermute x2, starting transfers between devices, shards(): arrived.append(lax.ppermute(edges[first], 'col', pairs))  3.55 us
    ppermute x3, waiting for transfers between devices, shards(): lax.ppermute(v, 'disp', [(i, i ^ 2 * m) for i in range(n)])  2.5 us
    ppermute x1, waiting for transfers between devices, shards(): got = lax.ppermute(give, 'disp', [(i, i ^ 1) for i in range(n)])  0.73 us
  transfers between devices with their start and end apart: 6, of which 5 were waited for; matrix products, arithmetic and copies ran while one was open for 0% of the time, Pallas kernels for 9%

profile of v5, /device:TPU:16, one launch (start us, length us, event | category | flops | bytes accessed | tf_op | source)
XLA Modules:
  0.0 30.5 jit_solution(14019439529449562116)
XLA Ops:
  0.6 0.9 %shard_map.77 = (bf16[80,256]{1,0:T(8,128)(2,1)S(1)}, bf16[80,256]{1,0:T(8,128)(2,1)S(1)}, bf16[80,256]{1,0:T(8,128)(2,1)S(1)}, bf16[80,256]{1,0:T(8,128)(2,1)S(1)}) custom-call(bf16[40,2,256]{2,1,0:T(2,128)(2,1)} %left_hbm.1, bf16[40,2,256]{2,1,0:T(2,128)(2,1)} %right_hbm.1), custom_call_target="tpu_custom_call" | custom-call | tf_op jit(solution)/shard_map/pallas_call | solution.py:475
  1.6 1.6 %collective-permute-start = (bf16[80,256]{1,0:T(8,128)(2,1)S(1)}, bf16[80,256]{1,0:T(8,128)(2,1)S(1)}, u32[]{:S(2)}, u32[]{:S(2)}) collective-permute-start(bf16[80,256]{1,0:T(8,128)(2,1)S(1)} %get-tuple-element.31), channel_id=1, source_target_pairs={{0,1},{2,3},{1,0},{3,2},{4,5},{6,7},{5,4},{7,6},{8,9},{10,11},{9,8... | collective-permute-start | bytes 122888 | tf_op jit(solution)/shard_map/ppermute | solution.py:501
  3.2 1.9 %collective-permute-start.1 = (bf16[80,256]{1,0:T(8,128)(2,1)S(1)}, bf16[80,256]{1,0:T(8,128)(2,1)S(1)}, u32[]{:S(2)}, u32[]{:S(2)}) collective-permute-start(bf16[80,256]{1,0:T(8,128)(2,1)S(1)} %get-tuple-element.32), channel_id=1, source_target_pairs={{1,2},{2,1},{5,6},{6,5},{9,10},{10,9},{13,14},{14,13},{17,18},{18,... | collective-permute-start | bytes 122888 | tf_op jit(solution)/shard_map/ppermute | solution.py:501
  5.1 0.5 %collective-permute-done.pair0_ref = bf16[80,256]{1,0:T(8,128)(2,1)S(1)} collective-permute-done((bf16[80,256]{1,0:T(8,128)(2,1)S(1)}, bf16[80,256]{1,0:T(8,128)(2,1)S(1)}, u32[]{:S(2)}, u32[]{:S(2)}) %collective-permute-start) | collective-permute-done | bytes 40992 | tf_op jit(solution)/shard_map/ppermute | solution.py:501
  5.6 3.5 %collective-permute-done.1.pair1_ref = bf16[80,256]{1,0:T(8,128)(2,1)S(1)} collective-permute-done((bf16[80,256]{1,0:T(8,128)(2,1)S(1)}, bf16[80,256]{1,0:T(8,128)(2,1)S(1)}, u32[]{:S(2)}, u32[]{:S(2)}) %collective-permute-start.1) | collective-permute-done | bytes 40992 | tf_op jit(solution)/shard_map/ppermute | solution.py:501
  9.1 0.2 shard_map.78
  9.4 1.6 %collective-permute-start.2 = (bf16[80,384]{1,0:T(8,128)(2,1)S(1)}, bf16[80,384]{1,0:T(8,128)(2,1)S(1)}, u32[]{:S(2)}, u32[]{:S(2)}) collective-permute-start(bf16[80,384]{1,0:T(8,128)(2,1)S(1)} %get-tuple-element.36), channel_id=1, source_target_pairs={{0,8},{4,12},{8,0},{12,4},{16,24},{20,28},{24,16},{28,20},{1,9},{5... | collective-permute-start | bytes 184328 | tf_op jit(solution)/shard_map/ppermute | solution.py:526
  10.9 1.5 %collective-permute-start.3 = (bf16[80,384]{1,0:T(8,128)(2,1)S(1)}, bf16[80,384]{1,0:T(8,128)(2,1)S(1)}, u32[]{:S(2)}, u32[]{:S(2)}) collective-permute-start(bf16[80,384]{1,0:T(8,128)(2,1)S(1)} %get-tuple-element.37), channel_id=1, source_target_pairs={{0,16},{4,20},{8,24},{12,28},{16,0},{20,4},{24,8},{28,12},{1,17},{... | collective-permute-start | bytes 184328 | tf_op jit(solution)/shard_map/ppermute | solution.py:526
  12.4 0.5 %collective-permute-start.4 = (bf16[80,384]{1,0:T(8,128)(2,1)S(1)}, bf16[80,384]{1,0:T(8,128)(2,1)S(1)}, u32[]{:S(2)}, u32[]{:S(2)}) collective-permute-start(bf16[80,384]{1,0:T(8,128)(2,1)S(1)} %get-tuple-element.38), channel_id=1, source_target_pairs={{0,24},{4,28},{8,16},{12,20},{16,8},{20,12},{24,0},{28,4},{1,25},{... | collective-permute-start | bytes 184328 | tf_op jit(solution)/shard_map/ppermute | solution.py:526
  12.9 2.1 %shard_map.79 = (bf16[192,240]{1,0:T(8,128)(2,1)S(1)}, bf16[192,192]{1,0:T(8,128)(2,1)S(1)}, bf16[192,192]{1,0:T(8,128)(2,1)S(1)}, f32[64,128]{1,0:T(8,128)S(1)}) custom-call(bf16[27,32,40]{2,1,0:T(8,128)(2,1)} %bitcast.10, bf16[27,32,32]{2,1,0:T(8,128)(2,1)} %bitcast.11, bf16[27,32,32]{2,1,0:T(8,128)(2,1)} %bitcast.12, f32[1,32]{1,0:T(1,128)} %bitcast.13), custom_call_target="tpu_custom_call" | custom-call | tf_op jit(solution)/shard_map/pallas_call | solution.py:475
  15.0 0.0 collective-permute-done.2.refs_1_
  15.1 0.3 collective-permute-done.3.refs_2_
  15.4 2.2 %collective-permute-done.4.refs_3_ = bf16[80,384]{1,0:T(8,128)(2,1)S(1)} collective-permute-done((bf16[80,384]{1,0:T(8,128)(2,1)S(1)}, bf16[80,384]{1,0:T(8,128)(2,1)S(1)}, u32[]{:S(2)}, u32[]{:S(2)}) %collective-permute-start.4) | collective-permute-done | bytes 61472 | tf_op jit(solution)/shard_map/ppermute | solution.py:526
  17.6 0.2 shard_map.80
  17.8 0.1 collective-permute-start.5
  17.8 0.6 %shard_map.81.refs_0_ = bf16[3,32,4864]{2,1,0:T(8,128)(2,1)S(1)} custom-call(bf16[4,80,256]{2,1,0:T(8,128)(2,1)S(1)} %get-tuple-element.50.keep_ref), custom_call_target="tpu_custom_call" | custom-call | tf_op jit(solution)/shard_map/pallas_call | solution.py:475
  18.5 0.7 %collective-permute-done.5.got_ref = bf16[4,80,256]{2,1,0:T(8,128)(2,1)S(1)} collective-permute-done((bf16[4,80,256]{2,1,0:T(8,128)(2,1)S(1)}, bf16[4,80,256]{2,1,0:T(8,128)(2,1)S(1)}, u32[]{:S(2)}, u32[]{:S(2)}) %collective-permute-start.5) | collective-permute-done | bytes 163872 | tf_op jit(solution)/shard_map/ppermute | solution.py:532
  19.2 3.2 %shard_map.82 = bf16[8,24,128]{2,1,0:T(8,128)(2,1)S(1)} custom-call(bf16[4,80,256]{2,1,0:T(8,128)(2,1)S(1)} %get-tuple-element.50.keep_ref, bf16[4,80,256]{2,1,0:T(8,128)(2,1)S(1)} %collective-permute-done.5.got_ref, bf16[3,32,4864]{2,1,0:T(8,128)(2,1)S(1)} %shard_map.81.refs_0_, bf16[192,240]{1,0:T(8,128)(2,1)S(1)} %get-tuple-element.52.refs_1_, ...), custom_call_target="tpu_custom_call" | custom-call | tf_op jit(solution)/shard_map/pallas_call | solution.py:475
  22.4 7.3 %all_to_all.5.y_ref = bf16[8,24,128]{2,1,0:T(8,128)(2,1)S(1)} all-to-all(bf16[8,24,128]{2,1,0:T(8,128)(2,1)S(1)} %shard_map.82), channel_id=1, replica_groups=mesh['disp'=8,'col'=4] {'disp'}, dimensions={0} | all-to-all | bytes 98304 | tf_op jit(solution)/shard_map/all_to_all | solution.py:567
  29.7 0.8 %shard_map.83 = (bf16[40,2,256]{2,1,0:T(2,128)(2,1)}, f32[2,256]{1,0:T(2,128)}) custom-call(bf16[8,24,128]{2,1,0:T(8,128)(2,1)S(1)} %all_to_all.5.y_ref), custom_call_target="tpu_custom_call" | custom-call | tf_op jit(solution)/shard_map/pallas_call | solution.py:475
Async XLA Ops:
  1.6 4.1 %collective-permute-start = (bf16[80,256]{1,0:T(8,128)(2,1)S(1)}, bf16[80,256]{1,0:T(8,128)(2,1)S(1)}, u32[]{:S(2)}, u32[]{:S(2)}) collective-permute-start(bf16[80,256]{1,0:T(8,128)(2,1)S(1)} %get-tuple-element.31), channel_id=1, source_target_pairs={{0,1},{2,3},{1,0},{3,2},{4,5},{6,7},{5,4},{7,6},{8,9},{10,11},{9,8... | collective-permute-start | bytes 122888 | tf_op jit(solution)/shard_map/ppermute | solution.py:501
  3.2 5.9 %collective-permute-start.1 = (bf16[80,256]{1,0:T(8,128)(2,1)S(1)}, bf16[80,256]{1,0:T(8,128)(2,1)S(1)}, u32[]{:S(2)}, u32[]{:S(2)}) collective-permute-start(bf16[80,256]{1,0:T(8,128)(2,1)S(1)} %get-tuple-element.32), channel_id=1, source_target_pairs={{1,2},{2,1},{5,6},{6,5},{9,10},{10,9},{13,14},{14,13},{17,18},{18,... | collective-permute-start | bytes 122888 | tf_op jit(solution)/shard_map/ppermute | solution.py:501
  9.4 5.7 %collective-permute-start.2 = (bf16[80,384]{1,0:T(8,128)(2,1)S(1)}, bf16[80,384]{1,0:T(8,128)(2,1)S(1)}, u32[]{:S(2)}, u32[]{:S(2)}) collective-permute-start(bf16[80,384]{1,0:T(8,128)(2,1)S(1)} %get-tuple-element.36), channel_id=1, source_target_pairs={{0,8},{4,12},{8,0},{12,4},{16,24},{20,28},{24,16},{28,20},{1,9},{5... | collective-permute-start | bytes 184328 | tf_op jit(solution)/shard_map/ppermute | solution.py:526
  10.9 4.4 %collective-permute-start.3 = (bf16[80,384]{1,0:T(8,128)(2,1)S(1)}, bf16[80,384]{1,0:T(8,128)(2,1)S(1)}, u32[]{:S(2)}, u32[]{:S(2)}) collective-permute-start(bf16[80,384]{1,0:T(8,128)(2,1)S(1)} %get-tuple-element.37), channel_id=1, source_target_pairs={{0,16},{4,20},{8,24},{12,28},{16,0},{20,4},{24,8},{28,12},{1,17},{... | collective-permute-start | bytes 184328 | tf_op jit(solution)/shard_map/ppermute | solution.py:526
  12.4 5.1 %collective-permute-start.4 = (bf16[80,384]{1,0:T(8,128)(2,1)S(1)}, bf16[80,384]{1,0:T(8,128)(2,1)S(1)}, u32[]{:S(2)}, u32[]{:S(2)}) collective-permute-start(bf16[80,384]{1,0:T(8,128)(2,1)S(1)} %get-tuple-element.38), channel_id=1, source_target_pairs={{0,24},{4,28},{8,16},{12,20},{16,8},{20,12},{24,0},{28,4},{1,25},{... | collective-permute-start | bytes 184328 | tf_op jit(solution)/shard_map/ppermute | solution.py:526
  17.8 1.5 %collective-permute-start.5 = (bf16[4,80,256]{2,1,0:T(8,128)(2,1)S(1)}, bf16[4,80,256]{2,1,0:T(8,128)(2,1)S(1)}, u32[]{:S(2)}, u32[]{:S(2)}) collective-permute-start(bf16[4,80,256]{2,1,0:T(8,128)(2,1)S(1)} %get-tuple-element.51), channel_id=1, source_target_pairs={{0,4},{4,0},{8,12},{12,8},{16,20},{20,16},{24,28},{28,24},{1,5},{5... | collective-permute-start | bytes 491528 | tf_op jit(solution)/shard_map/ppermute | solution.py:532

commit v6 on v5

--- a/solution.py
+++ b/solution.py
@@ -6,6 +6,7 @@
 from jax.experimental import pallas as pl
 from jax.experimental.pallas import tpu as pltpu
 from jax.sharding import PartitionSpec as P
+
 
 DG = 16
 CG = 8
@@ -516,16 +517,16 @@
         + [pltpu.VMEM((1, dm.f), f32), pltpu.SemaphoreType.DMA((4,))],
     )
 
-    own_window, *windows = call(
+    own_window, *sent = call(
         pack_kernel,
         [jax.ShapeDtypeStruct((dm.own_rows, dm.lw2), bf)] * dm.chips,
         [left, right] + arrived,
         scratch_shapes=[pltpu.VMEM((dm.chips, dm.own_rows, dm.lw2), bf)],
     )
-    windows = [own_window] + [
-        lax.ppermute(v, "disp", [(i, i ^ (2 * m)) for i in range(n)])
-        for m, v in enumerate(windows, 1)
-    ]
+    windows = [own_window]
+    for m in range(1, dm.chips):
+        pairs = [(i, i ^ (2 * m)) for i in range(n)]
+        windows.append(lax.ppermute(sent[m - 1], "disp", pairs))
     windows, (w1, w2, w3, head) = lax.optimization_barrier((windows, (w1, w2, w3, head)))
     half = jax.ShapeDtypeStruct((dm.chips, dm.own_rows, dm.lw), bf)
     keep, give = call(split_kernel, [half, half], windows)

time: 30.7 us -> 30.7 us (level)
  no operation moved by 1% of the time
where the time goes in v6:
time: 30.7 us; the launch traced here: 30.5 us
  Pallas kernels  8.1 us (26%)
  blocking collectives  7.31 us (24%)
  waiting for transfers between devices  7.2 us (23%)
  starting transfers between devices  7.17 us (23%)
  between operations  0.7 us (2%)
    pallas_call x7, Pallas kernels, call(): pl.pallas_call(functools.partial(kernel, dm), out_shape=out_shape, in_spe...  8.1 us
    all_to_all x1, blocking collectives, shards(): y = lax.all_to_all(packed, 'disp', 0, 0)  7.31 us
    ppermute x2, waiting for transfers between devices, shards(): arrived.append(lax.ppermute(edges[first], 'col', pairs))  3.97 us
    ppermute x3, starting transfers between devices, shards(): windows.append(lax.ppermute(sent[m - 1], 'disp', pairs))  3.55 us
    ppermute x2, starting transfers between devices, shards(): arrived.append(lax.ppermute(edges[first], 'col', pairs))  3.55 us
    ppermute x3, waiting for transfers between devices, shards(): windows.append(lax.ppermute(sent[m - 1], 'disp', pairs))  2.5 us
    ppermute x1, waiting for transfers between devices, shards(): got = lax.ppermute(give, 'disp', [(i, i ^ 1) for i in range(n)])  0.73 us
  transfers between devices with their start and end apart: 6, of which 5 were waited for; matrix products, arithmetic and copies ran while one was open for 0% of the time, Pallas kernels for 9%

profile of v6, /device:TPU:16, one launch (start us, length us, event | category | flops | bytes accessed | tf_op | source)
XLA Modules:
  0.0 30.5 jit_solution(14019439529449562116)
XLA Ops:
  0.6 0.9 %shard_map.77 = (bf16[80,256]{1,0:T(8,128)(2,1)S(1)}, bf16[80,256]{1,0:T(8,128)(2,1)S(1)}, bf16[80,256]{1,0:T(8,128)(2,1)S(1)}, bf16[80,256]{1,0:T(8,128)(2,1)S(1)}) custom-call(bf16[40,2,256]{2,1,0:T(2,128)(2,1)} %left_hbm.1, bf16[40,2,256]{2,1,0:T(2,128)(2,1)} %right_hbm.1), custom_call_target="tpu_custom_call" | custom-call | tf_op jit(solution)/shard_map/pallas_call | solution.py:476
  1.6 1.6 %collective-permute-start = (bf16[80,256]{1,0:T(8,128)(2,1)S(1)}, bf16[80,256]{1,0:T(8,128)(2,1)S(1)}, u32[]{:S(2)}, u32[]{:S(2)}) collective-permute-start(bf16[80,256]{1,0:T(8,128)(2,1)S(1)} %get-tuple-element.31), channel_id=1, source_target_pairs={{0,1},{2,3},{1,0},{3,2},{4,5},{6,7},{5,4},{7,6},{8,9},{10,11},{9,8... | collective-permute-start | bytes 122888 | tf_op jit(solution)/shard_map/ppermute | solution.py:502
  3.2 1.9 %collective-permute-start.1 = (bf16[80,256]{1,0:T(8,128)(2,1)S(1)}, bf16[80,256]{1,0:T(8,128)(2,1)S(1)}, u32[]{:S(2)}, u32[]{:S(2)}) collective-permute-start(bf16[80,256]{1,0:T(8,128)(2,1)S(1)} %get-tuple-element.32), channel_id=1, source_target_pairs={{1,2},{2,1},{5,6},{6,5},{9,10},{10,9},{13,14},{14,13},{17,18},{18,... | collective-permute-start | bytes 122888 | tf_op jit(solution)/shard_map/ppermute | solution.py:502
  5.1 0.5 %collective-permute-done.pair0_ref = bf16[80,256]{1,0:T(8,128)(2,1)S(1)} collective-permute-done((bf16[80,256]{1,0:T(8,128)(2,1)S(1)}, bf16[80,256]{1,0:T(8,128)(2,1)S(1)}, u32[]{:S(2)}, u32[]{:S(2)}) %collective-permute-start) | collective-permute-done | bytes 40992 | tf_op jit(solution)/shard_map/ppermute | solution.py:502
  5.6 3.5 %collective-permute-done.1.pair1_ref = bf16[80,256]{1,0:T(8,128)(2,1)S(1)} collective-permute-done((bf16[80,256]{1,0:T(8,128)(2,1)S(1)}, bf16[80,256]{1,0:T(8,128)(2,1)S(1)}, u32[]{:S(2)}, u32[]{:S(2)}) %collective-permute-start.1) | collective-permute-done | bytes 40992 | tf_op jit(solution)/shard_map/ppermute | solution.py:502
  9.1 0.2 shard_map.78
  9.4 1.6 %collective-permute-start.2 = (bf16[80,384]{1,0:T(8,128)(2,1)S(1)}, bf16[80,384]{1,0:T(8,128)(2,1)S(1)}, u32[]{:S(2)}, u32[]{:S(2)}) collective-permute-start(bf16[80,384]{1,0:T(8,128)(2,1)S(1)} %get-tuple-element.36), channel_id=1, source_target_pairs={{0,8},{4,12},{8,0},{12,4},{16,24},{20,28},{24,16},{28,20},{1,9},{5... | collective-permute-start | bytes 184328 | tf_op jit(solution)/shard_map/ppermute | solution.py:529
  10.9 1.5 %collective-permute-start.3 = (bf16[80,384]{1,0:T(8,128)(2,1)S(1)}, bf16[80,384]{1,0:T(8,128)(2,1)S(1)}, u32[]{:S(2)}, u32[]{:S(2)}) collective-permute-start(bf16[80,384]{1,0:T(8,128)(2,1)S(1)} %get-tuple-element.37), channel_id=1, source_target_pairs={{0,16},{4,20},{8,24},{12,28},{16,0},{20,4},{24,8},{28,12},{1,17},{... | collective-permute-start | bytes 184328 | tf_op jit(solution)/shard_map/ppermute | solution.py:529
  12.4 0.5 %collective-permute-start.4 = (bf16[80,384]{1,0:T(8,128)(2,1)S(1)}, bf16[80,384]{1,0:T(8,128)(2,1)S(1)}, u32[]{:S(2)}, u32[]{:S(2)}) collective-permute-start(bf16[80,384]{1,0:T(8,128)(2,1)S(1)} %get-tuple-element.38), channel_id=1, source_target_pairs={{0,24},{4,28},{8,16},{12,20},{16,8},{20,12},{24,0},{28,4},{1,25},{... | collective-permute-start | bytes 184328 | tf_op jit(solution)/shard_map/ppermute | solution.py:529
  12.9 2.1 %shard_map.79 = (bf16[192,240]{1,0:T(8,128)(2,1)S(1)}, bf16[192,192]{1,0:T(8,128)(2,1)S(1)}, bf16[192,192]{1,0:T(8,128)(2,1)S(1)}, f32[64,128]{1,0:T(8,128)S(1)}) custom-call(bf16[27,32,40]{2,1,0:T(8,128)(2,1)} %bitcast.10, bf16[27,32,32]{2,1,0:T(8,128)(2,1)} %bitcast.11, bf16[27,32,32]{2,1,0:T(8,128)(2,1)} %bitcast.12, f32[1,32]{1,0:T(1,128)} %bitcast.13), custom_call_target="tpu_custom_call" | custom-call | tf_op jit(solution)/shard_map/pallas_call | solution.py:476
  15.0 0.0 collective-permute-done.2.refs_1_
  15.1 0.3 collective-permute-done.3.refs_2_
  15.4 2.2 %collective-permute-done.4.refs_3_ = bf16[80,384]{1,0:T(8,128)(2,1)S(1)} collective-permute-done((bf16[80,384]{1,0:T(8,128)(2,1)S(1)}, bf16[80,384]{1,0:T(8,128)(2,1)S(1)}, u32[]{:S(2)}, u32[]{:S(2)}) %collective-permute-start.4) | collective-permute-done | bytes 61472 | tf_op jit(solution)/shard_map/ppermute | solution.py:529
  17.6 0.2 shard_map.80
  17.8 0.1 collective-permute-start.5
  17.8 0.6 %shard_map.81.refs_0_ = bf16[3,32,4864]{2,1,0:T(8,128)(2,1)S(1)} custom-call(bf16[4,80,256]{2,1,0:T(8,128)(2,1)S(1)} %get-tuple-element.50.keep_ref), custom_call_target="tpu_custom_call" | custom-call | tf_op jit(solution)/shard_map/pallas_call | solution.py:476
  18.5 0.7 %collective-permute-done.5.got_ref = bf16[4,80,256]{2,1,0:T(8,128)(2,1)S(1)} collective-permute-done((bf16[4,80,256]{2,1,0:T(8,128)(2,1)S(1)}, bf16[4,80,256]{2,1,0:T(8,128)(2,1)S(1)}, u32[]{:S(2)}, u32[]{:S(2)}) %collective-permute-start.5) | collective-permute-done | bytes 163872 | tf_op jit(solution)/shard_map/ppermute | solution.py:533
  19.2 3.2 %shard_map.82 = bf16[8,24,128]{2,1,0:T(8,128)(2,1)S(1)} custom-call(bf16[4,80,256]{2,1,0:T(8,128)(2,1)S(1)} %get-tuple-element.50.keep_ref, bf16[4,80,256]{2,1,0:T(8,128)(2,1)S(1)} %collective-permute-done.5.got_ref, bf16[3,32,4864]{2,1,0:T(8,128)(2,1)S(1)} %shard_map.81.refs_0_, bf16[192,240]{1,0:T(8,128)(2,1)S(1)} %get-tuple-element.52.refs_1_, ...), custom_call_target="tpu_custom_call" | custom-call | tf_op jit(solution)/shard_map/pallas_call | solution.py:476
  22.4 7.3 %all_to_all.5.y_ref = bf16[8,24,128]{2,1,0:T(8,128)(2,1)S(1)} all-to-all(bf16[8,24,128]{2,1,0:T(8,128)(2,1)S(1)} %shard_map.82), channel_id=1, replica_groups=mesh['disp'=8,'col'=4] {'disp'}, dimensions={0} | all-to-all | bytes 98304 | tf_op jit(solution)/shard_map/all_to_all | solution.py:568
  29.7 0.8 %shard_map.83 = (bf16[40,2,256]{2,1,0:T(2,128)(2,1)}, f32[2,256]{1,0:T(2,128)}) custom-call(bf16[8,24,128]{2,1,0:T(8,128)(2,1)S(1)} %all_to_all.5.y_ref), custom_call_target="tpu_custom_call" | custom-call | tf_op jit(solution)/shard_map/pallas_call | solution.py:476
Async XLA Ops:
  1.6 4.1 %collective-permute-start = (bf16[80,256]{1,0:T(8,128)(2,1)S(1)}, bf16[80,256]{1,0:T(8,128)(2,1)S(1)}, u32[]{:S(2)}, u32[]{:S(2)}) collective-permute-start(bf16[80,256]{1,0:T(8,128)(2,1)S(1)} %get-tuple-element.31), channel_id=1, source_target_pairs={{0,1},{2,3},{1,0},{3,2},{4,5},{6,7},{5,4},{7,6},{8,9},{10,11},{9,8... | collective-permute-start | bytes 122888 | tf_op jit(solution)/shard_map/ppermute | solution.py:502
  3.2 5.9 %collective-permute-start.1 = (bf16[80,256]{1,0:T(8,128)(2,1)S(1)}, bf16[80,256]{1,0:T(8,128)(2,1)S(1)}, u32[]{:S(2)}, u32[]{:S(2)}) collective-permute-start(bf16[80,256]{1,0:T(8,128)(2,1)S(1)} %get-tuple-element.32), channel_id=1, source_target_pairs={{1,2},{2,1},{5,6},{6,5},{9,10},{10,9},{13,14},{14,13},{17,18},{18,... | collective-permute-start | bytes 122888 | tf_op jit(solution)/shard_map/ppermute | solution.py:502
  9.4 5.7 %collective-permute-start.2 = (bf16[80,384]{1,0:T(8,128)(2,1)S(1)}, bf16[80,384]{1,0:T(8,128)(2,1)S(1)}, u32[]{:S(2)}, u32[]{:S(2)}) collective-permute-start(bf16[80,384]{1,0:T(8,128)(2,1)S(1)} %get-tuple-element.36), channel_id=1, source_target_pairs={{0,8},{4,12},{8,0},{12,4},{16,24},{20,28},{24,16},{28,20},{1,9},{5... | collective-permute-start | bytes 184328 | tf_op jit(solution)/shard_map/ppermute | solution.py:529
  10.9 4.4 %collective-permute-start.3 = (bf16[80,384]{1,0:T(8,128)(2,1)S(1)}, bf16[80,384]{1,0:T(8,128)(2,1)S(1)}, u32[]{:S(2)}, u32[]{:S(2)}) collective-permute-start(bf16[80,384]{1,0:T(8,128)(2,1)S(1)} %get-tuple-element.37), channel_id=1, source_target_pairs={{0,16},{4,20},{8,24},{12,28},{16,0},{20,4},{24,8},{28,12},{1,17},{... | collective-permute-start | bytes 184328 | tf_op jit(solution)/shard_map/ppermute | solution.py:529
  12.4 5.1 %collective-permute-start.4 = (bf16[80,384]{1,0:T(8,128)(2,1)S(1)}, bf16[80,384]{1,0:T(8,128)(2,1)S(1)}, u32[]{:S(2)}, u32[]{:S(2)}) collective-permute-start(bf16[80,384]{1,0:T(8,128)(2,1)S(1)} %get-tuple-element.38), channel_id=1, source_target_pairs={{0,24},{4,28},{8,16},{12,20},{16,8},{20,12},{24,0},{28,4},{1,25},{... | collective-permute-start | bytes 184328 | tf_op jit(solution)/shard_map/ppermute | solution.py:529
  17.8 1.5 %collective-permute-start.5 = (bf16[4,80,256]{2,1,0:T(8,128)(2,1)S(1)}, bf16[4,80,256]{2,1,0:T(8,128)(2,1)S(1)}, u32[]{:S(2)}, u32[]{:S(2)}) collective-permute-start(bf16[4,80,256]{2,1,0:T(8,128)(2,1)S(1)} %get-tuple-element.51), channel_id=1, source_target_pairs={{0,4},{4,0},{8,12},{12,8},{16,20},{20,16},{24,28},{28,24},{1,5},{5... | collective-permute-start | bytes 491528 | tf_op jit(solution)/shard_map/ppermute | solution.py:533

commit v7 on v6

--- a/solution.py
+++ b/solution.py
@@ -298,10 +298,10 @@
 
 def main_kernel(dm, keep_ref, got_ref, *refs):
     part_ref, refs = (refs[0], refs[1:]) if dm.split else (None, refs)
-    w1_ref, w2_ref, w3_ref, head_ref, out_ref, x_ref, lt_ref, lhs_ref, pc_ref = refs[:9]
-    a1_ref, a2_ref, a3_ref, p1_ref, p2_ref, p3_ref, s_ref = refs[9:]
+    w1_ref, w2_ref, w3_ref, head_ref, same_ref, other_ref, x_ref, lt_ref, lhs_ref, pc_ref = refs[:10]
+    a1_ref, a2_ref, a3_ref, p1_ref, p2_ref, p3_ref, s_ref = refs[10:]
     d, mw, h, f, bf = dm.d, dm.mw, dm.h, dm.f, jnp.bfloat16
-    chip, core = lax.axis_index("disp") // 2, lax.axis_index("disp") % 2
+    core = lax.axis_index("disp") % 2
     base = lax.axis_index("col") * dm.strip + lax.axis_index("disp") * dm.bw
     total = dm.strips * dm.strip
     chunks = dm.chunks[dm.early :]
@@ -427,19 +427,38 @@
     lines.append(jnp.zeros((dm.lg * dm.rg - dm.own_rows - len(lines), LANES), jnp.float32))
     lines = jnp.concatenate(lines, axis=0)
     group = lane_iota((dm.rg, LANES)) // dm.bw
+    blocks = []
     for j in range(dm.n):
         mine = jnp.concatenate([warped[j * dm.own_rows : (j + 1) * dm.own_rows], lines], axis=0)
         packed = mine[: dm.rg]
         for g in range(1, dm.lg):
             packed = jnp.where(group == g, mine[g * dm.rg : (g + 1) * dm.rg], packed)
+        blocks.append(packed)
+    for m in range(dm.chips):
         if dm.split:
-            target = (j % dm.chips ^ chip) * 2 + (j // dm.chips ^ core)
+            same, other = blocks[m], blocks[dm.chips + m]
         else:
-            target = (j // 2 ^ chip) * 2 + j % 2
-        out_ref[target] = packed.astype(out_ref.dtype)
-
-
-def unpack_kernel(dm, y_ref, warped_ref, disparity_ref):
+            pair = blocks[2 * m : 2 * m + 2]
+            same = jnp.where(core == 0, pair[0], pair[1])
+            other = jnp.where(core == 0, pair[1], pair[0])
+        same_ref[m] = same.astype(same_ref.dtype)
+        other_ref[m] = other.astype(other_ref.dtype)
+
+
+def join_kernel(dm, same_ref, theirs_ref, *outs):
+    for m, out in enumerate(outs, 1):
+        out[0] = same_ref[m]
+        out[1] = theirs_ref[m]
+
+
+def unpack_kernel(dm, same_ref, theirs_ref, *refs):
+    *others, warped_ref, disparity_ref, y_ref = refs
+    chip, core = lax.axis_index("disp") // 2, lax.axis_index("disp") % 2
+    y_ref[chip * 2 + core] = same_ref[0].astype(jnp.float32)
+    y_ref[chip * 2 + 1 - core] = theirs_ref[0].astype(jnp.float32)
+    for m, ref in enumerate(others, 1):
+        y_ref[(chip ^ m) * 2 + core] = ref[0].astype(jnp.float32)
+        y_ref[(chip ^ m) * 2 + 1 - core] = ref[1].astype(jnp.float32)
     per = LANES // dm.bw
     lane = lane_iota((dm.rg, LANES))
     tiles = []
@@ -448,7 +467,7 @@
         for g in range(dm.lg):
             total = None
             for p in range(per):
-                piece = rolled(flat(y_ref.at[t * per + p]), (p - g) * dm.bw)
+                piece = rolled(y_ref[t * per + p], (p - g) * dm.bw)
                 keep = (lane >= p * dm.bw) & (lane < (p + 1) * dm.bw)
                 total = piece if total is None else jnp.where(keep, piece, total)
             groups.append(total)
@@ -552,9 +571,10 @@
                 scratch_shapes=stage(dm.chunks[: dm.early]),
             )
         )
-    packed = call(
+    blocks = jax.ShapeDtypeStruct((dm.chips, dm.rg, LANES), bf)
+    same, other = call(
         main_kernel,
-        jax.ShapeDtypeStruct((n, dm.rg, LANES), bf),
+        [blocks, blocks],
         operands + [w1, w2, w3, head],
         mib=32,
         scratch_shapes=[
@@ -565,7 +585,16 @@
             pltpu.VMEM((dm.h, dm.bw, dm.d), f32),
         ],
     )
-    y = lax.all_to_all(packed, "disp", 0, 0)
+    theirs = lax.ppermute(other, "disp", [(i, i ^ 1) for i in range(n)])
+    joined = call(
+        join_kernel,
+        [jax.ShapeDtypeStruct((2, dm.rg, LANES), bf)] * (dm.chips - 1),
+        [same, theirs],
+    )
+    back = []
+    for m in range(1, dm.chips):
+        pairs = [(i, i ^ (2 * m)) for i in range(n)]
+        back.append(lax.ppermute(joined[m - 1], "disp", pairs))
     return tuple(
         call(
             unpack_kernel,
@@ -573,7 +602,8 @@
                 jax.ShapeDtypeStruct(left_feat.shape, bf),
                 jax.ShapeDtypeStruct((dm.h, dm.strip), f32),
             ],
-            [y],
+            [same, theirs] + back,
+            scratch_shapes=[pltpu.VMEM((n, dm.rg, LANES), f32)],
         )
     )
 

time: 30.7 us -> 30.3 us (0.987)
  blocking collectives: 7.31 us -> 0 us
  starting transfers between devices: 7.17 us -> 10.9 us
  waiting for transfers between devices: 7.2 us -> 10.4 us
    all_to_all x1 -> x0, blocking collectives: 7.31 us -> none  [shards(): y = lax.all_to_all(packed, 'disp', 0, 0)]
    ppermute x0 -> x4, starting transfers between devices: none -> 3.69 us  [the longest x3 3.49 us: shards(): back.append(lax.ppermute(joined[m - 1], 'disp', pairs))]
    ppermute x0 -> x4, waiting for transfers between devices: none -> 3.2 us  [the longest x3 2.14 us: shards(): back.append(lax.ppermute(joined[m - 1], 'disp', pairs))]
    pallas_call x7 -> x8, Pallas kernels: 8.1 us -> 8.15 us  [call(): pl.pallas_call(functools.partial(kernel, dm), out_shape=out_shape, in_spe...]
  transfers between devices with their start and end apart: 6 -> 10, of which waited for: 5 -> 9; matrix products, arithmetic and copies ran while one was open for 0% -> 0% of each run, Pallas kernels for 9% -> 9%
where the time goes in v7:
time: 30.3 us; the launch traced here: 30.1 us
  starting transfers between devices  10.9 us (36%)
  waiting for transfers between devices  10.4 us (34%)
  Pallas kernels  8.15 us (27%)
  between operations  0.71 us (2%)
    pallas_call x8, Pallas kernels, call(): pl.pallas_call(functools.partial(kernel, dm), out_shape=out_shape, in_spe...  8.15 us
    ppermute x2, waiting for transfers between devices, shards(): arrived.append(lax.ppermute(edges[first], 'col', pairs))  3.97 us
    ppermute x3, starting transfers between devices, shards(): windows.append(lax.ppermute(sent[m - 1], 'disp', pairs))  3.55 us
    ppermute x2, starting transfers between devices, shards(): arrived.append(lax.ppermute(edges[first], 'col', pairs))  3.55 us
    ppermute x3, starting transfers between devices, shards(): back.append(lax.ppermute(joined[m - 1], 'disp', pairs))  3.49 us
    ppermute x3, waiting for transfers between devices, shards(): windows.append(lax.ppermute(sent[m - 1], 'disp', pairs))  2.5 us
    ppermute x3, waiting for transfers between devices, shards(): back.append(lax.ppermute(joined[m - 1], 'disp', pairs))  2.14 us
    ppermute x1, waiting for transfers between devices, shards(): theirs = lax.ppermute(other, 'disp', [(i, i ^ 1) for i in range(n)])  1.06 us
  transfers between devices with their start and end apart: 10, of which 9 were waited for; matrix products, arithmetic and copies ran while one was open for 0% of the time, Pallas kernels for 9%

profile of v7, /device:TPU:16, one launch (start us, length us, event | category | flops | bytes accessed | tf_op | source)
XLA Modules:
  0.0 30.1 jit_solution(2406232133263624062)
XLA Ops:
  0.6 0.9 %shard_map.77 = (bf16[80,256]{1,0:T(8,128)(2,1)S(1)}, bf16[80,256]{1,0:T(8,128)(2,1)S(1)}, bf16[80,256]{1,0:T(8,128)(2,1)S(1)}, bf16[80,256]{1,0:T(8,128)(2,1)S(1)}) custom-call(bf16[40,2,256]{2,1,0:T(2,128)(2,1)} %left_hbm.1, bf16[40,2,256]{2,1,0:T(2,128)(2,1)} %right_hbm.1), custom_call_target="tpu_custom_call" | custom-call | tf_op jit(solution)/shard_map/pallas_call | solution.py:495
  1.6 1.6 %collective-permute-start = (bf16[80,256]{1,0:T(8,128)(2,1)S(1)}, bf16[80,256]{1,0:T(8,128)(2,1)S(1)}, u32[]{:S(2)}, u32[]{:S(2)}) collective-permute-start(bf16[80,256]{1,0:T(8,128)(2,1)S(1)} %get-tuple-element.36), channel_id=1, source_target_pairs={{0,1},{2,3},{1,0},{3,2},{4,5},{6,7},{5,4},{7,6},{8,9},{10,11},{9,8... | collective-permute-start | bytes 122888 | tf_op jit(solution)/shard_map/ppermute | solution.py:521
  3.2 1.9 %collective-permute-start.1 = (bf16[80,256]{1,0:T(8,128)(2,1)S(1)}, bf16[80,256]{1,0:T(8,128)(2,1)S(1)}, u32[]{:S(2)}, u32[]{:S(2)}) collective-permute-start(bf16[80,256]{1,0:T(8,128)(2,1)S(1)} %get-tuple-element.37), channel_id=1, source_target_pairs={{1,2},{2,1},{5,6},{6,5},{9,10},{10,9},{13,14},{14,13},{17,18},{18,... | collective-permute-start | bytes 122888 | tf_op jit(solution)/shard_map/ppermute | solution.py:521
  5.1 0.5 %collective-permute-done.pair0_ref = bf16[80,256]{1,0:T(8,128)(2,1)S(1)} collective-permute-done((bf16[80,256]{1,0:T(8,128)(2,1)S(1)}, bf16[80,256]{1,0:T(8,128)(2,1)S(1)}, u32[]{:S(2)}, u32[]{:S(2)}) %collective-permute-start) | collective-permute-done | bytes 40992 | tf_op jit(solution)/shard_map/ppermute | solution.py:521
  5.6 3.5 %collective-permute-done.1.pair1_ref = bf16[80,256]{1,0:T(8,128)(2,1)S(1)} collective-permute-done((bf16[80,256]{1,0:T(8,128)(2,1)S(1)}, bf16[80,256]{1,0:T(8,128)(2,1)S(1)}, u32[]{:S(2)}, u32[]{:S(2)}) %collective-permute-start.1) | collective-permute-done | bytes 40992 | tf_op jit(solution)/shard_map/ppermute | solution.py:521
  9.1 0.2 shard_map.78
  9.4 1.6 %collective-permute-start.2 = (bf16[80,384]{1,0:T(8,128)(2,1)S(1)}, bf16[80,384]{1,0:T(8,128)(2,1)S(1)}, u32[]{:S(2)}, u32[]{:S(2)}) collective-permute-start(bf16[80,384]{1,0:T(8,128)(2,1)S(1)} %get-tuple-element.41), channel_id=1, source_target_pairs={{0,8},{4,12},{8,0},{12,4},{16,24},{20,28},{24,16},{28,20},{1,9},{5... | collective-permute-start | bytes 184328 | tf_op jit(solution)/shard_map/ppermute | solution.py:548
  10.9 1.5 %collective-permute-start.3 = (bf16[80,384]{1,0:T(8,128)(2,1)S(1)}, bf16[80,384]{1,0:T(8,128)(2,1)S(1)}, u32[]{:S(2)}, u32[]{:S(2)}) collective-permute-start(bf16[80,384]{1,0:T(8,128)(2,1)S(1)} %get-tuple-element.42), channel_id=1, source_target_pairs={{0,16},{4,20},{8,24},{12,28},{16,0},{20,4},{24,8},{28,12},{1,17},{... | collective-permute-start | bytes 184328 | tf_op jit(solution)/shard_map/ppermute | solution.py:548
  12.4 0.5 %collective-permute-start.4 = (bf16[80,384]{1,0:T(8,128)(2,1)S(1)}, bf16[80,384]{1,0:T(8,128)(2,1)S(1)}, u32[]{:S(2)}, u32[]{:S(2)}) collective-permute-start(bf16[80,384]{1,0:T(8,128)(2,1)S(1)} %get-tuple-element.43), channel_id=1, source_target_pairs={{0,24},{4,28},{8,16},{12,20},{16,8},{20,12},{24,0},{28,4},{1,25},{... | collective-permute-start | bytes 184328 | tf_op jit(solution)/shard_map/ppermute | solution.py:548
  12.9 2.1 %shard_map.79 = (bf16[192,240]{1,0:T(8,128)(2,1)S(1)}, bf16[192,192]{1,0:T(8,128)(2,1)S(1)}, bf16[192,192]{1,0:T(8,128)(2,1)S(1)}, f32[64,128]{1,0:T(8,128)S(1)}) custom-call(bf16[27,32,40]{2,1,0:T(8,128)(2,1)} %bitcast.10, bf16[27,32,32]{2,1,0:T(8,128)(2,1)} %bitcast.11, bf16[27,32,32]{2,1,0:T(8,128)(2,1)} %bitcast.12, f32[1,32]{1,0:T(1,128)} %bitcast.13), custom_call_target="tpu_custom_call" | custom-call | tf_op jit(solution)/shard_map/pallas_call | solution.py:495
  15.1 0.3 %collective-permute-done.3.refs_2_ = bf16[80,384]{1,0:T(8,128)(2,1)S(1)} collective-permute-done((bf16[80,384]{1,0:T(8,128)(2,1)S(1)}, bf16[80,384]{1,0:T(8,128)(2,1)S(1)}, u32[]{:S(2)}, u32[]{:S(2)}) %collective-permute-start.3) | collective-permute-done | bytes 61472 | tf_op jit(solution)/shard_map/ppermute | solution.py:548
  15.4 2.2 %collective-permute-done.4.refs_3_ = bf16[80,384]{1,0:T(8,128)(2,1)S(1)} collective-permute-done((bf16[80,384]{1,0:T(8,128)(2,1)S(1)}, bf16[80,384]{1,0:T(8,128)(2,1)S(1)}, u32[]{:S(2)}, u32[]{:S(2)}) %collective-permute-start.4) | collective-permute-done | bytes 61472 | tf_op jit(solution)/shard_map/ppermute | solution.py:548
  17.8 0.6 %shard_map.81.refs_0_ = bf16[3,32,4864]{2,1,0:T(8,128)(2,1)S(1)} custom-call(bf16[4,80,256]{2,1,0:T(8,128)(2,1)S(1)} %get-tuple-element.55.keep_ref), custom_call_target="tpu_custom_call" | custom-call | tf_op jit(solution)/shard_map/pallas_call | solution.py:495
  18.5 0.7 %collective-permute-done.5.got_ref = bf16[4,80,256]{2,1,0:T(8,128)(2,1)S(1)} collective-permute-done((bf16[4,80,256]{2,1,0:T(8,128)(2,1)S(1)}, bf16[4,80,256]{2,1,0:T(8,128)(2,1)S(1)}, u32[]{:S(2)}, u32[]{:S(2)}) %collective-permute-start.5) | collective-permute-done | bytes 163872 | tf_op jit(solution)/shard_map/ppermute | solution.py:552
  19.2 3.2 %shard_map.82 = (bf16[4,24,128]{2,1,0:T(8,128)(2,1)S(1)}, bf16[4,24,128]{2,1,0:T(8,128)(2,1)S(1)}) custom-call(bf16[4,80,256]{2,1,0:T(8,128)(2,1)S(1)} %get-tuple-element.55.keep_ref, bf16[4,80,256]{2,1,0:T(8,128)(2,1)S(1)} %collective-permute-done.5.got_ref, bf16[3,32,4864]{2,1,0:T(8,128)(2,1)S(1)} %shard_map.81.refs_0_, ...), custom_call_target="tpu_custom_call" | custom-call | tf_op jit(solution)/shard_map/pallas_call | solution.py:495
  22.4 0.2 collective-permute-start.6
  22.6 1.1 %collective-permute-done.6.theirs_ref = bf16[4,24,128]{2,1,0:T(8,128)(2,1)S(1)} collective-permute-done((bf16[4,24,128]{2,1,0:T(8,128)(2,1)S(1)}, bf16[4,24,128]{2,1,0:T(8,128)(2,1)S(1)}, u32[]{:S(2)}, u32[]{:S(2)}) %collective-permute-start.6) | collective-permute-done | bytes 24608 | tf_op jit(solution)/shard_map/ppermute | solution.py:588
  23.7 0.5 %collective-permute-start.7 = (bf16[2,24,128]{2,1,0:T(8,128)(2,1)S(1)}, bf16[2,24,128]{2,1,0:T(8,128)(2,1)S(1)}, u32[]{:S(2)}, u32[]{:S(2)}) collective-permute-start(bf16[2,24,128]{2,1,0:T(8,128)(2,1)S(1)} %get-tuple-element.63), channel_id=1, source_target_pairs={{0,8},{4,12},{8,0},{12,4},{16,24},{20,28},{24,16},{28,20},{1,9},{5... | collective-permute-start | bytes 36872 | tf_op jit(solution)/shard_map/ppermute | solution.py:597
  24.2 0.5 %collective-permute-start.8 = (bf16[2,24,128]{2,1,0:T(8,128)(2,1)S(1)}, bf16[2,24,128]{2,1,0:T(8,128)(2,1)S(1)}, u32[]{:S(2)}, u32[]{:S(2)}) collective-permute-start(bf16[2,24,128]{2,1,0:T(8,128)(2,1)S(1)} %get-tuple-element.64), channel_id=1, source_target_pairs={{0,16},{4,20},{8,24},{12,28},{16,0},{20,4},{24,8},{28,12},{1,17},{... | collective-permute-start | bytes 36872 | tf_op jit(solution)/shard_map/ppermute | solution.py:597
  24.7 2.5 %collective-permute-start.9 = (bf16[2,24,128]{2,1,0:T(8,128)(2,1)S(1)}, bf16[2,24,128]{2,1,0:T(8,128)(2,1)S(1)}, u32[]{:S(2)}, u32[]{:S(2)}) collective-permute-start(bf16[2,24,128]{2,1,0:T(8,128)(2,1)S(1)} %get-tuple-element.65), channel_id=1, source_target_pairs={{0,24},{4,28},{8,16},{12,20},{16,8},{20,12},{24,0},{28,4},{1,25},{... | collective-permute-start | bytes 36872 | tf_op jit(solution)/shard_map/ppermute | solution.py:597
  27.2 0.2 collective-permute-done.7.refs_0_
  27.4 0.5 %collective-permute-done.8.refs_1_ = bf16[2,24,128]{2,1,0:T(8,128)(2,1)S(1)} collective-permute-done((bf16[2,24,128]{2,1,0:T(8,128)(2,1)S(1)}, bf16[2,24,128]{2,1,0:T(8,128)(2,1)S(1)}, u32[]{:S(2)}, u32[]{:S(2)}) %collective-permute-start.8) | collective-permute-done | bytes 12320 | tf_op jit(solution)/shard_map/ppermute | solution.py:597
  27.9 1.4 %collective-permute-done.9.refs_2_ = bf16[2,24,128]{2,1,0:T(8,128)(2,1)S(1)} collective-permute-done((bf16[2,24,128]{2,1,0:T(8,128)(2,1)S(1)}, bf16[2,24,128]{2,1,0:T(8,128)(2,1)S(1)}, u32[]{:S(2)}, u32[]{:S(2)}) %collective-permute-start.9) | collective-permute-done | bytes 12320 | tf_op jit(solution)/shard_map/ppermute | solution.py:597
  29.3 0.8 %shard_map.84 = (bf16[40,2,256]{2,1,0:T(2,128)(2,1)}, f32[2,256]{1,0:T(2,128)}) custom-call(bf16[4,24,128]{2,1,0:T(8,128)(2,1)S(1)} %get-tuple-element.61.same_ref, bf16[4,24,128]{2,1,0:T(8,128)(2,1)S(1)} %collective-permute-done.6.theirs_ref, bf16[2,24,128]{2,1,0:T(8,128)(2,1)S(1)} %collective-permute-done.7.refs_0_, ...), custom_call_target="tpu_custom_call" | custom-call | tf_op jit(solution)/shard_map/pallas_call | solution.py:495
  (4 shorter events, 0.3 us)
Async XLA Ops:
  1.6 4.1 %collective-permute-start = (bf16[80,256]{1,0:T(8,128)(2,1)S(1)}, bf16[80,256]{1,0:T(8,128)(2,1)S(1)}, u32[]{:S(2)}, u32[]{:S(2)}) collective-permute-start(bf16[80,256]{1,0:T(8,128)(2,1)S(1)} %get-tuple-element.36), channel_id=1, source_target_pairs={{0,1},{2,3},{1,0},{3,2},{4,5},{6,7},{5,4},{7,6},{8,9},{10,11},{9,8... | collective-permute-start | bytes 122888 | tf_op jit(solution)/shard_map/ppermute | solution.py:521
  3.2 5.9 %collective-permute-start.1 = (bf16[80,256]{1,0:T(8,128)(2,1)S(1)}, bf16[80,256]{1,0:T(8,128)(2,1)S(1)}, u32[]{:S(2)}, u32[]{:S(2)}) collective-permute-start(bf16[80,256]{1,0:T(8,128)(2,1)S(1)} %get-tuple-element.37), channel_id=1, source_target_pairs={{1,2},{2,1},{5,6},{6,5},{9,10},{10,9},{13,14},{14,13},{17,18},{18,... | collective-permute-start | bytes 122888 | tf_op jit(solution)/shard_map/ppermute | solution.py:521
  9.4 5.7 %collective-permute-start.2 = (bf16[80,384]{1,0:T(8,128)(2,1)S(1)}, bf16[80,384]{1,0:T(8,128)(2,1)S(1)}, u32[]{:S(2)}, u32[]{:S(2)}) collective-permute-start(bf16[80,384]{1,0:T(8,128)(2,1)S(1)} %get-tuple-element.41), channel_id=1, source_target_pairs={{0,8},{4,12},{8,0},{12,4},{16,24},{20,28},{24,16},{28,20},{1,9},{5... | collective-permute-start | bytes 184328 | tf_op jit(solution)/shard_map/ppermute | solution.py:548
  10.9 4.4 %collective-permute-start.3 = (bf16[80,384]{1,0:T(8,128)(2,1)S(1)}, bf16[80,384]{1,0:T(8,128)(2,1)S(1)}, u32[]{:S(2)}, u32[]{:S(2)}) collective-permute-start(bf16[80,384]{1,0:T(8,128)(2,1)S(1)} %get-tuple-element.42), channel_id=1, source_target_pairs={{0,16},{4,20},{8,24},{12,28},{16,0},{20,4},{24,8},{28,12},{1,17},{... | collective-permute-start | bytes 184328 | tf_op jit(solution)/shard_map/ppermute | solution.py:548
  12.4 5.1 %collective-permute-start.4 = (bf16[80,384]{1,0:T(8,128)(2,1)S(1)}, bf16[80,384]{1,0:T(8,128)(2,1)S(1)}, u32[]{:S(2)}, u32[]{:S(2)}) collective-permute-start(bf16[80,384]{1,0:T(8,128)(2,1)S(1)} %get-tuple-element.43), channel_id=1, source_target_pairs={{0,24},{4,28},{8,16},{12,20},{16,8},{20,12},{24,0},{28,4},{1,25},{... | collective-permute-start | bytes 184328 | tf_op jit(solution)/shard_map/ppermute | solution.py:548
  17.8 1.5 %collective-permute-start.5 = (bf16[4,80,256]{2,1,0:T(8,128)(2,1)S(1)}, bf16[4,80,256]{2,1,0:T(8,128)(2,1)S(1)}, u32[]{:S(2)}, u32[]{:S(2)}) collective-permute-start(bf16[4,80,256]{2,1,0:T(8,128)(2,1)S(1)} %get-tuple-element.56), channel_id=1, source_target_pairs={{0,4},{4,0},{8,12},{12,8},{16,20},{20,16},{24,28},{28,24},{1,5},{5... | collective-permute-start | bytes 491528 | tf_op jit(solution)/shard_map/ppermute | solution.py:552
  22.4 1.3 %collective-permute-start.6 = (bf16[4,24,128]{2,1,0:T(8,128)(2,1)S(1)}, bf16[4,24,128]{2,1,0:T(8,128)(2,1)S(1)}, u32[]{:S(2)}, u32[]{:S(2)}) collective-permute-start(bf16[4,24,128]{2,1,0:T(8,128)(2,1)S(1)} %get-tuple-element.62), channel_id=1, source_target_pairs={{0,4},{4,0},{8,12},{12,8},{16,20},{20,16},{24,28},{28,24},{1,5},{5... | collective-permute-start | bytes 73736 | tf_op jit(solution)/shard_map/ppermute | solution.py:588
  23.7 3.7 %collective-permute-start.7 = (bf16[2,24,128]{2,1,0:T(8,128)(2,1)S(1)}, bf16[2,24,128]{2,1,0:T(8,128)(2,1)S(1)}, u32[]{:S(2)}, u32[]{:S(2)}) collective-permute-start(bf16[2,24,128]{2,1,0:T(8,128)(2,1)S(1)} %get-tuple-element.63), channel_id=1, source_target_pairs={{0,8},{4,12},{8,0},{12,4},{16,24},{20,28},{24,16},{28,20},{1,9},{5... | collective-permute-start | bytes 36872 | tf_op jit(solution)/shard_map/ppermute | solution.py:597
  24.2 3.7 %collective-permute-start.8 = (bf16[2,24,128]{2,1,0:T(8,128)(2,1)S(1)}, bf16[2,24,128]{2,1,0:T(8,128)(2,1)S(1)}, u32[]{:S(2)}, u32[]{:S(2)}) collective-permute-start(bf16[2,24,128]{2,1,0:T(8,128)(2,1)S(1)} %get-tuple-element.64), channel_id=1, source_target_pairs={{0,16},{4,20},{8,24},{12,28},{16,0},{20,4},{24,8},{28,12},{1,17},{... | collective-permute-start | bytes 36872 | tf_op jit(solution)/shard_map/ppermute | solution.py:597
  24.7 4.6 %collective-permute-start.9 = (bf16[2,24,128]{2,1,0:T(8,128)(2,1)S(1)}, bf16[2,24,128]{2,1,0:T(8,128)(2,1)S(1)}, u32[]{:S(2)}, u32[]{:S(2)}) collective-permute-start(bf16[2,24,128]{2,1,0:T(8,128)(2,1)S(1)} %get-tuple-element.65), channel_id=1, source_target_pairs={{0,24},{4,28},{8,16},{12,20},{16,8},{20,12},{24,0},{28,4},{1,25},{... | collective-permute-start | bytes 36872 | tf_op jit(solution)/shard_map/ppermute | solution.py:597

commit v8 on v7

--- a/solution.py
+++ b/solution.py
@@ -270,7 +270,7 @@
     done = [0] * len(stages)
     while done[-1] < stages[-1][1]:
         before = list(done)
-        for k in reversed(range(len(stages))):
+        for k in range(len(stages)):
             run, count, beyond = stages[k]
             ready = count if k == 0 else min(count, before[k - 1] - beyond)
             size = ready - done[k] if ready == count else (ready - done[k]) // TILE * TILE
@@ -308,12 +308,10 @@
 
     if dm.split:
         half, early = dm.rows // 2, KROWS * dm.early
-        x_ref[:half] = keep_ref[...].reshape(half, dm.lw)
-        x_ref[half:] = got_ref[...].reshape(half, dm.lw)
-        sources = [x_ref[half + k * KROWS : half + (k + 1) * KROWS] for k in range(dm.early)]
+        halves = [ref[...].reshape(half, dm.lw) for ref in (keep_ref, got_ref)]
+        sources = [halves[1][k * KROWS : (k + 1) * KROWS] for k in range(dm.early)]
         if early < half:
-            rest = [keep_ref[...].reshape(half, dm.lw)[early:], got_ref[...].reshape(half, dm.lw)[early:]]
-            sources.append(jnp.concatenate(rest, axis=0))
+            sources.append(jnp.concatenate([x[early:] for x in halves], axis=0))
         at = 0
         for x in sources:
             lt_ref[:, at : at + x.shape[0]] = left_columns(dm, x)
@@ -409,9 +407,12 @@
         band = pltpu.roll(band, 3, 1, stride=1, stride_axis=0)
         bands += [band] * dm.lg
     band = jnp.concatenate(bands, axis=0)
-    sums = lax.dot_general(
-        x_ref[...], band.astype(bf), (((1,), (1,)), ((), ())), preferred_element_type=jnp.float32
-    )
+    band = band.astype(bf)
+    sums = [
+        lax.dot_general(x, band, (((1,), (1,)), ((), ())), preferred_element_type=jnp.float32)
+        for x in (halves if dm.split else [x_ref[...]])
+    ]
+    sums = jnp.concatenate(sums, axis=0)
     row = lax.broadcasted_iota(jnp.int32, (dm.rows, LANES), 0) % h
     warped = sums[:, :LANES]
     for k in range(1, h):

time: 30.3 us -> 30.3 us (level)
  no operation moved by 1% of the time
where the time goes in v8:
time: 30.3 us; the launch traced here: 30.1 us
  starting transfers between devices  10.9 us (36%)
  waiting for transfers between devices  10.4 us (34%)
  Pallas kernels  8.09 us (27%)
  between operations  0.71 us (2%)
    pallas_call x8, Pallas kernels, call(): pl.pallas_call(functools.partial(kernel, dm), out_shape=out_shape, in_spe...  8.09 us
    ppermute x2, waiting for transfers between devices, shards(): arrived.append(lax.ppermute(edges[first], 'col', pairs))  3.97 us
    ppermute x3, starting transfers between devices, shards(): windows.append(lax.ppermute(sent[m - 1], 'disp', pairs))  3.55 us
    ppermute x2, starting transfers between devices, shards(): arrived.append(lax.ppermute(edges[first], 'col', pairs))  3.55 us
    ppermute x3, starting transfers between devices, shards(): back.append(lax.ppermute(joined[m - 1], 'disp', pairs))  3.49 us
    ppermute x3, waiting for transfers between devices, shards(): windows.append(lax.ppermute(sent[m - 1], 'disp', pairs))  2.5 us
    ppermute x3, waiting for transfers between devices, shards(): back.append(lax.ppermute(joined[m - 1], 'disp', pairs))  2.15 us
    ppermute x1, waiting for transfers between devices, shards(): theirs = lax.ppermute(other, 'disp', [(i, i ^ 1) for i in range(n)])  1.05 us
  transfers between devices with their start and end apart: 10, of which 9 were waited for; matrix products, arithmetic and copies ran while one was open for 0% of the time, Pallas kernels for 9%

profile of v8, /device:TPU:16, one launch (start us, length us, event | category | flops | bytes accessed | tf_op | source)
XLA Modules:
  0.0 30.1 jit_solution(238759050209001275)
XLA Ops:
  0.6 0.9 %shard_map.77 = (bf16[80,256]{1,0:T(8,128)(2,1)S(1)}, bf16[80,256]{1,0:T(8,128)(2,1)S(1)}, bf16[80,256]{1,0:T(8,128)(2,1)S(1)}, bf16[80,256]{1,0:T(8,128)(2,1)S(1)}) custom-call(bf16[40,2,256]{2,1,0:T(2,128)(2,1)} %left_hbm.1, bf16[40,2,256]{2,1,0:T(2,128)(2,1)} %right_hbm.1), custom_call_target="tpu_custom_call" | custom-call | tf_op jit(solution)/shard_map/pallas_call | solution.py:496
  1.6 1.6 %collective-permute-start = (bf16[80,256]{1,0:T(8,128)(2,1)S(1)}, bf16[80,256]{1,0:T(8,128)(2,1)S(1)}, u32[]{:S(2)}, u32[]{:S(2)}) collective-permute-start(bf16[80,256]{1,0:T(8,128)(2,1)S(1)} %get-tuple-element.36), channel_id=1, source_target_pairs={{0,1},{2,3},{1,0},{3,2},{4,5},{6,7},{5,4},{7,6},{8,9},{10,11},{9,8... | collective-permute-start | bytes 122888 | tf_op jit(solution)/shard_map/ppermute | solution.py:522
  3.2 1.9 %collective-permute-start.1 = (bf16[80,256]{1,0:T(8,128)(2,1)S(1)}, bf16[80,256]{1,0:T(8,128)(2,1)S(1)}, u32[]{:S(2)}, u32[]{:S(2)}) collective-permute-start(bf16[80,256]{1,0:T(8,128)(2,1)S(1)} %get-tuple-element.37), channel_id=1, source_target_pairs={{1,2},{2,1},{5,6},{6,5},{9,10},{10,9},{13,14},{14,13},{17,18},{18,... | collective-permute-start | bytes 122888 | tf_op jit(solution)/shard_map/ppermute | solution.py:522
  5.1 0.5 %collective-permute-done.pair0_ref = bf16[80,256]{1,0:T(8,128)(2,1)S(1)} collective-permute-done((bf16[80,256]{1,0:T(8,128)(2,1)S(1)}, bf16[80,256]{1,0:T(8,128)(2,1)S(1)}, u32[]{:S(2)}, u32[]{:S(2)}) %collective-permute-start) | collective-permute-done | bytes 40992 | tf_op jit(solution)/shard_map/ppermute | solution.py:522
  5.6 3.5 %collective-permute-done.1.pair1_ref = bf16[80,256]{1,0:T(8,128)(2,1)S(1)} collective-permute-done((bf16[80,256]{1,0:T(8,128)(2,1)S(1)}, bf16[80,256]{1,0:T(8,128)(2,1)S(1)}, u32[]{:S(2)}, u32[]{:S(2)}) %collective-permute-start.1) | collective-permute-done | bytes 40992 | tf_op jit(solution)/shard_map/ppermute | solution.py:522
  9.1 0.2 shard_map.78
  9.4 1.6 %collective-permute-start.2 = (bf16[80,384]{1,0:T(8,128)(2,1)S(1)}, bf16[80,384]{1,0:T(8,128)(2,1)S(1)}, u32[]{:S(2)}, u32[]{:S(2)}) collective-permute-start(bf16[80,384]{1,0:T(8,128)(2,1)S(1)} %get-tuple-element.41), channel_id=1, source_target_pairs={{0,8},{4,12},{8,0},{12,4},{16,24},{20,28},{24,16},{28,20},{1,9},{5... | collective-permute-start | bytes 184328 | tf_op jit(solution)/shard_map/ppermute | solution.py:549
  10.9 1.5 %collective-permute-start.3 = (bf16[80,384]{1,0:T(8,128)(2,1)S(1)}, bf16[80,384]{1,0:T(8,128)(2,1)S(1)}, u32[]{:S(2)}, u32[]{:S(2)}) collective-permute-start(bf16[80,384]{1,0:T(8,128)(2,1)S(1)} %get-tuple-element.42), channel_id=1, source_target_pairs={{0,16},{4,20},{8,24},{12,28},{16,0},{20,4},{24,8},{28,12},{1,17},{... | collective-permute-start | bytes 184328 | tf_op jit(solution)/shard_map/ppermute | solution.py:549
  12.4 0.5 %collective-permute-start.4 = (bf16[80,384]{1,0:T(8,128)(2,1)S(1)}, bf16[80,384]{1,0:T(8,128)(2,1)S(1)}, u32[]{:S(2)}, u32[]{:S(2)}) collective-permute-start(bf16[80,384]{1,0:T(8,128)(2,1)S(1)} %get-tuple-element.43), channel_id=1, source_target_pairs={{0,24},{4,28},{8,16},{12,20},{16,8},{20,12},{24,0},{28,4},{1,25},{... | collective-permute-start | bytes 184328 | tf_op jit(solution)/shard_map/ppermute | solution.py:549
  12.9 2.1 %shard_map.79 = (bf16[192,240]{1,0:T(8,128)(2,1)S(1)}, bf16[192,192]{1,0:T(8,128)(2,1)S(1)}, bf16[192,192]{1,0:T(8,128)(2,1)S(1)}, f32[64,128]{1,0:T(8,128)S(1)}) custom-call(bf16[27,32,40]{2,1,0:T(8,128)(2,1)} %bitcast.10, bf16[27,32,32]{2,1,0:T(8,128)(2,1)} %bitcast.11, bf16[27,32,32]{2,1,0:T(8,128)(2,1)} %bitcast.12, f32[1,32]{1,0:T(1,128)} %bitcast.13), custom_call_target="tpu_custom_call" | custom-call | tf_op jit(solution)/shard_map/pallas_call | solution.py:496
  15.1 0.3 %collective-permute-done.3.refs_2_ = bf16[80,384]{1,0:T(8,128)(2,1)S(1)} collective-permute-done((bf16[80,384]{1,0:T(8,128)(2,1)S(1)}, bf16[80,384]{1,0:T(8,128)(2,1)S(1)}, u32[]{:S(2)}, u32[]{:S(2)}) %collective-permute-start.3) | collective-permute-done | bytes 61472 | tf_op jit(solution)/shard_map/ppermute | solution.py:549
  15.4 2.2 %collective-permute-done.4.refs_3_ = bf16[80,384]{1,0:T(8,128)(2,1)S(1)} collective-permute-done((bf16[80,384]{1,0:T(8,128)(2,1)S(1)}, bf16[80,384]{1,0:T(8,128)(2,1)S(1)}, u32[]{:S(2)}, u32[]{:S(2)}) %collective-permute-start.4) | collective-permute-done | bytes 61472 | tf_op jit(solution)/shard_map/ppermute | solution.py:549
  17.8 0.6 %shard_map.81.refs_0_ = bf16[3,32,4864]{2,1,0:T(8,128)(2,1)S(1)} custom-call(bf16[4,80,256]{2,1,0:T(8,128)(2,1)S(1)} %get-tuple-element.55.keep_ref), custom_call_target="tpu_custom_call" | custom-call | tf_op jit(solution)/shard_map/pallas_call | solution.py:496
  18.5 0.7 %collective-permute-done.5.got_ref = bf16[4,80,256]{2,1,0:T(8,128)(2,1)S(1)} collective-permute-done((bf16[4,80,256]{2,1,0:T(8,128)(2,1)S(1)}, bf16[4,80,256]{2,1,0:T(8,128)(2,1)S(1)}, u32[]{:S(2)}, u32[]{:S(2)}) %collective-permute-start.5) | collective-permute-done | bytes 163872 | tf_op jit(solution)/shard_map/ppermute | solution.py:553
  19.2 3.2 %shard_map.82 = (bf16[4,24,128]{2,1,0:T(8,128)(2,1)S(1)}, bf16[4,24,128]{2,1,0:T(8,128)(2,1)S(1)}) custom-call(bf16[4,80,256]{2,1,0:T(8,128)(2,1)S(1)} %get-tuple-element.55.keep_ref, bf16[4,80,256]{2,1,0:T(8,128)(2,1)S(1)} %collective-permute-done.5.got_ref, bf16[3,32,4864]{2,1,0:T(8,128)(2,1)S(1)} %shard_map.81.refs_0_, ...), custom_call_target="tpu_custom_call" | custom-call | tf_op jit(solution)/shard_map/pallas_call | solution.py:496
  22.4 0.2 collective-permute-start.6
  22.6 1.0 %collective-permute-done.6.theirs_ref = bf16[4,24,128]{2,1,0:T(8,128)(2,1)S(1)} collective-permute-done((bf16[4,24,128]{2,1,0:T(8,128)(2,1)S(1)}, bf16[4,24,128]{2,1,0:T(8,128)(2,1)S(1)}, u32[]{:S(2)}, u32[]{:S(2)}) %collective-permute-start.6) | collective-permute-done | bytes 24608 | tf_op jit(solution)/shard_map/ppermute | solution.py:589
  23.6 0.5 %collective-permute-start.7 = (bf16[2,24,128]{2,1,0:T(8,128)(2,1)S(1)}, bf16[2,24,128]{2,1,0:T(8,128)(2,1)S(1)}, u32[]{:S(2)}, u32[]{:S(2)}) collective-permute-start(bf16[2,24,128]{2,1,0:T(8,128)(2,1)S(1)} %get-tuple-element.63), channel_id=1, source_target_pairs={{0,8},{4,12},{8,0},{12,4},{16,24},{20,28},{24,16},{28,20},{1,9},{5... | collective-permute-start | bytes 36872 | tf_op jit(solution)/shard_map/ppermute | solution.py:598
  24.2 0.5 %collective-permute-start.8 = (bf16[2,24,128]{2,1,0:T(8,128)(2,1)S(1)}, bf16[2,24,128]{2,1,0:T(8,128)(2,1)S(1)}, u32[]{:S(2)}, u32[]{:S(2)}) collective-permute-start(bf16[2,24,128]{2,1,0:T(8,128)(2,1)S(1)} %get-tuple-element.64), channel_id=1, source_target_pairs={{0,16},{4,20},{8,24},{12,28},{16,0},{20,4},{24,8},{28,12},{1,17},{... | collective-permute-start | bytes 36872 | tf_op jit(solution)/shard_map/ppermute | solution.py:598
  24.7 2.4 %collective-permute-start.9 = (bf16[2,24,128]{2,1,0:T(8,128)(2,1)S(1)}, bf16[2,24,128]{2,1,0:T(8,128)(2,1)S(1)}, u32[]{:S(2)}, u32[]{:S(2)}) collective-permute-start(bf16[2,24,128]{2,1,0:T(8,128)(2,1)S(1)} %get-tuple-element.65), channel_id=1, source_target_pairs={{0,24},{4,28},{8,16},{12,20},{16,8},{20,12},{24,0},{28,4},{1,25},{... | collective-permute-start | bytes 36872 | tf_op jit(solution)/shard_map/ppermute | solution.py:598
  27.1 0.2 collective-permute-done.7.refs_0_
  27.3 0.5 %collective-permute-done.8.refs_1_ = bf16[2,24,128]{2,1,0:T(8,128)(2,1)S(1)} collective-permute-done((bf16[2,24,128]{2,1,0:T(8,128)(2,1)S(1)}, bf16[2,24,128]{2,1,0:T(8,128)(2,1)S(1)}, u32[]{:S(2)}, u32[]{:S(2)}) %collective-permute-start.8) | collective-permute-done | bytes 12320 | tf_op jit(solution)/shard_map/ppermute | solution.py:598
  27.9 1.4 %collective-permute-done.9.refs_2_ = bf16[2,24,128]{2,1,0:T(8,128)(2,1)S(1)} collective-permute-done((bf16[2,24,128]{2,1,0:T(8,128)(2,1)S(1)}, bf16[2,24,128]{2,1,0:T(8,128)(2,1)S(1)}, u32[]{:S(2)}, u32[]{:S(2)}) %collective-permute-start.9) | collective-permute-done | bytes 12320 | tf_op jit(solution)/shard_map/ppermute | solution.py:598
  29.3 0.8 %shard_map.84 = (bf16[40,2,256]{2,1,0:T(2,128)(2,1)}, f32[2,256]{1,0:T(2,128)}) custom-call(bf16[4,24,128]{2,1,0:T(8,128)(2,1)S(1)} %get-tuple-element.61.same_ref, bf16[4,24,128]{2,1,0:T(8,128)(2,1)S(1)} %collective-permute-done.6.theirs_ref, bf16[2,24,128]{2,1,0:T(8,128)(2,1)S(1)} %collective-permute-done.7.refs_0_, ...), custom_call_target="tpu_custom_call" | custom-call | tf_op jit(solution)/shard_map/pallas_call | solution.py:496
  (4 shorter events, 0.3 us)
Async XLA Ops:
  1.6 4.1 %collective-permute-start = (bf16[80,256]{1,0:T(8,128)(2,1)S(1)}, bf16[80,256]{1,0:T(8,128)(2,1)S(1)}, u32[]{:S(2)}, u32[]{:S(2)}) collective-permute-start(bf16[80,256]{1,0:T(8,128)(2,1)S(1)} %get-tuple-element.36), channel_id=1, source_target_pairs={{0,1},{2,3},{1,0},{3,2},{4,5},{6,7},{5,4},{7,6},{8,9},{10,11},{9,8... | collective-permute-start | bytes 122888 | tf_op jit(solution)/shard_map/ppermute | solution.py:522
  3.2 5.9 %collective-permute-start.1 = (bf16[80,256]{1,0:T(8,128)(2,1)S(1)}, bf16[80,256]{1,0:T(8,128)(2,1)S(1)}, u32[]{:S(2)}, u32[]{:S(2)}) collective-permute-start(bf16[80,256]{1,0:T(8,128)(2,1)S(1)} %get-tuple-element.37), channel_id=1, source_target_pairs={{1,2},{2,1},{5,6},{6,5},{9,10},{10,9},{13,14},{14,13},{17,18},{18,... | collective-permute-start | bytes 122888 | tf_op jit(solution)/shard_map/ppermute | solution.py:522
  9.4 5.7 %collective-permute-start.2 = (bf16[80,384]{1,0:T(8,128)(2,1)S(1)}, bf16[80,384]{1,0:T(8,128)(2,1)S(1)}, u32[]{:S(2)}, u32[]{:S(2)}) collective-permute-start(bf16[80,384]{1,0:T(8,128)(2,1)S(1)} %get-tuple-element.41), channel_id=1, source_target_pairs={{0,8},{4,12},{8,0},{12,4},{16,24},{20,28},{24,16},{28,20},{1,9},{5... | collective-permute-start | bytes 184328 | tf_op jit(solution)/shard_map/ppermute | solution.py:549
  10.9 4.4 %collective-permute-start.3 = (bf16[80,384]{1,0:T(8,128)(2,1)S(1)}, bf16[80,384]{1,0:T(8,128)(2,1)S(1)}, u32[]{:S(2)}, u32[]{:S(2)}) collective-permute-start(bf16[80,384]{1,0:T(8,128)(2,1)S(1)} %get-tuple-element.42), channel_id=1, source_target_pairs={{0,16},{4,20},{8,24},{12,28},{16,0},{20,4},{24,8},{28,12},{1,17},{... | collective-permute-start | bytes 184328 | tf_op jit(solution)/shard_map/ppermute | solution.py:549
  12.4 5.1 %collective-permute-start.4 = (bf16[80,384]{1,0:T(8,128)(2,1)S(1)}, bf16[80,384]{1,0:T(8,128)(2,1)S(1)}, u32[]{:S(2)}, u32[]{:S(2)}) collective-permute-start(bf16[80,384]{1,0:T(8,128)(2,1)S(1)} %get-tuple-element.43), channel_id=1, source_target_pairs={{0,24},{4,28},{8,16},{12,20},{16,8},{20,12},{24,0},{28,4},{1,25},{... | collective-permute-start | bytes 184328 | tf_op jit(solution)/shard_map/ppermute | solution.py:549
  17.8 1.5 %collective-permute-start.5 = (bf16[4,80,256]{2,1,0:T(8,128)(2,1)S(1)}, bf16[4,80,256]{2,1,0:T(8,128)(2,1)S(1)}, u32[]{:S(2)}, u32[]{:S(2)}) collective-permute-start(bf16[4,80,256]{2,1,0:T(8,128)(2,1)S(1)} %get-tuple-element.56), channel_id=1, source_target_pairs={{0,4},{4,0},{8,12},{12,8},{16,20},{20,16},{24,28},{28,24},{1,5},{5... | collective-permute-start | bytes 491528 | tf_op jit(solution)/shard_map/ppermute | solution.py:553
  22.4 1.3 %collective-permute-start.6 = (bf16[4,24,128]{2,1,0:T(8,128)(2,1)S(1)}, bf16[4,24,128]{2,1,0:T(8,128)(2,1)S(1)}, u32[]{:S(2)}, u32[]{:S(2)}) collective-permute-start(bf16[4,24,128]{2,1,0:T(8,128)(2,1)S(1)} %get-tuple-element.62), channel_id=1, source_target_pairs={{0,4},{4,0},{8,12},{12,8},{16,20},{20,16},{24,28},{28,24},{1,5},{5... | collective-permute-start | bytes 73736 | tf_op jit(solution)/shard_map/ppermute | solution.py:589
  23.6 3.7 %collective-permute-start.7 = (bf16[2,24,128]{2,1,0:T(8,128)(2,1)S(1)}, bf16[2,24,128]{2,1,0:T(8,128)(2,1)S(1)}, u32[]{:S(2)}, u32[]{:S(2)}) collective-permute-start(bf16[2,24,128]{2,1,0:T(8,128)(2,1)S(1)} %get-tuple-element.63), channel_id=1, source_target_pairs={{0,8},{4,12},{8,0},{12,4},{16,24},{20,28},{24,16},{28,20},{1,9},{5... | collective-permute-start | bytes 36872 | tf_op jit(solution)/shard_map/ppermute | solution.py:598
  24.2 3.7 %collective-permute-start.8 = (bf16[2,24,128]{2,1,0:T(8,128)(2,1)S(1)}, bf16[2,24,128]{2,1,0:T(8,128)(2,1)S(1)}, u32[]{:S(2)}, u32[]{:S(2)}) collective-permute-start(bf16[2,24,128]{2,1,0:T(8,128)(2,1)S(1)} %get-tuple-element.64), channel_id=1, source_target_pairs={{0,16},{4,20},{8,24},{12,28},{16,0},{20,4},{24,8},{28,12},{1,17},{... | collective-permute-start | bytes 36872 | tf_op jit(solution)/shard_map/ppermute | solution.py:598
  24.7 4.6 %collective-permute-start.9 = (bf16[2,24,128]{2,1,0:T(8,128)(2,1)S(1)}, bf16[2,24,128]{2,1,0:T(8,128)(2,1)S(1)}, u32[]{:S(2)}, u32[]{:S(2)}) collective-permute-start(bf16[2,24,128]{2,1,0:T(8,128)(2,1)S(1)} %get-tuple-element.65), channel_id=1, source_target_pairs={{0,24},{4,28},{8,16},{12,20},{16,8},{20,12},{24,0},{28,4},{1,25},{... | collective-permute-start | bytes 36872 | tf_op jit(solution)/shard_map/ppermute | solution.py:598

commit v9 on v8

--- a/solution.py
+++ b/solution.py
@@ -94,12 +94,10 @@
 
 
 def edge_kernel(dm, left_hbm, right_hbm, *refs):
-    *outs, flat_left_ref, flat_right_ref, left_ref, right_ref, sems = refs
+    *outs, left_ref, right_ref, sems = refs
     for wait in copied_in((left_hbm, right_hbm), (left_ref, right_ref), sems):
         wait()
     left, right = flat(left_ref), flat(right_ref)
-    flat_left_ref[...] = left.astype(flat_left_ref.dtype)
-    flat_right_ref[...] = right.astype(flat_right_ref.dtype)
     width = outs[0].shape[1]
     count = dm.hops[0]
     lane = lane_iota((dm.own_rows, width))
@@ -112,6 +110,14 @@
     outs[1][...] = jnp.where(even, down, up).astype(outs[1].dtype)
     for out, count in zip(outs[2:], dm.hops[1:]):
         out[...] = rolled(right, count - dm.strip)[:, : out.shape[1]].astype(out.dtype)
+
+
+def flat_kernel(dm, left_hbm, right_hbm, *refs):
+    *outs, left_ref, right_ref, sems = refs
+    sources = (left_ref, right_ref)
+    for wait, out, ref in zip(copied_in((left_hbm, right_hbm), sources, sems), outs, sources):
+        wait()
+        out[...] = flat(ref).astype(out.dtype)
 
 
 def pack_kernel(dm, left_ref, right_ref, pair0_ref, pair1_ref, *refs):
@@ -504,17 +510,16 @@
 
     wide = max(round_up(dm.hops[0] + 3, LANES), dm.strip)
     widths = [wide, wide] + [round_up(c, LANES) for c in dm.hops[1:]]
-    *edges, left, right = call(
-        edge_kernel,
-        [jax.ShapeDtypeStruct((dm.own_rows, w), bf) for w in widths + [dm.strip] * 2],
-        [left_feat, right_feat],
-        in_hbm=True,
-        scratch_shapes=[
-            pltpu.VMEM(left_feat.shape, bf),
-            pltpu.VMEM(left_feat.shape, bf),
-            pltpu.SemaphoreType.DMA((2,)),
-        ],
-    )
+    landing = [
+        pltpu.VMEM(left_feat.shape, bf),
+        pltpu.VMEM(left_feat.shape, bf),
+        pltpu.SemaphoreType.DMA((2,)),
+    ]
+    features = [left_feat, right_feat]
+    shapes = [jax.ShapeDtypeStruct((dm.own_rows, w), bf) for w in widths]
+    edges = call(edge_kernel, shapes, features, in_hbm=True, scratch_shapes=landing)
+    shapes = [jax.ShapeDtypeStruct((dm.own_rows, dm.strip), bf)] * 2
+    left, right = call(flat_kernel, shapes, features, in_hbm=True, scratch_shapes=landing)
     arrived = []
     for first in range(2):
         pairs = [(s, s + 1) for s in range(first, strips - 1, 2)]

time: 30.3 us -> 30.3 us (level)
  waiting for transfers between devices: 10.4 us -> 9.54 us
  Pallas kernels: 8.09 us -> 8.93 us
    ppermute x2, waiting for transfers between devices: 3.97 us -> 3.11 us  [shards(): arrived.append(lax.ppermute(edges[first], 'col', pairs))]
    pallas_call x8 -> x9, Pallas kernels: 8.09 us -> 8.93 us  [call(): pl.pallas_call(functools.partial(kernel, dm), out_shape=out_shape, in_spe...]
  transfers between devices with their start and end apart: 10 -> 10, of which waited for: 9 -> 8; matrix products, arithmetic and copies ran while one was open for 0% -> 0% of each run, Pallas kernels for 9% -> 12%
where the time goes in v9:
time: 30.3 us; the launch traced here: 30.1 us
  starting transfers between devices  10.9 us (36%)
  waiting for transfers between devices  9.54 us (31%)
  Pallas kernels  8.93 us (29%)
  between operations  0.72 us (2%)
    pallas_call x9, Pallas kernels, call(): pl.pallas_call(functools.partial(kernel, dm), out_shape=out_shape, in_spe...  8.93 us
    ppermute x3, starting transfers between devices, shards(): windows.append(lax.ppermute(sent[m - 1], 'disp', pairs))  3.55 us
    ppermute x2, starting transfers between devices, shards(): arrived.append(lax.ppermute(edges[first], 'col', pairs))  3.55 us
    ppermute x3, starting transfers between devices, shards(): back.append(lax.ppermute(joined[m - 1], 'disp', pairs))  3.49 us
    ppermute x2, waiting for transfers between devices, shards(): arrived.append(lax.ppermute(edges[first], 'col', pairs))  3.11 us
    ppermute x3, waiting for transfers between devices, shards(): windows.append(lax.ppermute(sent[m - 1], 'disp', pairs))  2.5 us
    ppermute x3, waiting for transfers between devices, shards(): back.append(lax.ppermute(joined[m - 1], 'disp', pairs))  2.14 us
    ppermute x1, waiting for transfers between devices, shards(): theirs = lax.ppermute(other, 'disp', [(i, i ^ 1) for i in range(n)])  1.05 us
  transfers between devices with their start and end apart: 10, of which 8 were waited for; matrix products, arithmetic and copies ran while one was open for 0% of the time, Pallas kernels for 12%

profile of v9, /device:TPU:16, one launch (start us, length us, event | category | flops | bytes accessed | tf_op | source)
XLA Modules:
  0.0 30.1 jit_solution(18040350459359710617)
XLA Ops:
  0.6 0.9 %shard_map.78 = (bf16[80,256]{1,0:T(8,128)(2,1)S(1)}, bf16[80,256]{1,0:T(8,128)(2,1)S(1)}) custom-call(bf16[40,2,256]{2,1,0:T(2,128)(2,1)} %left_hbm.3, bf16[40,2,256]{2,1,0:T(2,128)(2,1)} %right_hbm.3), custom_call_target="tpu_custom_call" | custom-call | tf_op jit(solution)/shard_map/pallas_call | solution.py:502
  1.6 1.6 %collective-permute-start = (bf16[80,256]{1,0:T(8,128)(2,1)S(1)}, bf16[80,256]{1,0:T(8,128)(2,1)S(1)}, u32[]{:S(2)}, u32[]{:S(2)}) collective-permute-start(bf16[80,256]{1,0:T(8,128)(2,1)S(1)} %get-tuple-element.36), channel_id=1, source_target_pairs={{0,1},{2,3},{1,0},{3,2},{4,5},{6,7},{5,4},{7,6},{8,9},{10,11},{9,8... | collective-permute-start | bytes 122888 | tf_op jit(solution)/shard_map/ppermute | solution.py:527
  3.2 1.9 %collective-permute-start.1 = (bf16[80,256]{1,0:T(8,128)(2,1)S(1)}, bf16[80,256]{1,0:T(8,128)(2,1)S(1)}, u32[]{:S(2)}, u32[]{:S(2)}) collective-permute-start(bf16[80,256]{1,0:T(8,128)(2,1)S(1)} %get-tuple-element.37), channel_id=1, source_target_pairs={{1,2},{2,1},{5,6},{6,5},{9,10},{10,9},{13,14},{14,13},{17,18},{18,... | collective-permute-start | bytes 122888 | tf_op jit(solution)/shard_map/ppermute | solution.py:527
  5.1 0.8 %shard_map.77 = (bf16[80,256]{1,0:T(8,128)(2,1)S(1)}, bf16[80,256]{1,0:T(8,128)(2,1)S(1)}) custom-call(bf16[40,2,256]{2,1,0:T(2,128)(2,1)} %left_hbm.3, bf16[40,2,256]{2,1,0:T(2,128)(2,1)} %right_hbm.3), custom_call_target="tpu_custom_call" | custom-call | tf_op jit(solution)/shard_map/pallas_call | solution.py:502
  6.0 3.1 %collective-permute-done.1.pair1_ref = bf16[80,256]{1,0:T(8,128)(2,1)S(1)} collective-permute-done((bf16[80,256]{1,0:T(8,128)(2,1)S(1)}, bf16[80,256]{1,0:T(8,128)(2,1)S(1)}, u32[]{:S(2)}, u32[]{:S(2)}) %collective-permute-start.1) | collective-permute-done | bytes 40992 | tf_op jit(solution)/shard_map/ppermute | solution.py:527
  9.1 0.2 shard_map.79
  9.4 1.6 %collective-permute-start.2 = (bf16[80,384]{1,0:T(8,128)(2,1)S(1)}, bf16[80,384]{1,0:T(8,128)(2,1)S(1)}, u32[]{:S(2)}, u32[]{:S(2)}) collective-permute-start(bf16[80,384]{1,0:T(8,128)(2,1)S(1)} %get-tuple-element.41), channel_id=1, source_target_pairs={{0,8},{4,12},{8,0},{12,4},{16,24},{20,28},{24,16},{28,20},{1,9},{5... | collective-permute-start | bytes 184328 | tf_op jit(solution)/shard_map/ppermute | solution.py:554
  10.9 1.5 %collective-permute-start.3 = (bf16[80,384]{1,0:T(8,128)(2,1)S(1)}, bf16[80,384]{1,0:T(8,128)(2,1)S(1)}, u32[]{:S(2)}, u32[]{:S(2)}) collective-permute-start(bf16[80,384]{1,0:T(8,128)(2,1)S(1)} %get-tuple-element.42), channel_id=1, source_target_pairs={{0,16},{4,20},{8,24},{12,28},{16,0},{20,4},{24,8},{28,12},{1,17},{... | collective-permute-start | bytes 184328 | tf_op jit(solution)/shard_map/ppermute | solution.py:554
  12.4 0.5 %collective-permute-start.4 = (bf16[80,384]{1,0:T(8,128)(2,1)S(1)}, bf16[80,384]{1,0:T(8,128)(2,1)S(1)}, u32[]{:S(2)}, u32[]{:S(2)}) collective-permute-start(bf16[80,384]{1,0:T(8,128)(2,1)S(1)} %get-tuple-element.43), channel_id=1, source_target_pairs={{0,24},{4,28},{8,16},{12,20},{16,8},{20,12},{24,0},{28,4},{1,25},{... | collective-permute-start | bytes 184328 | tf_op jit(solution)/shard_map/ppermute | solution.py:554
  12.9 2.1 %shard_map.80 = (bf16[192,240]{1,0:T(8,128)(2,1)S(1)}, bf16[192,192]{1,0:T(8,128)(2,1)S(1)}, bf16[192,192]{1,0:T(8,128)(2,1)S(1)}, f32[64,128]{1,0:T(8,128)S(1)}) custom-call(bf16[27,32,40]{2,1,0:T(8,128)(2,1)} %bitcast.10, bf16[27,32,32]{2,1,0:T(8,128)(2,1)} %bitcast.11, bf16[27,32,32]{2,1,0:T(8,128)(2,1)} %bitcast.12, f32[1,32]{1,0:T(1,128)} %bitcast.13), custom_call_target="tpu_custom_call" | custom-call | tf_op jit(solution)/shard_map/pallas_call | solution.py:502
  15.1 0.3 %collective-permute-done.3.refs_2_ = bf16[80,384]{1,0:T(8,128)(2,1)S(1)} collective-permute-done((bf16[80,384]{1,0:T(8,128)(2,1)S(1)}, bf16[80,384]{1,0:T(8,128)(2,1)S(1)}, u32[]{:S(2)}, u32[]{:S(2)}) %collective-permute-start.3) | collective-permute-done | bytes 61472 | tf_op jit(solution)/shard_map/ppermute | solution.py:554
  15.4 2.2 %collective-permute-done.4.refs_3_ = bf16[80,384]{1,0:T(8,128)(2,1)S(1)} collective-permute-done((bf16[80,384]{1,0:T(8,128)(2,1)S(1)}, bf16[80,384]{1,0:T(8,128)(2,1)S(1)}, u32[]{:S(2)}, u32[]{:S(2)}) %collective-permute-start.4) | collective-permute-done | bytes 61472 | tf_op jit(solution)/shard_map/ppermute | solution.py:554
  17.8 0.6 %shard_map.82.refs_0_ = bf16[3,32,4864]{2,1,0:T(8,128)(2,1)S(1)} custom-call(bf16[4,80,256]{2,1,0:T(8,128)(2,1)S(1)} %get-tuple-element.55.keep_ref), custom_call_target="tpu_custom_call" | custom-call | tf_op jit(solution)/shard_map/pallas_call | solution.py:502
  18.5 0.7 %collective-permute-done.5.got_ref = bf16[4,80,256]{2,1,0:T(8,128)(2,1)S(1)} collective-permute-done((bf16[4,80,256]{2,1,0:T(8,128)(2,1)S(1)}, bf16[4,80,256]{2,1,0:T(8,128)(2,1)S(1)}, u32[]{:S(2)}, u32[]{:S(2)}) %collective-permute-start.5) | collective-permute-done | bytes 163872 | tf_op jit(solution)/shard_map/ppermute | solution.py:558
  19.2 3.2 %shard_map.83 = (bf16[4,24,128]{2,1,0:T(8,128)(2,1)S(1)}, bf16[4,24,128]{2,1,0:T(8,128)(2,1)S(1)}) custom-call(bf16[4,80,256]{2,1,0:T(8,128)(2,1)S(1)} %get-tuple-element.55.keep_ref, bf16[4,80,256]{2,1,0:T(8,128)(2,1)S(1)} %collective-permute-done.5.got_ref, bf16[3,32,4864]{2,1,0:T(8,128)(2,1)S(1)} %shard_map.82.refs_0_, ...), custom_call_target="tpu_custom_call" | custom-call | tf_op jit(solution)/shard_map/pallas_call | solution.py:502
  22.4 0.2 collective-permute-start.6
  22.6 1.0 %collective-permute-done.6.theirs_ref = bf16[4,24,128]{2,1,0:T(8,128)(2,1)S(1)} collective-permute-done((bf16[4,24,128]{2,1,0:T(8,128)(2,1)S(1)}, bf16[4,24,128]{2,1,0:T(8,128)(2,1)S(1)}, u32[]{:S(2)}, u32[]{:S(2)}) %collective-permute-start.6) | collective-permute-done | bytes 24608 | tf_op jit(solution)/shard_map/ppermute | solution.py:594
  23.6 0.5 %collective-permute-start.7 = (bf16[2,24,128]{2,1,0:T(8,128)(2,1)S(1)}, bf16[2,24,128]{2,1,0:T(8,128)(2,1)S(1)}, u32[]{:S(2)}, u32[]{:S(2)}) collective-permute-start(bf16[2,24,128]{2,1,0:T(8,128)(2,1)S(1)} %get-tuple-element.63), channel_id=1, source_target_pairs={{0,8},{4,12},{8,0},{12,4},{16,24},{20,28},{24,16},{28,20},{1,9},{5... | collective-permute-start | bytes 36872 | tf_op jit(solution)/shard_map/ppermute | solution.py:603
  24.2 0.5 %collective-permute-start.8 = (bf16[2,24,128]{2,1,0:T(8,128)(2,1)S(1)}, bf16[2,24,128]{2,1,0:T(8,128)(2,1)S(1)}, u32[]{:S(2)}, u32[]{:S(2)}) collective-permute-start(bf16[2,24,128]{2,1,0:T(8,128)(2,1)S(1)} %get-tuple-element.64), channel_id=1, source_target_pairs={{0,16},{4,20},{8,24},{12,28},{16,0},{20,4},{24,8},{28,12},{1,17},{... | collective-permute-start | bytes 36872 | tf_op jit(solution)/shard_map/ppermute | solution.py:603
  24.7 2.5 %collective-permute-start.9 = (bf16[2,24,128]{2,1,0:T(8,128)(2,1)S(1)}, bf16[2,24,128]{2,1,0:T(8,128)(2,1)S(1)}, u32[]{:S(2)}, u32[]{:S(2)}) collective-permute-start(bf16[2,24,128]{2,1,0:T(8,128)(2,1)S(1)} %get-tuple-element.65), channel_id=1, source_target_pairs={{0,24},{4,28},{8,16},{12,20},{16,8},{20,12},{24,0},{28,4},{1,25},{... | collective-permute-start | bytes 36872 | tf_op jit(solution)/shard_map/ppermute | solution.py:603
  27.1 0.2 collective-permute-done.7.refs_0_
  27.3 0.5 %collective-permute-done.8.refs_1_ = bf16[2,24,128]{2,1,0:T(8,128)(2,1)S(1)} collective-permute-done((bf16[2,24,128]{2,1,0:T(8,128)(2,1)S(1)}, bf16[2,24,128]{2,1,0:T(8,128)(2,1)S(1)}, u32[]{:S(2)}, u32[]{:S(2)}) %collective-permute-start.8) | collective-permute-done | bytes 12320 | tf_op jit(solution)/shard_map/ppermute | solution.py:603
  27.9 1.4 %collective-permute-done.9.refs_2_ = bf16[2,24,128]{2,1,0:T(8,128)(2,1)S(1)} collective-permute-done((bf16[2,24,128]{2,1,0:T(8,128)(2,1)S(1)}, bf16[2,24,128]{2,1,0:T(8,128)(2,1)S(1)}, u32[]{:S(2)}, u32[]{:S(2)}) %collective-permute-start.9) | collective-permute-done | bytes 12320 | tf_op jit(solution)/shard_map/ppermute | solution.py:603
  29.3 0.8 %shard_map.85 = (bf16[40,2,256]{2,1,0:T(2,128)(2,1)}, f32[2,256]{1,0:T(2,128)}) custom-call(bf16[4,24,128]{2,1,0:T(8,128)(2,1)S(1)} %get-tuple-element.61.same_ref, bf16[4,24,128]{2,1,0:T(8,128)(2,1)S(1)} %collective-permute-done.6.theirs_ref, bf16[2,24,128]{2,1,0:T(8,128)(2,1)S(1)} %collective-permute-done.7.refs_0_, ...), custom_call_target="tpu_custom_call" | custom-call | tf_op jit(solution)/shard_map/pallas_call | solution.py:502
  (5 shorter events, 0.3 us)
Async XLA Ops:
  1.6 4.4 %collective-permute-start = (bf16[80,256]{1,0:T(8,128)(2,1)S(1)}, bf16[80,256]{1,0:T(8,128)(2,1)S(1)}, u32[]{:S(2)}, u32[]{:S(2)}) collective-permute-start(bf16[80,256]{1,0:T(8,128)(2,1)S(1)} %get-tuple-element.36), channel_id=1, source_target_pairs={{0,1},{2,3},{1,0},{3,2},{4,5},{6,7},{5,4},{7,6},{8,9},{10,11},{9,8... | collective-permute-start | bytes 122888 | tf_op jit(solution)/shard_map/ppermute | solution.py:527
  3.2 5.9 %collective-permute-start.1 = (bf16[80,256]{1,0:T(8,128)(2,1)S(1)}, bf16[80,256]{1,0:T(8,128)(2,1)S(1)}, u32[]{:S(2)}, u32[]{:S(2)}) collective-permute-start(bf16[80,256]{1,0:T(8,128)(2,1)S(1)} %get-tuple-element.37), channel_id=1, source_target_pairs={{1,2},{2,1},{5,6},{6,5},{9,10},{10,9},{13,14},{14,13},{17,18},{18,... | collective-permute-start | bytes 122888 | tf_op jit(solution)/shard_map/ppermute | solution.py:527
  9.4 5.7 %collective-permute-start.2 = (bf16[80,384]{1,0:T(8,128)(2,1)S(1)}, bf16[80,384]{1,0:T(8,128)(2,1)S(1)}, u32[]{:S(2)}, u32[]{:S(2)}) collective-permute-start(bf16[80,384]{1,0:T(8,128)(2,1)S(1)} %get-tuple-element.41), channel_id=1, source_target_pairs={{0,8},{4,12},{8,0},{12,4},{16,24},{20,28},{24,16},{28,20},{1,9},{5... | collective-permute-start | bytes 184328 | tf_op jit(solution)/shard_map/ppermute | solution.py:554
  10.9 4.4 %collective-permute-start.3 = (bf16[80,384]{1,0:T(8,128)(2,1)S(1)}, bf16[80,384]{1,0:T(8,128)(2,1)S(1)}, u32[]{:S(2)}, u32[]{:S(2)}) collective-permute-start(bf16[80,384]{1,0:T(8,128)(2,1)S(1)} %get-tuple-element.42), channel_id=1, source_target_pairs={{0,16},{4,20},{8,24},{12,28},{16,0},{20,4},{24,8},{28,12},{1,17},{... | collective-permute-start | bytes 184328 | tf_op jit(solution)/shard_map/ppermute | solution.py:554
  12.4 5.1 %collective-permute-start.4 = (bf16[80,384]{1,0:T(8,128)(2,1)S(1)}, bf16[80,384]{1,0:T(8,128)(2,1)S(1)}, u32[]{:S(2)}, u32[]{:S(2)}) collective-permute-start(bf16[80,384]{1,0:T(8,128)(2,1)S(1)} %get-tuple-element.43), channel_id=1, source_target_pairs={{0,24},{4,28},{8,16},{12,20},{16,8},{20,12},{24,0},{28,4},{1,25},{... | collective-permute-start | bytes 184328 | tf_op jit(solution)/shard_map/ppermute | solution.py:554
  17.8 1.5 %collective-permute-start.5 = (bf16[4,80,256]{2,1,0:T(8,128)(2,1)S(1)}, bf16[4,80,256]{2,1,0:T(8,128)(2,1)S(1)}, u32[]{:S(2)}, u32[]{:S(2)}) collective-permute-start(bf16[4,80,256]{2,1,0:T(8,128)(2,1)S(1)} %get-tuple-element.56), channel_id=1, source_target_pairs={{0,4},{4,0},{8,12},{12,8},{16,20},{20,16},{24,28},{28,24},{1,5},{5... | collective-permute-start | bytes 491528 | tf_op jit(solution)/shard_map/ppermute | solution.py:558
  22.4 1.3 %collective-permute-start.6 = (bf16[4,24,128]{2,1,0:T(8,128)(2,1)S(1)}, bf16[4,24,128]{2,1,0:T(8,128)(2,1)S(1)}, u32[]{:S(2)}, u32[]{:S(2)}) collective-permute-start(bf16[4,24,128]{2,1,0:T(8,128)(2,1)S(1)} %get-tuple-element.62), channel_id=1, source_target_pairs={{0,4},{4,0},{8,12},{12,8},{16,20},{20,16},{24,28},{28,24},{1,5},{5... | collective-permute-start | bytes 73736 | tf_op jit(solution)/shard_map/ppermute | solution.py:594
  23.6 3.7 %collective-permute-start.7 = (bf16[2,24,128]{2,1,0:T(8,128)(2,1)S(1)}, bf16[2,24,128]{2,1,0:T(8,128)(2,1)S(1)}, u32[]{:S(2)}, u32[]{:S(2)}) collective-permute-start(bf16[2,24,128]{2,1,0:T(8,128)(2,1)S(1)} %get-tuple-element.63), channel_id=1, source_target_pairs={{0,8},{4,12},{8,0},{12,4},{16,24},{20,28},{24,16},{28,20},{1,9},{5... | collective-permute-start | bytes 36872 | tf_op jit(solution)/shard_map/ppermute | solution.py:603
  24.2 3.7 %collective-permute-start.8 = (bf16[2,24,128]{2,1,0:T(8,128)(2,1)S(1)}, bf16[2,24,128]{2,1,0:T(8,128)(2,1)S(1)}, u32[]{:S(2)}, u32[]{:S(2)}) collective-permute-start(bf16[2,24,128]{2,1,0:T(8,128)(2,1)S(1)} %get-tuple-element.64), channel_id=1, source_target_pairs={{0,16},{4,20},{8,24},{12,28},{16,0},{20,4},{24,8},{28,12},{1,17},{... | collective-permute-start | bytes 36872 | tf_op jit(solution)/shard_map/ppermute | solution.py:603
  24.7 4.6 %collective-permute-start.9 = (bf16[2,24,128]{2,1,0:T(8,128)(2,1)S(1)}, bf16[2,24,128]{2,1,0:T(8,128)(2,1)S(1)}, u32[]{:S(2)}, u32[]{:S(2)}) collective-permute-start(bf16[2,24,128]{2,1,0:T(8,128)(2,1)S(1)} %get-tuple-element.65), channel_id=1, source_target_pairs={{0,24},{4,28},{8,16},{12,20},{16,8},{20,12},{24,0},{28,4},{1,25},{... | collective-permute-start | bytes 36872 | tf_op jit(solution)/shard_map/ppermute | solution.py:603
